TPU v7x, 32 devices: a whole 2x2x4 slice. The times are simulated.
32 devices in a mesh: rep: 8 (over y, x, core), grp: 4 (over z).
Axes of the slice: x: 2, y: 2, z: 4, core: 2. Of those that a mesh axis runs over, the one named last changes fastest.
Arguments:
- tokens: bfloat16 [16, 1024, 1024], P('rep', 'grp'), may hold values from -6 to 6
- positions: int32 [3, 16, 1024], P(None, 'rep', 'grp'), may hold values from 0 to 15
- ln1_gain: bfloat16 [1024], P('grp'), may hold values from 0.099609375 to 1.8984375
- ln1_bias: bfloat16 [1024], P('grp'), may hold values from -3 to 3
- w_qkv: bfloat16 [1024, 3072], P('grp'), may hold values from -0.1875 to 0.1875
- b_qkv: bfloat16 [3072], P('grp'), may hold values from -3 to 3
- w_out: bfloat16 [1024, 1024], P('grp'), may hold values from -0.75 to 0.75
- b_out: bfloat16 [1024], P('grp'), may hold values from -3 to 3
- ln2_gain: bfloat16 [1024], P('grp'), may hold values from 0.099609375 to 1.8984375
- ln2_bias: bfloat16 [1024], P('grp'), may hold values from -3 to 3
- w_up: bfloat16 [1024, 4096], P('grp'), may hold values from -0.1875 to 0.1875
- b_up: bfloat16 [4096], P('grp'), may hold values from -3 to 3
- w_down: bfloat16 [4096, 1024], P('grp'), may hold values from -0.09375 to 0.09375
- b_down: bfloat16 [1024], P('grp'), may hold values from -3 to 3
- cotangent: bfloat16 [16, 1024, 1024], P('rep', 'grp'), may hold values from -6 to 6
Outputs:
- output: bfloat16 [16, 1024, 1024], P('rep', 'grp')
- grad_tokens: bfloat16 [16, 1024, 1024], P('rep', 'grp')
- grad_ln1_gain: float32 [1024], P('grp')
- grad_ln1_bias: float32 [1024], P('grp')
- grad_w_qkv: float32 [1024, 3072], P('grp')
- grad_b_qkv: float32 [3072], P('grp')
- grad_w_out: float32 [1024, 1024], P('grp')
- grad_b_out: float32 [1024], P('grp')
- grad_ln2_gain: float32 [1024], P('grp')
- grad_ln2_bias: float32 [1024], P('grp')
- grad_w_up: float32 [1024, 4096], P('grp')
- grad_b_up: float32 [4096], P('grp')
- grad_w_down: float32 [4096, 1024], P('grp')
- grad_b_down: float32 [1024], P('grp')
Inputs may be any that keep to these rules, and one draw needn't show every extreme that they name: `positions`: frame, row and column indices of a token.
All inputs are finite; a program needn't handle non-finite values.
Results may differ from a plain program's by a relative error of at most 0.02.
Values may be sent and summed in bfloat16 or wider, within the bound.
A program may use at most 320 MiB of HBM per device.

v0:
```python
import jax
import jax.numpy as jnp
from jax import lax
from jax.sharding import PartitionSpec as P

SCALE = 0.125
EPS = 1e-06


def rotary_angles(positions):
    pair = jnp.arange(32)
    band = (pair >= 10).astype(jnp.int32) + (pair >= 21).astype(jnp.int32)
    start = jnp.where(band == 0, 0, jnp.where(band == 1, 10, 21))
    count = jnp.where(band == 0, 10, 11)
    freq = jnp.power(
        jnp.float32(10000.0), -(pair - start).astype(jnp.float32) / count.astype(jnp.float32)
    )
    pos_f = positions.astype(jnp.float32)
    chosen = jnp.where(
        band[None, :] == 0,
        pos_f[0][:, None],
        jnp.where(band[None, :] == 1, pos_f[1][:, None], pos_f[2][:, None]),
    )
    return chosen * freq[None, :]


def rotate(field, cosine, sine):
    first = field[..., :32]
    second = field[..., 32:]
    return jnp.concatenate(
        [first * cosine - second * sine, first * sine + second * cosine], axis=-1
    )


def normalize(field):
    centred = field - jnp.mean(field, axis=-1, keepdims=True)
    variance = jnp.mean(centred * centred, axis=-1, keepdims=True)
    factor = lax.rsqrt(variance + EPS)
    return (centred * factor, factor)


def norm_back(grad_norm, normed, factor):
    return factor * (
        grad_norm
        - jnp.mean(grad_norm, axis=-1, keepdims=True)
        - normed * jnp.mean(grad_norm * normed, axis=-1, keepdims=True)
    )


def outer(left, right):
    return lax.dot_general(
        left, right, (((0,), (0,)), ((), ())), preferred_element_type=jnp.float32
    )


def back(left, right):
    return lax.dot_general(
        left, right, (((1,), (1,)), ((), ())), preferred_element_type=jnp.float32
    )


def exact_gelu(value):
    return jax.nn.gelu(value, approximate=False)


def column_sum(value):
    return jnp.sum(value.astype(jnp.float32), axis=0)


def forward_pass(params, field_in, positions):
    g1, b1, wqkv, bqkv, wo, bo, g2, b2, w1, bu, w2, bd = params
    field = field_in.astype(jnp.float32)
    count, width = field.shape
    heads = width // 64
    angles = rotary_angles(positions)
    cosine = jnp.cos(angles)[:, None, :]
    sine = jnp.sin(angles)[:, None, :]
    normed1, factor1 = normalize(field)
    h1 = (normed1 * g1.astype(jnp.float32) + b1.astype(jnp.float32)).astype(jnp.bfloat16)
    qkv = jnp.dot(h1, wqkv, preferred_element_type=jnp.float32) + bqkv.astype(jnp.float32)
    query_rot = rotate(qkv[:, :width].reshape(count, heads, 64), cosine, sine).astype(jnp.bfloat16)
    keys_rot = (
        rotate(qkv[:, width : 2 * width].reshape(count, heads, 64), cosine, sine)
        .astype(jnp.bfloat16)
        .reshape(count, width)
    )
    values = qkv[:, 2 * width :].astype(jnp.bfloat16)
    keys_all, values_all = (
        lax.all_gather(keys_rot, "grp", axis=0, tiled=True),
        lax.all_gather(values, "grp", axis=0, tiled=True),
    )
    total = keys_all.shape[0]
    keys_all = keys_all.reshape(total, heads, 64)
    values_all = values_all.reshape(total, heads, 64)
    scores = (
        jnp.einsum("thd,shd->hts", query_rot, keys_all, preferred_element_type=jnp.float32) * SCALE
    )
    top = jnp.max(scores, axis=-1, keepdims=True)
    lse = top + jnp.log(jnp.sum(jnp.exp(scores - top), axis=-1, keepdims=True))
    probs = jnp.exp(scores - lse).astype(jnp.bfloat16)
    mixed = (
        jnp.einsum("hts,shd->thd", probs, values_all, preferred_element_type=jnp.float32)
        .reshape(count, width)
        .astype(jnp.bfloat16)
    )
    second = field + jnp.dot(mixed, wo, preferred_element_type=jnp.float32) + bo.astype(jnp.float32)
    normed2, factor2 = normalize(second)
    h2 = (normed2 * g2.astype(jnp.float32) + b2.astype(jnp.float32)).astype(jnp.bfloat16)
    hidden = jnp.dot(h2, w1, preferred_element_type=jnp.float32) + bu.astype(jnp.float32)
    active = exact_gelu(hidden).astype(jnp.bfloat16)
    result = (
        second + jnp.dot(active, w2, preferred_element_type=jnp.float32) + bd.astype(jnp.float32)
    )
    saved = (
        normed1,
        factor1,
        h1,
        query_rot,
        keys_rot,
        values,
        lse,
        mixed,
        normed2,
        factor2,
        h2,
        hidden,
        active,
        cosine,
        sine,
    )
    return (saved, result.astype(jnp.bfloat16))


def backward_pass(params, saved, grad_in, totals):
    g1, b1, wqkv, bqkv, wo, bo, g2, b2, w1, bu, w2, bd = params
    (
        normed1,
        factor1,
        h1,
        query_rot,
        keys_rot,
        values,
        lse,
        mixed,
        normed2,
        factor2,
        h2,
        hidden,
        active,
        cosine,
        sine,
    ) = saved
    grad_out = grad_in.astype(jnp.float32)
    count, width = grad_out.shape
    heads = width // 64
    grad_y2 = grad_out.astype(jnp.bfloat16)
    grad_w2 = outer(active, grad_y2)
    grad_bd = column_sum(grad_y2)
    grad_act = back(grad_y2, w2)
    unused, pull = jax.vjp(exact_gelu, hidden)
    grad_hidden = pull(grad_act)[0].astype(jnp.bfloat16)
    grad_w1 = outer(h2, grad_hidden)
    grad_bu = column_sum(grad_hidden)
    grad_h2 = back(grad_hidden, w1)
    grad_g2 = jnp.sum(grad_h2 * normed2, axis=0)
    grad_b2 = jnp.sum(grad_h2, axis=0)
    grad_second = grad_out + norm_back(grad_h2 * g2.astype(jnp.float32), normed2, factor2)
    grad_y1 = grad_second.astype(jnp.bfloat16)
    grad_wo = outer(mixed, grad_y1)
    grad_bo = column_sum(grad_y1)
    grad_mixed = back(grad_y1, wo).astype(jnp.bfloat16).reshape(count, heads, 64)
    keys_all, values_all = (
        lax.all_gather(keys_rot, "grp", axis=0, tiled=True),
        lax.all_gather(values, "grp", axis=0, tiled=True),
    )
    total = keys_all.shape[0]
    keys_all = keys_all.reshape(total, heads, 64)
    values_all = values_all.reshape(total, heads, 64)
    scores = (
        jnp.einsum("thd,shd->hts", query_rot, keys_all, preferred_element_type=jnp.float32) * SCALE
    )
    probs = jnp.exp(scores - lse)
    grad_probs = jnp.einsum(
        "thd,shd->hts", grad_mixed, values_all, preferred_element_type=jnp.float32
    )
    delta = jnp.sum(probs * grad_probs, axis=-1, keepdims=True)
    grad_scores = (probs * (grad_probs - delta)).astype(jnp.bfloat16)
    grad_query = (
        jnp.einsum("hts,shd->thd", grad_scores, keys_all, preferred_element_type=jnp.float32)
        * SCALE
    )
    probs_low = probs.astype(jnp.bfloat16)
    grad_values = jnp.einsum(
        "hts,thd->shd", probs_low, grad_mixed, preferred_element_type=jnp.float32
    )
    grad_keys = (
        jnp.einsum("hts,thd->shd", grad_scores, query_rot, preferred_element_type=jnp.float32)
        * SCALE
    )
    keys_own, values_own = (
        lax.psum_scatter(
            grad_keys.reshape(total, width).astype(jnp.bfloat16),
            "grp",
            scatter_dimension=0,
            tiled=True,
        ).astype(jnp.float32),
        lax.psum_scatter(
            grad_values.reshape(total, width).astype(jnp.bfloat16),
            "grp",
            scatter_dimension=0,
            tiled=True,
        ).astype(jnp.float32),
    )
    query_back = rotate(grad_query, cosine, -sine).reshape(count, width)
    keys_back = rotate(keys_own.reshape(count, heads, 64), cosine, -sine).reshape(count, width)
    grad_qkv = jnp.concatenate([query_back, keys_back, values_own], axis=1).astype(jnp.bfloat16)
    grad_wqkv = outer(h1, grad_qkv)
    grad_bqkv = column_sum(grad_qkv)
    grad_h1 = back(grad_qkv, wqkv)
    grad_g1 = jnp.sum(grad_h1 * normed1, axis=0)
    grad_b1 = jnp.sum(grad_h1, axis=0)
    grad_field = grad_second + norm_back(grad_h1 * g1.astype(jnp.float32), normed1, factor1)
    terms = (
        grad_g1,
        grad_b1,
        grad_wqkv,
        grad_bqkv,
        grad_wo,
        grad_bo,
        grad_g2,
        grad_b2,
        grad_w1,
        grad_bu,
        grad_w2,
        grad_bd,
    )
    totals = tuple((a + b for a, b in zip(totals, terms)))
    return (grad_field.astype(jnp.bfloat16), totals)


def local(
    tokens,
    positions,
    ln1_gain,
    ln1_bias,
    w_qkv,
    b_qkv,
    w_out,
    b_out,
    ln2_gain,
    ln2_bias,
    w_up,
    b_up,
    w_down,
    b_down,
    cotangent,
):
    shards = (
        ln1_gain,
        ln1_bias,
        w_qkv,
        b_qkv,
        w_out,
        b_out,
        ln2_gain,
        ln2_bias,
        w_up,
        b_up,
        w_down,
        b_down,
    )
    groups = lax.axis_size("grp")
    totals = tuple((jnp.zeros((s.shape[0] * groups,) + s.shape[1:], jnp.float32) for s in shards))
    outputs = []
    gradients = []
    for index in range(tokens.shape[0]):
        forward_params = (
            lax.all_gather(ln1_gain, "grp", axis=0, tiled=True),
            lax.all_gather(ln1_bias, "grp", axis=0, tiled=True),
            lax.all_gather(w_qkv, "grp", axis=0, tiled=True),
            lax.all_gather(b_qkv, "grp", axis=0, tiled=True),
            lax.all_gather(w_out, "grp", axis=0, tiled=True),
            lax.all_gather(b_out, "grp", axis=0, tiled=True),
            lax.all_gather(ln2_gain, "grp", axis=0, tiled=True),
            lax.all_gather(ln2_bias, "grp", axis=0, tiled=True),
            lax.all_gather(w_up, "grp", axis=0, tiled=True),
            lax.all_gather(b_up, "grp", axis=0, tiled=True),
            lax.all_gather(w_down, "grp", axis=0, tiled=True),
            lax.all_gather(b_down, "grp", axis=0, tiled=True),
        )
        saved, result = forward_pass(forward_params, tokens[index], positions[:, index, :])
        outputs.append(result)
        backward_params = (
            lax.all_gather(ln1_gain, "grp", axis=0, tiled=True),
            lax.all_gather(ln1_bias, "grp", axis=0, tiled=True),
            lax.all_gather(w_qkv, "grp", axis=0, tiled=True),
            lax.all_gather(b_qkv, "grp", axis=0, tiled=True),
            lax.all_gather(w_out, "grp", axis=0, tiled=True),
            lax.all_gather(b_out, "grp", axis=0, tiled=True),
            lax.all_gather(ln2_gain, "grp", axis=0, tiled=True),
            lax.all_gather(ln2_bias, "grp", axis=0, tiled=True),
            lax.all_gather(w_up, "grp", axis=0, tiled=True),
            lax.all_gather(b_up, "grp", axis=0, tiled=True),
            lax.all_gather(w_down, "grp", axis=0, tiled=True),
            lax.all_gather(b_down, "grp", axis=0, tiled=True),
        )
        grad_field, totals = backward_pass(backward_params, saved, cotangent[index], totals)
        gradients.append(grad_field)
    owned = (
        lax.psum_scatter(
            totals[0].astype(jnp.bfloat16), "grp", scatter_dimension=0, tiled=True
        ).astype(jnp.float32),
        lax.psum_scatter(
            totals[1].astype(jnp.bfloat16), "grp", scatter_dimension=0, tiled=True
        ).astype(jnp.float32),
        lax.psum_scatter(
            totals[2].astype(jnp.bfloat16), "grp", scatter_dimension=0, tiled=True
        ).astype(jnp.float32),
        lax.psum_scatter(
            totals[3].astype(jnp.bfloat16), "grp", scatter_dimension=0, tiled=True
        ).astype(jnp.float32),
        lax.psum_scatter(
            totals[4].astype(jnp.bfloat16), "grp", scatter_dimension=0, tiled=True
        ).astype(jnp.float32),
        lax.psum_scatter(
            totals[5].astype(jnp.bfloat16), "grp", scatter_dimension=0, tiled=True
        ).astype(jnp.float32),
        lax.psum_scatter(
            totals[6].astype(jnp.bfloat16), "grp", scatter_dimension=0, tiled=True
        ).astype(jnp.float32),
        lax.psum_scatter(
            totals[7].astype(jnp.bfloat16), "grp", scatter_dimension=0, tiled=True
        ).astype(jnp.float32),
        lax.psum_scatter(
            totals[8].astype(jnp.bfloat16), "grp", scatter_dimension=0, tiled=True
        ).astype(jnp.float32),
        lax.psum_scatter(
            totals[9].astype(jnp.bfloat16), "grp", scatter_dimension=0, tiled=True
        ).astype(jnp.float32),
        lax.psum_scatter(
            totals[10].astype(jnp.bfloat16), "grp", scatter_dimension=0, tiled=True
        ).astype(jnp.float32),
        lax.psum_scatter(
            totals[11].astype(jnp.bfloat16), "grp", scatter_dimension=0, tiled=True
        ).astype(jnp.float32),
    )
    summed = (
        lax.psum(owned[0].astype(jnp.bfloat16), "rep").astype(jnp.float32),
        lax.psum(owned[1].astype(jnp.bfloat16), "rep").astype(jnp.float32),
        lax.psum(owned[2].astype(jnp.bfloat16), "rep").astype(jnp.float32),
        lax.psum(owned[3].astype(jnp.bfloat16), "rep").astype(jnp.float32),
        lax.psum(owned[4].astype(jnp.bfloat16), "rep").astype(jnp.float32),
        lax.psum(owned[5].astype(jnp.bfloat16), "rep").astype(jnp.float32),
        lax.psum(owned[6].astype(jnp.bfloat16), "rep").astype(jnp.float32),
        lax.psum(owned[7].astype(jnp.bfloat16), "rep").astype(jnp.float32),
        lax.psum(owned[8].astype(jnp.bfloat16), "rep").astype(jnp.float32),
        lax.psum(owned[9].astype(jnp.bfloat16), "rep").astype(jnp.float32),
        lax.psum(owned[10].astype(jnp.bfloat16), "rep").astype(jnp.float32),
        lax.psum(owned[11].astype(jnp.bfloat16), "rep").astype(jnp.float32),
    )
    output = jnp.stack(outputs, axis=0)
    grad_tokens = jnp.stack(gradients, axis=0)
    return (
        output,
        grad_tokens,
        summed[0],
        summed[1],
        summed[2],
        summed[3],
        summed[4],
        summed[5],
        summed[6],
        summed[7],
        summed[8],
        summed[9],
        summed[10],
        summed[11],
    )


def solution(mesh):
    placed = (
        P("rep", "grp", None),
        P(None, "rep", "grp"),
        P("grp"),
        P("grp"),
        P("grp", None),
        P("grp"),
        P("grp", None),
        P("grp"),
        P("grp"),
        P("grp"),
        P("grp", None),
        P("grp"),
        P("grp", None),
        P("grp"),
        P("rep", "grp", None),
    )
    return jax.shard_map(
        local,
        mesh=mesh,
        in_specs=placed,
        out_specs=(
            P("rep", "grp", None),
            P("rep", "grp", None),
            P("grp"),
            P("grp"),
            P("grp", None),
            P("grp"),
            P("grp", None),
            P("grp"),
            P("grp"),
            P("grp"),
            P("grp", None),
            P("grp"),
            P("grp", None),
            P("grp"),
        ),
        check_vma=False,
    )
```

profile of v0, /device:TPU:9, one launch (start us, length us, event | category | flops | bytes accessed | tf_op | source)
XLA Modules:
  0.0 1494.8 jit_solution(1610655362138257316)
XLA Ops:
  41.4 81.9 %all-gather.16.cloned.1.call-done = bf16[1024,3072]{1,0:T(8,128)(2,1)} async-done(((bf16[256,3072]{1,0:T(8,128)(2,1)}), bf16[1024,3072]{1,0:T(8,128)(2,1)}) %all-gather.16.cloned.1.call-update) | async-done | bytes 6291472 | tf_op jit(solution)/shard_map/all_gather | solution.py:280
  162.4 13.3 all_gather.43
  203.3 22.8 %all-gather.28.cloned.1.call-done = bf16[1024,1024]{1,0:T(8,128)(2,1)} async-done(((bf16[256,1024]{1,0:T(8,128)(2,1)}), bf16[1024,1024]{1,0:T(8,128)(2,1)}) %all-gather.28.cloned.1.call-update) | async-done | bytes 2097168 | tf_op jit(solution)/shard_map/all_gather | solution.py:90
  228.9 43.6 %all-gather.18.cloned.1.call-done = bf16[1024,1024]{1,0:T(8,128)(2,1)} async-done(((bf16[256,1024]{1,0:T(8,128)(2,1)}), bf16[1024,1024]{1,0:T(8,128)(2,1)}) %all-gather.18.cloned.1.call-update) | async-done | bytes 2097168 | tf_op jit(solution)/shard_map/all_gather | solution.py:90
  285.4 33.0 %all-gather.22.cloned.1.call-done = bf16[1024,1024]{1,0:T(8,128)(2,1)} async-done(((bf16[256,1024]{1,0:T(8,128)(2,1)}), bf16[1024,1024]{1,0:T(8,128)(2,1)}) %all-gather.22.cloned.1.call-update) | async-done | bytes 2097168 | tf_op jit(solution)/shard_map/all_gather | solution.py:282
  322.3 41.3 %all-gather.20.cloned.1.call-done = bf16[1024,1024]{0,1:T(8,128)(2,1)} async-done(((bf16[256,1024]{0,1:T(8,128)(2,1)}), bf16[1024,1024]{0,1:T(8,128)(2,1)}) %all-gather.20.cloned.1.call-update) | async-done | bytes 2097168 | tf_op jit(solution)/shard_map/all_gather | solution.py:89
  380.3 133.6 %all-gather.24.cloned.1.call-done = bf16[1024,4096]{1,0:T(8,128)(2,1)} async-done(((bf16[256,4096]{1,0:T(8,128)(2,1)}), bf16[1024,4096]{1,0:T(8,128)(2,1)}) %all-gather.24.cloned.1.call-update) | async-done | bytes 8388624 | tf_op jit(solution)/shard_map/all_gather | solution.py:286
  513.8 17.5 %multiply_convert_fusion.4 = (bf16[256,4096]{1,0:T(8,128)(2,1)}, f32[256,4096]{1,0:T(8,128)}, f32[256,4096]{1,0:T(8,128)}) fusion(f32[4096]{0:T(1024)} %convert_element_type.404, bf16[1024,4096]{1,0:T(8,128)(2,1)} %all-gather.24.cloned.1.call-done, f32[256,1024]{1,0:T(8,128)} %copy-done.16, f32[256]{0:T(256)S(1)} %add_rsqrt_fusion, f32[256]{0:T(256)} %copy-done.89, ...), kind=kOutput, calls=%fused_computation.28 | convolution fusion | flops 2218000384 | bytes 19949568 | tf_op jit(solution)/shard_map/dot_general | solution.py:109
  531.3 16.7 %multiply_convert_fusion.5 = (bf16[256,4096]{1,0:T(8,128)(2,1)}, f32[256,4096]{1,0:T(8,128)}, f32[256,4096]{1,0:T(8,128)}) fusion(f32[4096]{0:T(1024)S(1)} %copy-done.83, bf16[1024,4096]{1,0:T(8,128)(2,1)S(1)} %copy-done.100, f32[256,1024]{1,0:T(8,128)S(1)} %copy-done.11, f32[1024]{0:T(1024)S(1)} %bitcast.273, f32[1024]{0:T(1024)S(1)} %bitcast.267, ...), kind=kOutput, calls=%fused_computation.41 | convolution fusion | flops 2218000384 | bytes 19949568 | tf_op jit(solution)/shard_map/dot_general | solution.py:109
  548.0 115.2 %all-gather.26.cloned.1.call-done = bf16[4096,1024]{1,0:T(8,128)(2,1)} async-done(((bf16[1024,1024]{1,0:T(8,128)(2,1)}), bf16[4096,1024]{1,0:T(8,128)(2,1)}) %all-gather.26.cloned.1.call-update) | async-done | bytes 8388624 | tf_op jit(solution)/shard_map/all_gather | solution.py:288
  680.4 11.9 convert_reduce_fusion.1
  707.6 15.6 %multiply_reduce_fusion = (f32[16,256]{1,0:T(8,128)}, f32[16,256,1024]{2,1,0:T(8,128)}) fusion(f32[16,256,1024]{2,1,0:T(8,128)} %copy-done, f32[16,256]{1,0:T(8,128)} %copy-done.56, bf16[256,16,64]{0,2,1:T(8,128)(2,1)} %bitcast.234, bf16[1024,16,64]{0,2,1:T(8,128)(2,1)} %bitcast.219), kind=kOutput, calls=%fused_computation.3 | convolution fusion | flops 553644032 | bytes 36208640 | tf_op jit(solution)/shard_map/thd,shd->hts/dot_general | solution.py:183
  742.1 16.5 %multiply_reduce_fusion.1 = (f32[16,256]{1,0:T(8,128)}, f32[16,256,1024]{2,1,0:T(8,128)}) fusion(f32[16,256,1024]{2,1,0:T(8,128)} %copy-done.1, f32[16,256]{1,0:T(8,128)} %copy-done.58, bf16[256,16,64]{0,2,1:T(8,128)(2,1)} %bitcast.236, bf16[1024,16,64]{0,2,1:T(8,128)(2,1)} %bitcast.216), kind=kOutput, calls=%fused_computation.5 | convolution fusion | flops 553644032 | bytes 36208640 | tf_op jit(solution)/shard_map/thd,shd->hts/dot_general | solution.py:183
  811.2 14.8 reduce-scatter.9.cloned.1.call-done
  832.5 37.8 %reduce-scatter.11.cloned.1.call-done = bf16[256,1024]{0,1:T(8,128)(2,1)} async-done(((bf16[1024,1024]{0,1:T(8,128)(2,1)}), bf16[256,1024]{0,1:T(8,128)(2,1)}) %reduce-scatter.11.cloned.1.call-update) | async-done | bytes 524304 | tf_op jit(solution)/shard_map/reduce_scatter | solution.py:207
  878.3 37.5 %reduce-scatter.15.cloned.1.call-done = bf16[256,1024]{0,1:T(8,128)(2,1)} async-done(((bf16[1024,1024]{0,1:T(8,128)(2,1)}), bf16[256,1024]{0,1:T(8,128)(2,1)}) %reduce-scatter.15.cloned.1.call-update) | async-done | bytes 524304 | tf_op jit(solution)/shard_map/reduce_scatter | solution.py:207
  936.5 11.8 add_convert_fusion.1
  958.3 11.6 add_convert_fusion
  997.2 77.9 %reduce-scatter.17.cloned.1.call-done = bf16[256,3072]{1,0:T(8,128)(2,1)} async-done(((bf16[1024,3072]{1,0:T(8,128)(2,1)}), bf16[256,3072]{1,0:T(8,128)(2,1)}) %reduce-scatter.17.cloned.1.call-update) | async-done | bytes 1572880 | tf_op jit(solution)/shard_map/reduce_scatter | solution.py:316
  1075.1 147.0 %reduce-scatter.21.cloned.1.call-done = bf16[256,4096]{1,0:T(8,128)(2,1)} async-done(((bf16[1024,4096]{1,0:T(8,128)(2,1)}), bf16[256,4096]{1,0:T(8,128)(2,1)}) %reduce-scatter.21.cloned.1.call-update) | async-done | bytes 2097168 | tf_op jit(solution)/shard_map/reduce_scatter | solution.py:334
  1222.0 147.5 %reduce-scatter.23.cloned.1.call-done = bf16[1024,1024]{1,0:T(8,128)(2,1)} async-done(((bf16[4096,1024]{1,0:T(8,128)(2,1)}), bf16[1024,1024]{1,0:T(8,128)(2,1)}) %reduce-scatter.23.cloned.1.call-update) | async-done | bytes 2097168 | tf_op jit(solution)/shard_map/reduce_scatter | solution.py:340
  1382.0 12.9 all-reduce.10
  1395.4 15.2 %all-reduce.8 = (bf16[256]{0:T(256)(128)(2,1)S(1)}, bf16[256]{0:T(256)(128)(2,1)S(1)}, bf16[768]{0:T(1024)(128)(2,1)S(1)}, bf16[256]{0:T(256)(128)(2,1)S(1)}, bf...) all-reduce(bf16[256]{0:T(256)(128)(2,1)S(1)} %dynamic-slice.1, ...), channel_id=1, replica_groups=mesh['rep'=8,'grp'=4] {'rep'}, use_global_device_ids=true, to_apply=%region_29.30 | all-reduce | flops 3328 | bytes 13312 | tf_op jit(solution)/shard_map/psum | solution.py:348
  1418.6 59.6 %all-reduce.13.cloned.1.call-done = (bf16[256,3072]{1,0:T(8,128)(2,1)}, bf16[256,1024]{1,0:T(8,128)(2,1)}, bf16[256,4096]{1,0:T(8,128)(2,1)}, bf16[1024,1024]{1,0:T(8,128)(2,1)}) async-done(((bf16[256,3072]{1,0:T(8,128)(2,1)}, bf16[256,1024]{1,0:T(8,128)(2,1)}, bf16[256,4096]{1,0:T(8,128)(2,1)}, bf16[1024,1024]{1,0:T(8,128)(2,1)}), (bf16[256,3072]{1,0:T(8,128)(2,1)}, bf16[256,1024]{1,0:T(8,128)(2,1)}, ...) | async-done | bytes 6291472 | tf_op jit(solution)/shard_map/psum | solution.py:350
  (409 shorter events, 340.6 us)
Async XLA Ops:
  7.2 116.1 %all-gather.16.cloned.1.call-start = ((), (), s32[]{:S(2)}) async-start(), calls=%async_computation.8 | async-start | bytes 7864320 | tf_op jit(solution)/shard_map/all_gather | solution.py:280
  7.9 181.8 %all-gather.30.cloned.1.call-start = ((), (), s32[]{:S(2)}) async-start(), calls=%async_computation.15 | async-start | bytes 2621440 | tf_op jit(solution)/shard_map/all_gather | solution.py:89
  19.2 109.0 %copy-start.92 = (f32[4,1,768]{2,1,0:T(1,128)}, f32[4,1,768]{2,1,0:T(1,128)S(1)}, u32[]{:S(2)}) copy-start(f32[4,1,768]{2,1,0:T(1,128)S(1)} %convert_element_type.476) | copy-start | bytes 36868
  26.4 110.0 %copy-start.54 = (f32[4,1,256]{2,1,0:T(1,128)}, f32[4,1,256]{2,1,0:T(1,128)S(1)}, u32[]{:S(2)}) copy-start(f32[4,1,256]{2,1,0:T(1,128)S(1)} %convert_element_type.475) | copy-start | bytes 12292
  134.2 91.9 %all-gather.28.cloned.1.call-start = ((), (), s32[]{:S(2)}) async-start(), calls=%async_computation.14 | async-start | bytes 2621440 | tf_op jit(solution)/shard_map/all_gather | solution.py:90
  136.4 136.2 %all-gather.18.cloned.1.call-start = ((), (), s32[]{:S(2)}) async-start(), calls=%async_computation.9 | async-start | bytes 2621440 | tf_op jit(solution)/shard_map/all_gather | solution.py:90
  143.7 174.7 %all-gather.22.cloned.1.call-start = ((), (), s32[]{:S(2)}) async-start(), calls=%async_computation.11 | async-start | bytes 2621440 | tf_op jit(solution)/shard_map/all_gather | solution.py:282
  144.3 219.3 %all-gather.20.cloned.1.call-start = ((), (), s32[]{:S(2)}) async-start(), calls=%async_computation.10 | async-start | bytes 2621440 | tf_op jit(solution)/shard_map/all_gather | solution.py:89
  151.1 362.8 %all-gather.24.cloned.1.call-start = ((), (), s32[]{:S(2)}) async-start(), calls=%async_computation.12 | async-start | bytes 10485760 | tf_op jit(solution)/shard_map/all_gather | solution.py:286
  151.8 511.4 %all-gather.26.cloned.1.call-start = ((), (), s32[]{:S(2)}) async-start(), calls=%async_computation.13 | async-start | bytes 10485760 | tf_op jit(solution)/shard_map/all_gather | solution.py:288
  152.6 657.5 %reduce-scatter.13.cloned.1.call-start = ((), (), s32[]{:S(2)}) async-start(), calls=%async_computation.18 | async-start | bytes 2621440 | tf_op jit(solution)/shard_map/reduce_scatter | solution.py:201
  379.0 321.4 %copy-start.69 = (f32[256]{0:T(256)}, f32[256]{0:T(256)S(1)}, u32[]{:S(2)}) copy-start(f32[256]{0:T(256)S(1)} %broadcast_multiply_fusion.10) | copy-start | bytes 3076
  380.2 320.2 %copy-start.93 = (f32[256]{0:T(256)}, f32[256]{0:T(256)S(1)}, u32[]{:S(2)}) copy-start(f32[256]{0:T(256)S(1)} %add_rsqrt_fusion) | copy-start | bytes 3076
  380.3 320.1 %copy-start.77 = (f32[256]{0:T(256)}, f32[256]{0:T(256)S(1)}, u32[]{:S(2)}) copy-start(f32[256]{0:T(256)S(1)} %add_rsqrt_fusion.2) | copy-start | bytes 3076
  737.2 88.8 %reduce-scatter.9.cloned.1.call-start = ((), (), s32[]{:S(2)}) async-start(), calls=%async_computation.16 | async-start | bytes 2621440 | tf_op jit(solution)/shard_map/reduce_scatter | solution.py:201
  771.9 98.3 %reduce-scatter.11.cloned.1.call-start = ((), (), s32[]{:S(2)}) async-start(), calls=%async_computation.17 | async-start | bytes 2621440 | tf_op jit(solution)/shard_map/reduce_scatter | solution.py:207
  781.4 134.4 %reduce-scatter.15.cloned.1.call-start = ((), (), s32[]{:S(2)}) async-start(), calls=%async_computation.19 | async-start | bytes 2621440 | tf_op jit(solution)/shard_map/reduce_scatter | solution.py:207
  790.8 206.4 %reduce-scatter.19.cloned.1.call-start = ((), (), s32[]{:S(2)}) async-start(), calls=%async_computation.21 | async-start | bytes 2621440 | tf_op jit(solution)/shard_map/reduce_scatter | solution.py:322
  794.9 280.2 %reduce-scatter.17.cloned.1.call-start = ((), (), s32[]{:S(2)}) async-start(), calls=%async_computation.20 | async-start | bytes 7864320 | tf_op jit(solution)/shard_map/reduce_scatter | solution.py:316
  925.7 296.3 %reduce-scatter.21.cloned.1.call-start = ((), (), s32[]{:S(2)}) async-start(), calls=%async_computation.22 | async-start | bytes 10485760 | tf_op jit(solution)/shard_map/reduce_scatter | solution.py:334
  948.3 421.2 %reduce-scatter.23.cloned.1.call-start = ((), (), s32[]{:S(2)}) async-start(), calls=%async_computation.23 | async-start | bytes 10485760 | tf_op jit(solution)/shard_map/reduce_scatter | solution.py:340
  969.9 508.2 %all-reduce.13.cloned.1.call-start = ((), (), s32[]{:S(2)}) async-start(), calls=%async_computation.24 | async-start | bytes 12582912 | tf_op jit(solution)/shard_map/psum | solution.py:350
  995.9 373.6 %copy-start.21 = (bf16[256,16,64]{0,2,1:T(8,128)(2,1)S(1)}, bf16[256,16,64]{0,2,1:T(8,128)(2,1)}, u32[]{:S(2)}) copy-start(bf16[256,16,64]{0,2,1:T(8,128)(2,1)} %pad_maximum_fusion.11) | copy-start | bytes 1572868
  995.9 373.6 %copy-start.22 = (bf16[256,16,64]{0,2,1:T(8,128)(2,1)S(1)}, bf16[256,16,64]{0,2,1:T(8,128)(2,1)}, u32[]{:S(2)}) copy-start(bf16[256,16,64]{0,2,1:T(8,128)(2,1)} %pad_maximum_fusion.10) | copy-start | bytes 1572868
  (108 other events, 1997.5 us)
Sparse Core Ops, SparseCore 0:
  9.6 113.6 all-gather.15
  134.3 43.6 all-gather.29
  180.1 45.8 all-gather.27
  228.1 44.4 all-gather.17
  274.0 44.4 all-gather.21
  320.4 43.1 all-gather.19
  365.2 148.5 all-gather.23
  515.4 147.7 all-gather.25
  737.3 42.7 reduce-scatter.12
  782.2 43.6 reduce-scatter.8
  828.3 41.9 reduce-scatter.10
  873.0 42.8 reduce-scatter.14
  918.1 42.8 reduce-scatter.18
  963.2 111.8 reduce-scatter.16
  1077.3 144.7 reduce-scatter.20
  1224.3 145.2 reduce-scatter.22
  1373.0 105.1 all-reduce.12
where the time goes:
time: 1500 us; the launch traced here: 1490 us
  waiting for transfers between devices  996 us (66%)
  matrix products  270 us (18%)
  blocking collectives  101 us (7%)
  other arithmetic  63.2 us (4%)
  local copies, waits for them, and re-layouts  45.4 us (3%)
  between operations  17.9 us (1%)
    reduce_scatter x1, waiting for transfers between devices, local(): lax.psum_scatter(totals[10].astype(jnp.bfloat16), 'grp', scatter_dimensio...  147 us
    reduce_scatter x1, waiting for transfers between devices, local(): lax.psum_scatter(totals[8].astype(jnp.bfloat16), 'grp', scatter_dimension...  147 us
    all_gather x1, waiting for transfers between devices, local(): lax.all_gather(w_up, 'grp', axis=0, tiled=True)  134 us
    all_gather x1, waiting for transfers between devices, local(): lax.all_gather(w_down, 'grp', axis=0, tiled=True)  115 us
    all_gather x1, waiting for transfers between devices, local(): lax.all_gather(w_qkv, 'grp', axis=0, tiled=True)  81.9 us
    reduce_scatter x1, waiting for transfers between devices, local(): lax.psum_scatter(totals[2].astype(jnp.bfloat16), 'grp', scatter_dimension...  77.9 us
    reduce_scatter x2, waiting for transfers between devices, backward_pass(): lax.psum_scatter(grad_values.reshape(total, width).astype(jnp.bfloat16),...  75.3 us
    all_gather x2, waiting for transfers between devices, forward_pass(): lax.all_gather(values, 'grp', axis=0, tiled=True)  66.4 us
  transfers between devices with their start and end apart: 17, of which 14 were waited for; matrix products, arithmetic and copies ran while one was open for 18% of the time, Pallas kernels for 0%

commit v1 on v0

--- a/solution.py
+++ b/solution.py
@@ -1,10 +1,664 @@
+import functools
+
 import jax
 import jax.numpy as jnp
 from jax import lax
+from jax.experimental import pallas as pl
+from jax.experimental.pallas import tpu as pltpu
+from jax.sharding import Mesh
 from jax.sharding import PartitionSpec as P
 
 SCALE = 0.125
 EPS = 1e-06
+HEAD = 64
+BF = jnp.bfloat16
+F32 = jnp.float32
+MESH = pl.DeviceIdType.MESH
+ANY = pl.BlockSpec(memory_space=pl.ANY)
+VM = pl.BlockSpec(memory_space=pltpu.VMEM)
+
+
+def where_am_i():
+    return lax.axis_index("rp"), lax.axis_index("core"), lax.axis_index("grp")
+
+
+def remote(src, dst, send, recv, target):
+    return pltpu.make_async_remote_copy(
+        src_ref=src,
+        dst_ref=dst,
+        send_sem=send,
+        recv_sem=recv,
+        device_id=target,
+        device_id_type=MESH,
+    )
+
+
+def enter(p, c, z, groups):
+    barrier = pltpu.get_barrier_semaphore()
+    for k in range(groups):
+        for d in range(2):
+            if k == 0 and d == 0:
+                continue
+            pl.semaphore_signal(
+                barrier, inc=1, device_id=(p, c ^ d, lax.rem(z + k, groups)), device_id_type=MESH
+            )
+    for b in (1, 2):
+        pl.semaphore_signal(barrier, inc=1, device_id=(p ^ b, c, z), device_id_type=MESH)
+    pl.semaphore_wait(barrier, 2 * groups - 1 + 2)
+
+
+def move_tokens(refs, outs, send, recv, p, c, z, clips):
+    core, slot = lax.div(z, clips), lax.rem(z, clips)
+
+    def route(i):
+        return core, c * clips + i
+
+    def here(i):
+        return jnp.logical_and(core == c, c * clips + i == z)
+
+    def start():
+        for n, (src, dst) in enumerate(zip(refs, outs)):
+            for i in range(clips):
+                tc, tz = route(i)
+
+                @pl.when(here(i))
+                def _():
+                    pltpu.make_async_copy(src.at[i], dst.at[slot], recv.at[n, slot]).start()
+
+                @pl.when(jnp.logical_not(here(i)))
+                def _():
+                    remote(
+                        src.at[i], dst.at[slot], send.at[n, i], recv.at[n, slot], (p, tc, tz)
+                    ).start()
+
+    def finish():
+        for n, (src, dst) in enumerate(zip(refs, outs)):
+            for i in range(clips):
+
+                @pl.when(jnp.logical_not(here(i)))
+                def _():
+                    remote(
+                        src.at[i], dst.at[slot], send.at[n, i], recv.at[n, slot], (p, c ^ 1, z)
+                    ).wait_send()
+
+            for m in range(clips):
+                pltpu.make_async_copy(src.at[0], dst.at[m], recv.at[n, m]).wait()
+
+    return start, finish
+
+
+def gather_body(groups, clips, count, *refs):
+    halves, (small, x, pos) = refs[:count], refs[count : count + 3]
+    outs = refs[count + 3 : 2 * count + 3]
+    small_o, x_o, pos_o = refs[2 * count + 3 : 2 * count + 6]
+    zs, zr, xs, xr, ys, yr, fs, fr, ls, ss, sr, ts, tr = refs[2 * count + 6 :]
+    p, c, z = where_am_i()
+    enter(p, c, z, groups)
+    col = [(p, c, lax.rem(z + k, groups)) for k in range(groups)]
+    org = [lax.rem(z + groups - k, groups) for k in range(groups)]
+    xn, yn = (p ^ 1, c, z), (p ^ 2, c, z)
+    start, finish = move_tokens((x, pos), (x_o, pos_o), ts, tr, p, c, z, clips)
+    start()
+    smalls = [
+        remote(small, small_o.at[z], ss.at[k], sr.at[k], col[k]) for k in range(1, groups)
+    ]
+    for s in smalls:
+        s.start()
+    keep = [pltpu.make_async_copy(small, small_o.at[z], ls.at[count])]
+    for w in range(count):
+        keep.append(pltpu.make_async_copy(halves[w], outs[w].at[z], ls.at[w]))
+    for k in keep:
+        k.start()
+    first = {}
+    for w in range(count):
+        for k in range(1, groups):
+            first[w, k] = remote(
+                halves[w].at[p], outs[w].at[z, p], zs.at[w, k], zr.at[w, k], col[k]
+            )
+            first[w, k].start()
+    units = [(w, k) for w in range(count) for k in range(1, groups)]
+    xc, yc, fa, fb = {}, {}, {}, {}
+
+    def plane(u):
+        w, k = u
+        o = outs[w].at[org[k]]
+        remote(halves[w].at[p], o.at[p], zs.at[w, k], zr.at[w, k], col[k]).wait_recv()
+        xc[u] = remote(o.at[p], o.at[p], xs.at[w, k], xr.at[w, k], xn)
+        yc[u] = remote(o.at[p], o.at[p], ys.at[w, k], yr.at[w, k], yn)
+        xc[u].start()
+        yc[u].start()
+
+    def forward(u):
+        w, k = u
+        o = outs[w].at[org[k]]
+        q = p ^ 1
+        remote(o.at[q], o.at[q], xs.at[w, k], xr.at[w, k], xn).wait_recv()
+        fa[u] = remote(o.at[q, 0], o.at[q, 0], fs.at[w, k, 0], fr.at[w, k, 0], yn)
+        fa[u].start()
+        q = p ^ 2
+        remote(o.at[q], o.at[q], ys.at[w, k], yr.at[w, k], yn).wait_recv()
+        fb[u] = remote(o.at[q, 1], o.at[q, 1], fs.at[w, k, 1], fr.at[w, k, 1], xn)
+        fb[u].start()
+
+    lag = 2
+    for n in range(len(units) + lag):
+        if n < len(units):
+            plane(units[n])
+        if n >= lag:
+            forward(units[n - lag])
+    for u in units:
+        w, k = u
+        q = p ^ 3
+        o = outs[w].at[org[k]]
+        remote(o.at[q, 0], o.at[q, 0], fs.at[w, k, 0], fr.at[w, k, 0], yn).wait_recv()
+        remote(o.at[q, 1], o.at[q, 1], fs.at[w, k, 1], fr.at[w, k, 1], xn).wait_recv()
+    for k in range(1, groups):
+        remote(small, small_o.at[org[k]], ss.at[k], sr.at[k], col[k]).wait_recv()
+    for u in units:
+        first[u].wait_send()
+        xc[u].wait_send()
+        yc[u].wait_send()
+        fa[u].wait_send()
+        fb[u].wait_send()
+    for s in smalls:
+        s.wait_send()
+    for k in keep:
+        k.wait()
+    finish()
+
+
+def gather(halves, small, x, pos, groups):
+    count, clips = len(halves), x.shape[0]
+    dma = pltpu.SemaphoreType.DMA
+    shapes = [jax.ShapeDtypeStruct((groups,) + h.shape, h.dtype) for h in halves]
+    shapes += [jax.ShapeDtypeStruct((groups,) + small.shape, small.dtype)]
+    shapes += [jax.ShapeDtypeStruct(x.shape, x.dtype), jax.ShapeDtypeStruct(pos.shape, pos.dtype)]
+    return pl.pallas_call(
+        functools.partial(gather_body, groups, clips, count),
+        out_shape=shapes,
+        in_specs=[VM] * count + [VM, ANY, ANY],
+        out_specs=[ANY] * len(shapes),
+        scratch_shapes=[dma((count, groups))] * 6
+        + [dma((count, groups, 2))] * 2
+        + [dma((count + 1,)), dma((groups,)), dma((groups,)), dma((2, clips)), dma((2, clips))],
+        compiler_params=pltpu.CompilerParams(collective_id=0, has_side_effects=True),
+        name="gather",
+    )(*halves, small, x, pos)
+
+
+def reduce_body(groups, clips, count, *refs):
+    grads, (small, gx) = refs[:count], refs[count : count + 2]
+    outs = refs[count + 2 : 2 * count + 2]
+    small_o, gx_o = refs[2 * count + 2 : 2 * count + 4]
+    scratch = refs[2 * count + 4 :]
+    own_a, own_b, one_a, one_b, two_a, two_b, mine, three, full = (
+        scratch[i * count : (i + 1) * count] for i in range(9)
+    )
+    small_r, small_z = scratch[9 * count : 9 * count + 2]
+    (os, s1, r1, s2, r2, s3, r3, s4, r4, s5, r5, cs, cr, ls, ss, sr, ts, tr) = scratch[9 * count + 2 :]
+    p, c, z = where_am_i()
+    hi, lo = lax.div(p, 2), lax.rem(p, 2)
+    enter(p, c, z, groups)
+    col = [(p, c, lax.rem(z + k, groups)) for k in range(groups)]
+    xn, yn, cn = (p ^ 1, c, z), (p ^ 2, c, z), (p, c ^ 1, z)
+    start, finish = move_tokens((gx,), (gx_o,), ts, tr, p, c, z, clips)
+    start()
+    small_o[...] = small[...]
+    for n, target in enumerate((cn, xn, yn)):
+        copy = remote(small_o, small_r.at[n], ss.at[n], sr.at[n], target)
+        copy.start()
+        copy.wait()
+        small_o[...] += small_r[n]
+    tails = [
+        remote(small_o, small_z.at[k], ss.at[2 + k], sr.at[2 + k], col[k]) for k in range(1, groups)
+    ]
+    for t in tails:
+        t.start()
+    units = [(w, k) for w in range(count) for k in range(groups)]
+    load, c1, c2, c3, c4, c5 = {}, {}, {}, {}, {}, {}
+    for u in units:
+        w, k = u
+        g = grads[w].at[k]
+        c1[u, 0] = remote(g.at[:, 1 - lo, 0], one_a[w].at[k], s1.at[w, k, 0], r1.at[w, k, 0], xn)
+        c1[u, 1] = remote(g.at[1 - hi, :, 1], one_b[w].at[k], s1.at[w, k, 1], r1.at[w, k, 1], yn)
+        load[u, 0] = pltpu.make_async_copy(g.at[:, lo, 0], own_a[w].at[k], os.at[w, k, 0])
+        load[u, 1] = pltpu.make_async_copy(g.at[hi, :, 1], own_b[w].at[k], os.at[w, k, 1])
+        c1[u, 0].start()
+        c1[u, 1].start()
+        load[u, 0].start()
+        load[u, 1].start()
+
+    def stage_one(u):
+        w, k = u
+        for n, (own, one, two, side, target) in enumerate(
+            ((own_a, one_a, two_a, hi, yn), (own_b, one_b, two_b, lo, xn))
+        ):
+            load[u, n].wait()
+            c1[u, n].wait_recv()
+            o = own[w].at[k]
+            o[...] = (o[...].astype(F32) + one[w][k].astype(F32)).astype(BF)
+            c2[u, n] = remote(o.at[1 - side], two[w].at[k], s2.at[w, k, n], r2.at[w, k, n], target)
+            c2[u, n].start()
+
+    def stage_two(u):
+        w, k = u
+        for n, (own, two, side) in enumerate(((own_a, two_a, hi), (own_b, two_b, lo))):
+            c2[u, n].wait_recv()
+            mine[w][k, n] = (own[w][k, side].astype(F32) + two[w][k].astype(F32)).astype(BF)
+
+        @pl.when(z != k)
+        def _():
+            remote(
+                mine[w].at[k],
+                three[w].at[lax.rem(k - z + groups, groups)],
+                s3.at[w, k],
+                r3.at[w, lax.rem(k - z + groups, groups)],
+                (p, c, k),
+            ).start()
+
+    def stage_three(w):
+        total = mine[w][z].astype(F32)
+        for k in range(1, groups):
+            remote(mine[w].at[0], three[w].at[k], s3.at[w, 0], r3.at[w, k], col[k]).wait_recv()
+            total = total + three[w][k].astype(F32)
+        full[w][p] = total.astype(BF)
+        for n, target in enumerate((xn, yn)):
+            f = full[w].at[p]
+            c4[w, n] = remote(f, f, s4.at[w, n], r4.at[w, n], target)
+            c4[w, n].start()
+
+    def stage_four(w):
+        for n, (q, target) in enumerate(((p ^ 1, yn), (p ^ 2, xn))):
+            f = full[w].at[q]
+            remote(f, f, s4.at[w, n], r4.at[w, n], target).wait_recv()
+            f = full[w].at[q, n]
+            c5[w, n] = remote(f, f, s5.at[w, n], r5.at[w, n], target)
+            c5[w, n].start()
+
+    def stage_five(w):
+        for n in range(2):
+            f = full[w].at[p ^ 3, n]
+            remote(f, f, s5.at[w, n], r5.at[w, n], xn).wait_recv()
+        pltpu.make_async_copy(full[w], outs[w].at[c], ls.at[w]).start()
+        remote(full[w], outs[w].at[c], cs.at[w], cr.at[w], cn).start()
+
+    lag = 3
+    for n in range(len(units) + lag):
+        if n < len(units):
+            stage_one(units[n])
+        if n >= lag:
+            stage_two(units[n - lag])
+    for w in range(count):
+        stage_three(w)
+        if w >= 1:
+            stage_four(w - 1)
+        if w >= 2:
+            stage_five(w - 2)
+    stage_four(count - 1)
+    for w in range(max(count - 2, 0), count):
+        stage_five(w)
+    for k in range(1, groups):
+        tails[k - 1].wait()
+    for k in range(1, groups):
+        small_o[...] += small_z[k]
+    for u in units:
+        w, k = u
+        for n in range(2):
+            c1[u, n].wait_send()
+            c2[u, n].wait_send()
+
+        @pl.when(z != k)
+        def _():
+            remote(mine[w].at[k], three[w].at[0], s3.at[w, k], r3.at[w, 0], xn).wait_send()
+
+    for w in range(count):
+        for n in range(2):
+            c4[w, n].wait_send()
+            c5[w, n].wait_send()
+        pltpu.make_async_copy(full[w], outs[w].at[c], ls.at[w]).wait()
+        remote(full[w], outs[w].at[1 - c], cs.at[w], cr.at[w], cn).wait()
+    finish()
+
+
+def reduce(grads, small, gx, groups):
+    count, clips = len(grads), gx.shape[0]
+    dma = pltpu.SemaphoreType.DMA
+    tiles = [g.shape[4:] for g in grads]
+    shapes = [jax.ShapeDtypeStruct((2, 4, 2) + t, BF) for t in tiles]
+    shapes += [
+        jax.ShapeDtypeStruct(small.shape, small.dtype),
+        jax.ShapeDtypeStruct(gx.shape, gx.dtype),
+    ]
+    scratch = []
+    for lead in (
+        (groups, 2),
+        (groups, 2),
+        (groups, 2),
+        (groups, 2),
+        (groups,),
+        (groups,),
+        (groups, 2),
+        (groups, 2),
+        (4, 2),
+    ):
+        scratch += [pltpu.VMEM(lead + t, BF) for t in tiles]
+    scratch += [pltpu.VMEM((3,) + small.shape, F32), pltpu.VMEM((groups,) + small.shape, F32)]
+    pair = dma((count, groups, 2))
+    scratch += [pair] * 5 + [dma((count, groups))] * 2 + [dma((count, 2))] * 4
+    scratch += [dma((count,))] * 3 + [dma((2 + groups,))] * 2 + [dma((1, clips))] * 2
+    return pl.pallas_call(
+        functools.partial(reduce_body, groups, clips, count),
+        out_shape=shapes,
+        in_specs=[ANY] * count + [VM, ANY],
+        out_specs=[ANY] * count + [VM, ANY],
+        scratch_shapes=scratch,
+        compiler_params=pltpu.CompilerParams(
+            collective_id=1, has_side_effects=True, vmem_limit_bytes=60 * 1024 * 1024
+        ),
+        name="reduce",
+    )(*grads, small, gx)
+
+
+def turn(u, cosine, sine):
+    half = HEAD // 2
+    first, second = u[:half], u[half:]
+    return jnp.concatenate(
+        [first * cosine - second * sine, first * sine + second * cosine], axis=0
+    )
+
+
+def dot(a, b):
+    return jnp.dot(a, b, preferred_element_type=F32)
+
+
+def attention_body(step, q_ref, k_ref, v_ref, cos_ref, sin_ref, qs_ref, kr_ref, vb_ref, o_ref, l_ref):
+    cosine, sine = cos_ref[...], sin_ref[...]
+    length = cosine.shape[1]
+    kr = turn(k_ref[...], cosine, sine).astype(BF)
+    vb = v_ref[...].astype(BF)
+    qs = (turn(q_ref[...], cosine, sine).astype(BF).astype(F32) * SCALE).astype(BF)
+    kr_ref[...] = kr
+    vb_ref[...] = vb
+    qs_ref[...] = qs
+    keys = kr.T
+    for i in range(0, length, step):
+        scores = dot(keys, qs[:, i : i + step])
+        top = jnp.max(scores, axis=0, keepdims=True)
+        e = jnp.exp(scores - top)
+        total = jnp.sum(e, axis=0, keepdims=True)
+        mixed = dot(vb, e.astype(BF))
+        o_ref[:, i : i + step] = (mixed / total).astype(BF)
+        l_ref[0, :, i : i + step] = top + jnp.log(total)
+
+
+def attention(qkv, cosine, sine, step=256):
+    rows, length = qkv.shape
+    width = rows // 3
+    heads = width // HEAD
+    block = [pl.BlockSpec((HEAD, length), lambda h, n=n: (n * heads + h, 0)) for n in range(3)]
+    table = pl.BlockSpec((HEAD // 2, length), lambda h: (0, 0))
+    out = pl.BlockSpec((HEAD, length), lambda h: (h, 0))
+    shape = jax.ShapeDtypeStruct((width, length), BF)
+    return pl.pallas_call(
+        functools.partial(attention_body, step),
+        out_shape=[shape] * 4 + [jax.ShapeDtypeStruct((heads, 1, length), F32)],
+        grid=(heads,),
+        in_specs=block + [table, table],
+        out_specs=[out] * 4 + [pl.BlockSpec((1, 1, length), lambda h: (h, 0, 0))],
+        cost_estimate=pl.CostEstimate(
+            flops=4 * width * length * length,
+            transcendentals=heads * length * length,
+            bytes_accessed=width * length * 24,
+        ),
+        name="attention",
+    )(qkv, qkv, qkv, cosine, sine)
+
+
+def attention_back_body(
+    step, q_ref, k_ref, v_ref, o_ref, l_ref, g_ref, cos_ref, sin_ref, dq_ref, dk_ref, dv_ref, ak, av
+):
+    cosine, sine = cos_ref[...], sin_ref[...]
+    length = cosine.shape[1]
+    kt, keys, values = k_ref[...], k_ref[...].T, v_ref[...].T
+    queries, grads = q_ref[...].T, g_ref[...].T
+    for i in range(0, length, step):
+        s = slice(i, i + step)
+        g = g_ref[:, s]
+        scores = dot(keys, q_ref[:, s])
+        p = jnp.exp(scores - l_ref[0, :, s])
+        dp = dot(values, g)
+        delta = jnp.sum(o_ref[:, s].astype(F32) * g.astype(F32), axis=0, keepdims=True)
+        ds = (p * (dp - delta)).astype(BF)
+        dq = dot(kt, ds) * SCALE
+        dq_ref[:, s] = turn(dq, cosine[:, s], -sine[:, s]).astype(BF)
+        dv = dot(p.astype(BF), grads[s])
+        dk = dot(ds, queries[s])
+        if i == 0:
+            ak[...] = dk
+            av[...] = dv
+        else:
+            ak[...] += dk
+            av[...] += dv
+    dk_ref[...] = turn(ak[...].T, cosine, -sine).astype(BF)
+    dv_ref[...] = av[...].T.astype(BF)
+
+
+def attention_back(qs, kr, vb, out, lse, grad, cosine, sine, step=256):
+    width, length = qs.shape
+    heads = width // HEAD
+    row = pl.BlockSpec((HEAD, length), lambda h: (h, 0))
+    table = pl.BlockSpec((HEAD // 2, length), lambda h: (0, 0))
+    line = pl.BlockSpec((1, 1, length), lambda h: (h, 0, 0))
+    shape = jax.ShapeDtypeStruct((width, length), BF)
+    return pl.pallas_call(
+        functools.partial(attention_back_body, step),
+        out_shape=[shape] * 3,
+        grid=(heads,),
+        in_specs=[row] * 4 + [line, row, table, table],
+        out_specs=[row] * 3,
+        scratch_shapes=[pltpu.VMEM((length, HEAD), F32)] * 2,
+        cost_estimate=pl.CostEstimate(
+            flops=10 * width * length * length,
+            transcendentals=heads * length * length,
+            bytes_accessed=width * length * 18,
+        ),
+        name="attention_back",
+    )(qs, kr, vb, out, lse, grad, cosine, sine)
+
+
+def swap(value):
+    return lax.ppermute(value, "core", [(0, 1), (1, 0)])
+
+
+def both(value):
+    return jnp.concatenate([value, swap(value)], axis=0)
+
+
+def contract(left, right, a, b):
+    return lax.dot_general(left, right, (((a,), (b,)), ((), ())), preferred_element_type=F32)
+
+
+def own_sum(partial):
+    half = partial.shape[0] // 2
+    return partial[:half] + swap(partial[half:].astype(BF)).astype(F32)
+
+
+def move_blocks(x, clips, groups):
+    c, z = lax.axis_index("core"), lax.axis_index("grp")
+    got = []
+    for t in range(clips):
+        pairs = []
+        for cc in range(2):
+            for zz in range(groups):
+                i = (t + zz) % clips
+                pairs.append((cc * groups + zz, (zz // clips) * groups + cc * clips + i))
+        block = lax.dynamic_index_in_dim(x, lax.rem(t + z, clips), 0, keepdims=False)
+        got.append(lax.ppermute(block, ("core", "grp"), pairs))
+    stacked = jnp.stack(got)
+    return jnp.stack(
+        [
+            lax.dynamic_index_in_dim(stacked, lax.rem(z - m + clips, clips), 0, keepdims=False)
+            for m in range(clips)
+        ]
+    )
+
+
+def paired(
+    tokens,
+    positions,
+    ln1_gain,
+    ln1_bias,
+    w_qkv,
+    b_qkv,
+    w_out,
+    b_out,
+    ln2_gain,
+    ln2_bias,
+    w_up,
+    b_up,
+    w_down,
+    b_down,
+    cotangent,
+):
+    groups = lax.axis_size("grp")
+    clips, part, width = tokens.shape
+    hidden = w_down.shape[0] * groups
+    own = clips * part
+    length = 2 * own
+    c, z = lax.axis_index("core"), lax.axis_index("grp")
+    wide = width // 2
+    deep = hidden // 2
+    row = width // groups
+
+    def pick(value, axis):
+        return lax.dynamic_index_in_dim(value, c, axis, keepdims=False)
+
+    halves = [
+        pick(w_qkv.reshape(row, 3, groups, 2, row // 2), 3).reshape(row, 3 * wide),
+        pick(w_out.reshape(2, row // 2, width), 0),
+        pick(w_up.reshape(row, groups, 2, deep // groups), 2).reshape(row, deep),
+        pick(w_down.reshape(2, deep // groups, width), 0),
+    ]
+    halves = [h.reshape(4, 2, h.shape[0] // 8, h.shape[1]) for h in halves]
+    bq, bu = b_qkv.shape[0] // row, b_up.shape[0] // row
+    small = jnp.concatenate(
+        [ln1_gain, ln1_bias, b_out, ln2_gain, ln2_bias, b_down, b_qkv, b_up]
+    ).reshape(6 + bq + bu, row)
+    lines = small.shape[0]
+    small = jnp.pad(small, ((0, -lines % 16), (0, 0)))
+    pos = jnp.pad(jnp.moveaxis(positions, 0, 1).astype(F32), ((0, 0), (0, 5), (0, 0)))
+    wq, wo, w1, w2, small, x, pos = gather(halves, small, tokens, pos, groups)
+    wq = wq.reshape(width, 3 * wide)
+    wo = wo.reshape(wide, width)
+    w1 = w1.reshape(width, deep)
+    w2 = w2.reshape(deep, width)
+    small = small.astype(F32)
+    g1, b1, bo, g2, b2, bd = (small[:, n].reshape(1, width) for n in range(6))
+    bq_own = pick(small[:, 6 : 6 + bq].reshape(3, groups, 2, row // 2), 2).reshape(3 * wide, 1)
+    bu_own = pick(small[:, 6 + bq : lines].reshape(groups, 2, deep // groups), 1).reshape(1, deep)
+
+    grad_out = move_blocks(cotangent, clips, groups).reshape(own, width)
+    grad_all = both(grad_out)
+    grad_f = grad_out.astype(F32)
+
+    pos = jnp.moveaxis(pos[:, :3], 1, 0).reshape(3, own)
+    pos = jnp.concatenate([pos, swap(pos)], axis=1)
+    pair = jnp.arange(HEAD // 2)
+    band = (pair >= 10).astype(jnp.int32) + (pair >= 21).astype(jnp.int32)
+    begin = jnp.where(band == 0, 0, jnp.where(band == 1, 10, 21))
+    count = jnp.where(band == 0, 10, 11)
+    freq = jnp.power(F32(10000.0), -(pair - begin).astype(F32) / count.astype(F32))
+    band = band[:, None]
+    chosen = jnp.where(band == 0, pos[0:1], jnp.where(band == 1, pos[1:2], pos[2:3]))
+    angles = chosen * freq[:, None]
+    cosine, sine = jnp.cos(angles), jnp.sin(angles)
+
+    x = x.reshape(own, width).astype(F32)
+    n1, r1 = normalize(x)
+    h1 = both((n1 * g1 + b1).astype(BF))
+    qkv = contract(wq, h1, 0, 1) + bq_own
+    qs, kr, vb, mixed, lse = attention(qkv, cosine, sine)
+    x2 = x + own_sum(contract(mixed, wo, 0, 0)) + bo
+    n2, r2 = normalize(x2)
+    h2 = both((n2 * g2 + b2).astype(BF))
+    u = contract(h2, w1, 1, 0) + bu_own
+    cdf = 0.5 * (1.0 + lax.erf(u * F32(0.7071067811865476)))
+    act = (u * cdf).astype(BF)
+    slope = (cdf + u * jnp.exp(-0.5 * u * u) * F32(0.3989422804014327)).astype(BF)
+    result = (x2 + own_sum(contract(act, w2, 1, 0)) + bd).astype(BF)
+    output = move_blocks(result.reshape(clips, part, width), clips, groups)
+
+    gw2 = contract(act, grad_all, 0, 0).astype(BF)
+    gu = (contract(grad_all, w2, 1, 1) * slope.astype(F32)).astype(BF)
+    gw1 = contract(h2, gu, 0, 0).astype(BF)
+    gbu = jnp.sum(gu.astype(F32), axis=0)
+    dh2 = own_sum(contract(gu, w1, 1, 1))
+    gg2, gb2 = jnp.sum(dh2 * n2, axis=0), jnp.sum(dh2, axis=0)
+    dx2 = grad_f + norm_back(dh2 * g2, n2, r2)
+    low = dx2.astype(BF)
+    low_all = both(low)
+    gwo = contract(mixed, low_all, 1, 0).astype(BF)
+    da = contract(wo, low_all, 1, 1).astype(BF)
+    dqkv = jnp.concatenate(attention_back(qs, kr, vb, mixed, lse, da, cosine, sine), axis=0)
+    gwq = contract(h1, dqkv, 0, 1).astype(BF)
+    gbq = jnp.sum(dqkv.astype(F32), axis=1)
+    dh1 = own_sum(contract(dqkv, wq, 0, 1))
+    gg1, gb1 = jnp.sum(dh1 * n1, axis=0), jnp.sum(dh1, axis=0)
+    gx = (dx2 + norm_back(dh1 * g1, n1, r1)).astype(BF)
+
+    mine = (jnp.arange(2) == c).astype(F32)
+    gbq = gbq.reshape(3, groups, 1, row // 2) * mine[None, None, :, None]
+    gbu = gbu.reshape(groups, 1, deep // groups) * mine[None, :, None]
+    sums = jnp.concatenate(
+        [
+            gg1,
+            gb1,
+            jnp.sum(low.astype(F32), axis=0),
+            gg2,
+            gb2,
+            jnp.sum(grad_f, axis=0),
+            gbq.reshape(-1),
+            gbu.reshape(-1),
+        ]
+    ).reshape(lines, width)
+    sums = jnp.pad(sums, ((0, -lines % 8), (0, 0)))
+    grads = [g.reshape(groups, 2, 2, 2, g.shape[0] // (8 * groups), g.shape[1]) for g in (gwq, gwo, gw1, gw2)]
+    gwq, gwo, gw1, gw2, sums, gx = reduce(grads, sums, gx.reshape(clips, part, width), groups)
+
+    gwq = gwq.reshape(2, row, 3, groups, row // 2)
+    gwq = jnp.transpose(gwq, (1, 2, 3, 0, 4)).reshape(row, 3 * width).astype(F32)
+    gw1 = gw1.reshape(2, row, groups, deep // groups)
+    gw1 = jnp.transpose(gw1, (1, 2, 0, 3)).reshape(row, hidden).astype(F32)
+    gwo = gwo.reshape(row, width).astype(F32)
+    gw2 = gw2.reshape(hidden // groups, width).astype(F32)
+    cut = lambda v: lax.dynamic_index_in_dim(v.reshape(groups, -1), z, 0, keepdims=False)
+    gg1, gb1, gbo, gg2, gb2, gbd = (cut(sums[n]) for n in range(6))
+    return (
+        output,
+        gx,
+        gg1,
+        gb1,
+        gwq,
+        cut(sums[6 : 6 + bq]),
+        gwo,
+        gbo,
+        gg2,
+        gb2,
+        gw1,
+        cut(sums[6 + bq : lines]),
+        gw2,
+        gbd,
+    )
+
+
+def paired_specs():
+    rep = ("rp", "core")
+    ins = (P(rep, "grp", None), P(None, rep, "grp"))
+    one, two = P("grp"), P("grp", None)
+    ins += (one, one, two, one, two, one, one, one, two, one, two, one, P(rep, "grp", None))
+    outs = (P(rep, "grp", None),) * 2
+    outs += (one, one, two, one, two, one, one, one, two, one, two, one)
+    return ins, outs
 
 
 def rotary_angles(positions):
@@ -378,7 +1032,7 @@
     )
 
 
-def solution(mesh):
+def spread(mesh):
     placed = (
         P("rep", "grp", None),
         P(None, "rep", "grp"),
@@ -418,3 +1072,20 @@
         ),
         check_vma=False,
     )
+
+
+def solution(mesh):
+    reps, groups = mesh.devices.shape
+    flat = mesh.devices.reshape(-1)
+
+    def run(*args):
+        clips = args[0].shape[0] // reps
+        if reps == 8 and groups == 2 * clips:
+            split = Mesh(flat.reshape(reps // 2, 2, groups), ("rp", "core", "grp"))
+            ins, outs = paired_specs()
+            return jax.shard_map(
+                paired, mesh=split, in_specs=ins, out_specs=outs, check_vma=False
+            )(*args)
+        return spread(mesh)(*args)
+
+    return run

time: 1500 us -> 609 us (0.41)
  waiting for transfers between devices: 996 us -> 35.3 us
  Pallas kernels: 0 us -> 330 us
  matrix products: 270 us -> 76 us
  blocking collectives: 101 us -> 0 us
  local copies, waits for them, and re-layouts: 45.4 us -> 87.3 us
  starting transfers between devices: 1.08 us -> 41.2 us
  other arithmetic: 63.2 us -> 27 us
  between operations: 17.9 us -> 1.76 us
    all_gather x8 -> x0, waiting for transfers between devices: 471 us -> none  [the longest x1 134 us: local(): lax.all_gather(w_up, 'grp', axis=0, tiled=True)]
    reduce_scatter x8 -> x0, waiting for transfers between devices: 462 us -> none  [the longest x1 147 us: local(): lax.psum_scatter(totals[10].astype(jnp.bfloat16), 'grp', scatter_dimensio...]
    pallas_call x0 -> x4, Pallas kernels: none -> 330 us  [the longest x1 171 us: reduce(): pl.pallas_call(functools.partial(reduce_body, groups, clips, count), out_...]
    dot_general x36 -> x12, matrix products: 270 us -> 76 us  [contract(): lax.dot_general(left, right, (((a,), (b,)), ((), ())), preferred_element_...]
    all_gather x8 -> x0, blocking collectives: 72.9 us -> none  [the longest x1 13.3 us: local(): lax.all_gather(b_up, 'grp', axis=0, tiled=True)]
    psum x1 -> x0, waiting for transfers between devices: 59.6 us -> none  [local(): lax.psum(owned[2].astype(jnp.bfloat16), 'rep').astype(jnp.float32)]
    ppermute x0 -> x13, starting transfers between devices: none -> 41.2 us  [the longest x9 28 us: swap(): return lax.ppermute(value, 'core', [(0, 1), (1, 0)])]
    ppermute x0 -> x13, waiting for transfers between devices: none -> 35.3 us  [the longest x4 30.9 us: move_blocks(): got.append(lax.ppermute(block, ('core', 'grp'), pairs))]
  transfers between devices with their start and end apart: 17 -> 13, of which waited for: 14 -> 5; matrix products, arithmetic and copies ran while one was open for 18% -> 8% of each run, Pallas kernels for 0% -> 0%
where the time goes in v1:
time: 609 us; the launch traced here: 598 us
  Pallas kernels  330 us (54%)
  local copies, waits for them, and re-layouts  87.3 us (14%)
  matrix products  76 us (12%)
  starting transfers between devices  41.2 us (7%)
  waiting for transfers between devices  35.3 us (6%)
  other arithmetic  27 us (4%)
    pallas_call x1, Pallas kernels, reduce(): pl.pallas_call(functools.partial(reduce_body, groups, clips, count), out_...  171 us
    pallas_call x1, Pallas kernels, gather(): pl.pallas_call(functools.partial(gather_body, groups, clips, count), out_...  106 us
    dot_general x12, matrix products, contract(): lax.dot_general(left, right, (((a,), (b,)), ((), ())), preferred_element_...  76 us
    ppermute x4, waiting for transfers between devices, move_blocks(): got.append(lax.ppermute(block, ('core', 'grp'), pairs))  30.9 us
    ppermute x9, starting transfers between devices, swap(): return lax.ppermute(value, 'core', [(0, 1), (1, 0)])  28 us
    pallas_call x1, Pallas kernels, attention_back(): pl.pallas_call(functools.partial(attention_back_body, step), out_shape=[s...  27.9 us
    pallas_call x1, Pallas kernels, attention(): pl.pallas_call(functools.partial(attention_body, step), out_shape=[shape]...  24.7 us
    convert_element_type x3, local copies, waits for them, and re-layouts, paired(): gw1 = jnp.transpose(gw1, (1, 2, 0, 3)).reshape(row, hidden).astype(F32)  18.5 us
  transfers between devices with their start and end apart: 13, of which 5 were waited for; matrix products, arithmetic and copies ran while one was open for 8% of the time, Pallas kernels for 0%

profile of v1, /device:TPU:9, one launch (start us, length us, event | category | flops | bytes accessed | tf_op | source)
XLA Modules:
  0.0 598.3 jit_solution(16290944524507359796)
XLA Ops:
  15.0 5.0 dynamic-slice_reduce_fusion.1
  24.7 6.5 %dynamic-slice_reduce_fusion = bf16[256,4,512]{2,1,0:T(4,128)(2,1)S(1)} fusion(bf16[256,4,2,512]{3,2,1,0:T(2,128)(2,1)S(1)} %reshape.247, s32[]{:T(128)S(6)} %select_n.73), kind=kLoop, calls=%fused_computation.58 | loop fusion | bytes 2097156 | tf_op jit(solution)/shard_map/jit(dynamic_index_in_dim)/dynamic_slice | solution.py:534
  34.0 106.3 %gather.1 = (bf16[4,4,2,32,1536]{4,3,2,1,0:T(8,128)(2,1)}, bf16[4,4,2,16,1024]{4,3,2,1,0:T(8,128)(2,1)}, bf16[4,4,2,32,2048]{4,3,2,1,0:T(8,128)(2,1)}, bf16[4,4,...) custom-call(bf16[4,2,32,1536]{3,2,1,0:T(8,128)(2,1)} %reshape_reshap, ...), custom_call_target="tpu_custom_call" | custom-call | tf_op jit(solution)/shard_map/gather/pallas_call | solution.py:176
  144.1 26.3 %collective-permute-start = (bf16[512,1024]{1,0:T(8,128)(2,1)S(1)}, bf16[512,1024]{1,0:T(8,128)(2,1)S(1)}, u32[]{:S(2)}, u32[]{:S(2)}) collective-permute-start(bf16[512,1024]{1,0:T(8,128)(2,1)S(1)} %fusion.18), channel_id=1, source_target_pairs={{0,4},{4,0},{1,5},{5,1},{2,6},{6,2},{3,7},{7,3},{8,12},{12,8},{9,1... | collective-permute-start | bytes 3145736 | tf_op jit(solution)/shard_map/ppermute | solution.py:470
  174.0 8.8 %convolution_add_fusion.q_ref.k_ref.v_ref = f32[1536,1024]{1,0:T(8,128)} fusion(bf16[1024,1536]{1,0:T(8,128)(2,1)} %bitcast.176, f32[1536]{0:T(1024)S(1)} %add.193, bf16[512,1024]{1,0:T(8,128)(2,1)S(1)} %collective-permute-done, bf16[512,1024]{1,0:T(8,128)(2,1)S(1)} %fusion.18), kind=kOutput, calls=%fused_computation.11 | convolution fusion | flops 3226992640 | bytes 11540480 | tf_op jit(solution)/shard_map/dot_general | solution.py:478
  182.8 24.7 %attention.1 = (bf16[512,1024]{1,0:T(8,128)(2,1)}, bf16[512,1024]{1,0:T(8,128)(2,1)}, bf16[512,1024]{1,0:T(8,128)(2,1)}, bf16[512,1024]{1,0:T(8,128)(2,1)}, f32[8,1,1024]{2,1,0:T(1,128)}) custom-call(f32[1536,1024]{1,0:T(8,128)} %convolution_add_fusion.q_ref.k_ref.v_ref, f32[1536,1024]{1,0:T(8,128)} %convolution_add_fusion.q_ref.k_ref.v_ref, ...), custom_call_target="tpu_custom_call" | custom-call | flops 2147483648 | bytes 12582912 | tf_op jit(solution)/shard_map/attention/pallas_call | solution.py:402
  217.7 5.8 collective-permute-start.8
  225.5 15.5 %collective-permute-done.8 = bf16[256,1024]{1,0:T(8,128)(2,1)} collective-permute-done((bf16[256,1024]{1,0:T(8,128)(2,1)}, bf16[256,1024]{1,0:T(8,128)(2,1)}, u32[]{:S(2)}, u32[]{:S(2)}) %collective-permute-start.8) | collective-permute-done | bytes 524320 | tf_op jit(solution)/shard_map/ppermute | solution.py:496
  241.0 5.6 collective-permute-done.7
  249.1 7.9 %multiply_convert_fusion.1 = (bf16[1024,2048]{1,0:T(8,128)(2,1)S(1)}, f32[1024,2048]{1,0:T(8,128)S(1)}) fusion(f32[2048]{0:T(1024)S(1)} %bitcast.163, bf16[1024,2048]{1,0:T(8,128)(2,1)S(1)} %bitcast.172, bf16[512,1024]{1,0:T(8,128)(2,1)} %collective-permute-done.3, bf16[512,1024]{1,0:T(8,128)(2,1)} %add_convert_fusion), kind=kOutput, calls=%fused_computation.8 | convolution fusion | flops 4311744512 | bytes 18882560 | tf_op jit(solution)/shard_map/dot_general | solution.py:478
  257.1 6.1 %fusion.52 = f32[1024,1024]{1,0:T(8,128)} fusion(bf16[1024,2048]{1,0:T(8,128)(2,1)S(1)} %get-tuple-element.97, bf16[2048,1024]{1,0:T(8,128)(2,1)S(1)} %bitcast.174), kind=kOutput, calls=%fused_computation.156 | convolution fusion | flops 4294967296 | bytes 12582912 | tf_op jit(solution)/shard_map/dot_general | solution.py:478
  263.2 10.0 %convert_reduce_fusion = (f32[2048]{0:T(1024)S(1)}, bf16[1024,2048]{1,0:T(8,128)(2,1)}) fusion(f32[1024,2048]{1,0:T(8,128)S(1)} %get-tuple-element.98, f32[2048]{0:T(1024)S(1)} %bitcast.164, bf16[2048,1024]{1,0:T(8,128)(2,1)S(1)} %bitcast.175, bf16[512,1024]{1,0:T(8,128)(2,1)S(1)} %collective-permute-done.9, bf16[512,1024]{1,0:T(8,128)(2,1)S(1)} %bitcast.125), kind=kOutput, calls=%fused_computation.6 | convolution fusion | flops 4330616832 | bytes 18890752 | tf_op jit(solution)/shard_map/dot_general | solution.py:478
  273.2 8.3 %fusion.53 = f32[1024,1024]{1,0:T(8,128)} fusion(bf16[1024,2048]{1,0:T(8,128)(2,1)} %get-tuple-element.100, bf16[1024,2048]{1,0:T(8,128)(2,1)S(1)} %bitcast.173), kind=kOutput, calls=%fused_computation.157 | convolution fusion | flops 4294967296 | bytes 12582912 | tf_op jit(solution)/shard_map/dot_general | solution.py:478
  285.7 8.7 %convolution_convert_fusion.1 = bf16[2048,1024]{1,0:T(8,128)(2,1)} fusion(bf16[1024,2048]{1,0:T(8,128)(2,1)} %copy-done.34, bf16[512,1024]{1,0:T(8,128)(2,1)S(1)} %copy-done.32, bf16[512,1024]{1,0:T(8,128)(2,1)S(1)} %bitcast.126), kind=kOutput, calls=%fused_computation.13 | convolution fusion | flops 4301258752 | bytes 10485760 | tf_op jit(solution)/shard_map/dot_general | solution.py:478
  299.5 5.5 collective-permute-start.5
  305.1 7.7 %convolution_convert_fusion.2 = bf16[1024,2048]{1,0:T(8,128)(2,1)} fusion(bf16[1024,2048]{1,0:T(8,128)(2,1)S(1)} %copy-done.33, bf16[512,1024]{1,0:T(8,128)(2,1)} %collective-permute-done.3, bf16[512,1024]{1,0:T(8,128)(2,1)} %add_convert_fusion), kind=kOutput, calls=%fused_computation.14 | convolution fusion | flops 4301258752 | bytes 10485760 | tf_op jit(solution)/shard_map/dot_general | solution.py:478
  312.8 9.7 %collective-permute-done.5 = bf16[256,1024]{1,0:T(8,128)(2,1)S(1)} collective-permute-done((bf16[256,1024]{1,0:T(8,128)(2,1)S(1)}, bf16[256,1024]{1,0:T(8,128)(2,1)S(1)}, u32[]{:S(2)}, u32[]{:S(2)}) %collective-permute-start.5) | collective-permute-done | bytes 524320 | tf_op jit(solution)/shard_map/ppermute | solution.py:496
  326.3 27.9 %attention_back.1 = (bf16[512,1024]{1,0:T(8,128)(2,1)}, bf16[512,1024]{1,0:T(8,128)(2,1)}, bf16[512,1024]{1,0:T(8,128)(2,1)}) custom-call(bf16[512,1024]{1,0:T(8,128)(2,1)} %get-tuple-element.43.q_ref, bf16[512,1024]{1,0:T(8,128)(2,1)} %get-tuple-element.44.k_ref, bf16[512,1024]{1,0:T(8,128)(2,1)} %get-tuple-element.45.v_ref, ...), custom_call_target="tpu_custom_call" | custom-call | flops 5368709120 | bytes 9437184 | tf_op jit(solution)/shard_map/attention_back/pallas_call | solution.py:453
  359.2 5.0 fusion.54
  370.0 5.1 convolution_convert_fusion
  380.8 170.9 %reduce.38 = (bf16[2,4,2,32,1536]{4,3,2,1,0:T(8,128)(2,1)}, bf16[2,4,2,16,1024]{4,3,2,1,0:T(8,128)(2,1)}, bf16[2,4,2,32,2048]{4,3,2,1,0:T(8,128)(2,1)}, bf16[2,4...) custom-call(bf16[4,2,2,2,32,1536]{5,4,3,2,1,0:T(8,128)(2,1)} %bitcast.132, ...), custom_call_target="tpu_custom_call" | custom-call | tf_op jit(solution)/shard_map/reduce/pallas_call | solution.py:349
  568.5 5.6 reshape.268
  578.6 7.5 %copy.38 = f32[256,4,2,512]{3,2,1,0:T(2,128)} copy(f32[256,4,2,512]{3,1,0,2:T(4,128)} %bitcast.122) | data formatting | bytes 8388608 | tf_op jit(solution)/shard_map/convert_element_type | solution.py:631
  586.0 6.6 %reshape.270 = f32[256,4096]{1,0:T(8,128)} reshape(f32[256,4,2,512]{3,2,1,0:T(2,128)} %copy.38) | data formatting | bytes 8388608 | tf_op jit(solution)/shard_map/convert_element_type | solution.py:631
  (200 shorter events, 99.5 us)
Async XLA Ops:
  0.6 9.3 %copy-start = (bf16[1024,1024]{1,0:T(8,128)(2,1)S(1)}, bf16[1024,1024]{1,0:T(8,128)(2,1)}, u32[]{:S(2)}) copy-start(bf16[1024,1024]{1,0:T(8,128)(2,1)} %param.27) | copy-start | bytes 6291460
  140.3 30.0 %copy-start.24 = (f32[2,8,256]{2,1,0:T(8,128)S(1)}, f32[2,8,256]{2,1,0:T(8,128)}, u32[]{:S(2)}) copy-start(f32[2,8,256]{2,1,0:T(8,128)} %get-tuple-element.38) | copy-start | bytes 49156
  144.0 38.7 %copy-start.16 = (bf16[512,1024]{1,0:T(8,128)(2,1)}, bf16[512,1024]{1,0:T(8,128)(2,1)S(1)}, u32[]{:S(2)}) copy-start(bf16[512,1024]{1,0:T(8,128)(2,1)S(1)} %fusion.18) | copy-start | bytes 3145732
  144.1 29.9 %collective-permute-start = (bf16[512,1024]{1,0:T(8,128)(2,1)S(1)}, bf16[512,1024]{1,0:T(8,128)(2,1)S(1)}, u32[]{:S(2)}, u32[]{:S(2)}) collective-permute-start(bf16[512,1024]{1,0:T(8,128)(2,1)S(1)} %fusion.18), channel_id=1, source_target_pairs={{0,4},{4,0},{1,5},{5,1},{2,6},{6,2},{3,7},{7,3},{8,12},{12,8},{9,1... | collective-permute-start | bytes 3145736 | tf_op jit(solution)/shard_map/ppermute | solution.py:470
  170.4 2.3 collective-permute-start.1
  174.0 8.8 %copy-start.28 = (bf16[512,1024]{1,0:T(8,128)(2,1)}, bf16[512,1024]{1,0:T(8,128)(2,1)S(1)}, u32[]{:S(2)}) copy-start(bf16[512,1024]{1,0:T(8,128)(2,1)S(1)} %collective-permute-done) | copy-start | bytes 3145732
  182.8 24.7 %copy-start.21 = (bf16[4,4,2,16,1024]{4,3,2,1,0:T(8,128)(2,1)S(1)}, bf16[4,4,2,16,1024]{4,3,2,1,0:T(8,128)(2,1)}, u32[]{:S(2)}) copy-start(bf16[4,4,2,16,1024]{4,3,2,1,0:T(8,128)(2,1)} %get-tuple-element.40) | copy-start | bytes 3145732
  210.1 2.7 collective-permute-start.2
  215.1 33.6 %collective-permute-start.3 = (bf16[512,1024]{1,0:T(8,128)(2,1)}, bf16[512,1024]{1,0:T(8,128)(2,1)}, u32[]{:S(2)}, u32[]{:S(2)}) collective-permute-start(bf16[512,1024]{1,0:T(8,128)(2,1)} %add_convert_fusion), channel_id=1, source_target_pairs={{0,4},{4,0},{1,5},{5,1},{2,6},{6,2},{3,7},{7,3},{8,12},{12,8},{9,1... | collective-permute-start | bytes 3145736 | tf_op jit(solution)/shard_map/ppermute | solution.py:470
  217.7 23.3 %collective-permute-start.8 = (bf16[256,1024]{1,0:T(8,128)(2,1)}, bf16[256,1024]{1,0:T(8,128)(2,1)}, u32[]{:S(2)}, u32[]{:S(2)}) collective-permute-start(bf16[256,1024]{1,0:T(8,128)(2,1)} %get-tuple-element.78), channel_id=1, source_target_pairs={{0,1},{1,0},{2,5},{3,4},{4,3},{5,2},{6,7},{7,6},{8,9},{9,8},{10,13... | collective-permute-start | bytes 1572872 | tf_op jit(solution)/shard_map/ppermute | solution.py:496
  223.5 23.1 %collective-permute-start.7 = (bf16[256,1024]{1,0:T(8,128)(2,1)}, bf16[256,1024]{1,0:T(8,128)(2,1)}, u32[]{:S(2)}, u32[]{:S(2)}) collective-permute-start(bf16[256,1024]{1,0:T(8,128)(2,1)} %get-tuple-element.79), channel_id=1, source_target_pairs={{0,0},{1,1},{2,4},{3,5},{4,2},{5,3},{6,6},{7,7},{8,8},{9,9},{10,12... | collective-permute-start | bytes 1572872 | tf_op jit(solution)/shard_map/ppermute | solution.py:496
  248.5 14.7 %copy-start.8 = (bf16[2,256,1024]{2,1,0:T(8,128)(2,1)}, bf16[2,256,1024]{2,1,0:T(8,128)(2,1)S(1)}, u32[]{:S(2)}) copy-start(bf16[2,256,1024]{2,1,0:T(8,128)(2,1)S(1)} %pad_maximum_fusion.13) | copy-start | bytes 3145732
  248.5 14.7 %collective-permute-start.9 = (bf16[512,1024]{1,0:T(8,128)(2,1)S(1)}, bf16[512,1024]{1,0:T(8,128)(2,1)S(1)}, u32[]{:S(2)}, u32[]{:S(2)}) collective-permute-start(bf16[512,1024]{1,0:T(8,128)(2,1)S(1)} %bitcast.124), channel_id=1, source_target_pairs={{0,4},{4,0},{1,5},{5,1},{2,6},{6,2},{3,7},{7,3},{8,12},{12,8},{9,1... | collective-permute-start | bytes 3145736 | tf_op jit(solution)/shard_map/ppermute | solution.py:470
  249.1 8.0 %copy-start.26 = (bf16[4,4,2,64,1024]{4,3,2,1,0:T(8,128)(2,1)S(1)}, bf16[4,4,2,64,1024]{4,3,2,1,0:T(8,128)(2,1)}, u32[]{:S(2)}) copy-start(bf16[4,4,2,64,1024]{4,3,2,1,0:T(8,128)(2,1)} %get-tuple-element.42) | copy-start | bytes 12582916
  263.2 10.0 %copy-start.31 = (bf16[512,1024]{1,0:T(8,128)(2,1)}, bf16[512,1024]{1,0:T(8,128)(2,1)S(1)}, u32[]{:S(2)}) copy-start(bf16[512,1024]{1,0:T(8,128)(2,1)S(1)} %collective-permute-done.9) | copy-start | bytes 3145732
  285.1 9.4 %copy-start.4 = (f32[1024,1024]{1,0:T(8,128)S(1)}, f32[1024,1024]{1,0:T(8,128)}, u32[]{:S(2)}) copy-start(f32[1024,1024]{1,0:T(8,128)} %fusion.53) | copy-start | bytes 12582916
  285.2 10.4 %collective-permute-start.4 = (bf16[512,1024]{1,0:T(8,128)(2,1)S(1)}, bf16[512,1024]{1,0:T(8,128)(2,1)S(1)}, u32[]{:S(2)}, u32[]{:S(2)}) collective-permute-start(bf16[512,1024]{1,0:T(8,128)(2,1)S(1)} %slice.178), channel_id=1, source_target_pairs={{0,4},{4,0},{1,5},{5,1},{2,6},{6,2},{3,7},{7,3},{8,12},{12,8},{9,1... | collective-permute-start | bytes 3145736 | tf_op jit(solution)/shard_map/ppermute | solution.py:470
  285.4 9.1 %collective-permute-start.10 = (bf16[512,1024]{1,0:T(8,128)(2,1)S(1)}, bf16[512,1024]{1,0:T(8,128)(2,1)S(1)}, u32[]{:S(2)}, u32[]{:S(2)}) collective-permute-start(bf16[512,1024]{1,0:T(8,128)(2,1)S(1)} %slice.177), channel_id=1, source_target_pairs={{0,4},{4,0},{1,5},{5,1},{2,6},{6,2},{3,7},{7,3},{8,12},{12,8},{9,1... | collective-permute-start | bytes 3145736 | tf_op jit(solution)/shard_map/ppermute | solution.py:470
  296.7 8.4 %copy-start.33 = (bf16[1024,2048]{1,0:T(8,128)(2,1)S(1)}, bf16[1024,2048]{1,0:T(8,128)(2,1)}, u32[]{:S(2)}) copy-start(bf16[1024,2048]{1,0:T(8,128)(2,1)} %get-tuple-element.100) | copy-start | bytes 12582916
  299.4 24.6 %copy-start.14 = (bf16[512,1024]{1,0:T(8,128)(2,1)}, bf16[512,1024]{1,0:T(8,128)(2,1)S(1)}, u32[]{:S(2)}) copy-start(bf16[512,1024]{1,0:T(8,128)(2,1)S(1)} %get-tuple-element.71) | copy-start | bytes 3145732
  299.4 13.4 %collective-permute-start.6 = (bf16[256,1024]{1,0:T(8,128)(2,1)S(1)}, bf16[256,1024]{1,0:T(8,128)(2,1)S(1)}, u32[]{:S(2)}, u32[]{:S(2)}) collective-permute-start(bf16[256,1024]{1,0:T(8,128)(2,1)S(1)} %get-tuple-element.82), channel_id=1, source_target_pairs={{0,1},{1,0},{2,5},{3,4},{4,3},{5,2},{6,7},{7,6},{8,9},{9,8},{10,13... | collective-permute-start | bytes 1572872 | tf_op jit(solution)/shard_map/ppermute | solution.py:496
  299.5 23.0 %collective-permute-start.5 = (bf16[256,1024]{1,0:T(8,128)(2,1)S(1)}, bf16[256,1024]{1,0:T(8,128)(2,1)S(1)}, u32[]{:S(2)}, u32[]{:S(2)}) collective-permute-start(bf16[256,1024]{1,0:T(8,128)(2,1)S(1)} %get-tuple-element.83), channel_id=1, source_target_pairs={{0,0},{1,1},{2,4},{3,5},{4,2},{5,3},{6,6},{7,7},{8,8},{9,9},{10,12... | collective-permute-start | bytes 1572872 | tf_op jit(solution)/shard_map/ppermute | solution.py:496
  305.0 19.0 %collective-permute-start.11 = (bf16[512,1024]{1,0:T(8,128)(2,1)S(1)}, bf16[512,1024]{1,0:T(8,128)(2,1)S(1)}, u32[]{:S(2)}, u32[]{:S(2)}) collective-permute-start(bf16[512,1024]{1,0:T(8,128)(2,1)S(1)} %get-tuple-element.71), channel_id=1, source_target_pairs={{0,4},{4,0},{1,5},{5,1},{2,6},{6,2},{3,7},{7,3},{8,12},{12,8},{9,1... | collective-permute-start | bytes 3145736 | tf_op jit(solution)/shard_map/ppermute | solution.py:470
  366.1 9.0 %collective-permute-start.12 = (bf16[512,1024]{1,0:T(8,128)(2,1)S(1)}, bf16[512,1024]{1,0:T(8,128)(2,1)S(1)}, u32[]{:S(2)}, u32[]{:S(2)}) collective-permute-start(bf16[512,1024]{1,0:T(8,128)(2,1)S(1)} %slice.176), channel_id=1, source_target_pairs={{0,4},{4,0},{1,5},{5,1},{2,6},{6,2},{3,7},{7,3},{8,12},{12,8},{9,1... | collective-permute-start | bytes 3145736 | tf_op jit(solution)/shard_map/ppermute | solution.py:470
  (24 other events, 75.9 us)

commit v2 on v1

--- a/solution.py
+++ b/solution.py
@@ -87,12 +87,30 @@
     return start, finish
 
 
-def gather_body(groups, clips, count, *refs):
-    halves, (small, x, pos) = refs[:count], refs[count : count + 3]
-    outs = refs[count + 3 : 2 * count + 3]
-    small_o, x_o, pos_o = refs[2 * count + 3 : 2 * count + 6]
-    zs, zr, xs, xr, ys, yr, fs, fr, ls, ss, sr, ts, tr = refs[2 * count + 6 :]
+def cuts(whole, half, c, blocks):
+    if blocks == 0:
+        return [(whole.at[c], half)]
+    size = half.shape[3] // blocks
+    return [
+        (
+            whole.at[:, :, :, pl.ds(pl.multiple_of((2 * b + c) * size, size), size)],
+            half.at[:, :, :, pl.ds(b * size, size)],
+        )
+        for b in range(blocks)
+    ]
+
+
+def gather_body(groups, clips, blocks, *refs):
+    count = len(blocks)
+    raw, (small, x, pos, dy) = refs[:count], refs[count : count + 4]
+    outs = refs[count + 4 : 2 * count + 4]
+    small_o, x_o, pos_o, dy_o = refs[2 * count + 4 : 2 * count + 8]
+    halves = refs[2 * count + 8 : 3 * count + 8]
+    zs, zr, xs, xr, ys, yr, fs, fr, hs, ls, ss, sr, ts, tr, us, ur = refs[3 * count + 8 :]
     p, c, z = where_am_i()
+    for w in range(count):
+        for src, dst in cuts(raw[w], halves[w], c, blocks[w]):
+            pltpu.make_async_copy(src, dst, hs.at[w]).start()
     enter(p, c, z, groups)
     col = [(p, c, lax.rem(z + k, groups)) for k in range(groups)]
     org = [lax.rem(z + groups - k, groups) for k in range(groups)]
@@ -105,17 +123,19 @@
     for s in smalls:
         s.start()
     keep = [pltpu.make_async_copy(small, small_o.at[z], ls.at[count])]
-    for w in range(count):
-        keep.append(pltpu.make_async_copy(halves[w], outs[w].at[z], ls.at[w]))
-    for k in keep:
-        k.start()
+    keep[0].start()
     first = {}
     for w in range(count):
+        pltpu.make_async_copy(halves[w], halves[w], hs.at[w]).wait()
+        keep.append(pltpu.make_async_copy(halves[w], outs[w].at[z], ls.at[w]))
+        keep[-1].start()
         for k in range(1, groups):
             first[w, k] = remote(
                 halves[w].at[p], outs[w].at[z, p], zs.at[w, k], zr.at[w, k], col[k]
             )
             first[w, k].start()
+    start_dy, finish_dy = move_tokens((dy,), (dy_o,), us, ur, p, c, z, clips)
+    start_dy()
     units = [(w, k) for w in range(count) for k in range(1, groups)]
     xc, yc, fa, fb = {}, {}, {}, {}
 
@@ -165,28 +185,38 @@
     for k in keep:
         k.wait()
     finish()
-
-
-def gather(halves, small, x, pos, groups):
-    count, clips = len(halves), x.shape[0]
+    finish_dy()
+
+
+def half_shape(raw, blocks):
+    return raw.shape[1:] if blocks == 0 else raw.shape[:3] + (raw.shape[3] // 2,)
+
+
+def gather(raw, blocks, small, x, pos, dy, groups):
+    count, clips = len(raw), x.shape[0]
     dma = pltpu.SemaphoreType.DMA
-    shapes = [jax.ShapeDtypeStruct((groups,) + h.shape, h.dtype) for h in halves]
+    halves = [half_shape(r, b) for r, b in zip(raw, blocks)]
+    shapes = [jax.ShapeDtypeStruct((groups,) + h, BF) for h in halves]
     shapes += [jax.ShapeDtypeStruct((groups,) + small.shape, small.dtype)]
-    shapes += [jax.ShapeDtypeStruct(x.shape, x.dtype), jax.ShapeDtypeStruct(pos.shape, pos.dtype)]
+    shapes += [jax.ShapeDtypeStruct(v.shape, v.dtype) for v in (x, pos, dy)]
     return pl.pallas_call(
-        functools.partial(gather_body, groups, clips, count),
+        functools.partial(gather_body, groups, clips, blocks),
         out_shape=shapes,
-        in_specs=[VM] * count + [VM, ANY, ANY],
+        in_specs=[ANY] * count + [VM, ANY, ANY, ANY],
         out_specs=[ANY] * len(shapes),
-        scratch_shapes=[dma((count, groups))] * 6
+        scratch_shapes=[pltpu.VMEM(h, BF) for h in halves]
+        + [dma((count, groups))] * 6
         + [dma((count, groups, 2))] * 2
-        + [dma((count + 1,)), dma((groups,)), dma((groups,)), dma((2, clips)), dma((2, clips))],
+        + [dma((count,)), dma((count + 1,)), dma((groups,)), dma((groups,))]
+        + [dma((2, clips))] * 2
+        + [dma((1, clips))] * 2,
         compiler_params=pltpu.CompilerParams(collective_id=0, has_side_effects=True),
         name="gather",
-    )(*halves, small, x, pos)
-
-
-def reduce_body(groups, clips, count, *refs):
+    )(*raw, small, x, pos, dy)
+
+
+def reduce_body(groups, clips, blocks, *refs):
+    count = len(blocks)
     grads, (small, gx) = refs[:count], refs[count : count + 2]
     outs = refs[count + 2 : 2 * count + 2]
     small_o, gx_o = refs[2 * count + 2 : 2 * count + 4]
@@ -194,8 +224,8 @@
     own_a, own_b, one_a, one_b, two_a, two_b, mine, three, full = (
         scratch[i * count : (i + 1) * count] for i in range(9)
     )
-    small_r, small_z = scratch[9 * count : 9 * count + 2]
-    (os, s1, r1, s2, r2, s3, r3, s4, r4, s5, r5, cs, cr, ls, ss, sr, ts, tr) = scratch[9 * count + 2 :]
+    small_s, small_r, small_z = scratch[9 * count : 9 * count + 3]
+    (os, s1, r1, s2, r2, s3, r3, s4, r4, s5, r5, cs, cr, ls, ss, sr, ts, tr) = scratch[9 * count + 3 :]
     p, c, z = where_am_i()
     hi, lo = lax.div(p, 2), lax.rem(p, 2)
     enter(p, c, z, groups)
@@ -203,14 +233,15 @@
     xn, yn, cn = (p ^ 1, c, z), (p ^ 2, c, z), (p, c ^ 1, z)
     start, finish = move_tokens((gx,), (gx_o,), ts, tr, p, c, z, clips)
     start()
-    small_o[...] = small[...]
+    small_s[...] = small[...]
     for n, target in enumerate((cn, xn, yn)):
-        copy = remote(small_o, small_r.at[n], ss.at[n], sr.at[n], target)
+        copy = remote(small_s, small_r.at[n], ss.at[n], sr.at[n], target)
         copy.start()
         copy.wait()
-        small_o[...] += small_r[n]
+        small_s[...] += small_r[n]
     tails = [
-        remote(small_o, small_z.at[k], ss.at[2 + k], sr.at[2 + k], col[k]) for k in range(1, groups)
+        remote(small_s.at[col[k][2]], small_z.at[k], ss.at[2 + k], sr.at[2 + k], col[k])
+        for k in range(1, groups)
     ]
     for t in tails:
         t.start()
@@ -279,8 +310,9 @@
         for n in range(2):
             f = full[w].at[p ^ 3, n]
             remote(f, f, s5.at[w, n], r5.at[w, n], xn).wait_recv()
-        pltpu.make_async_copy(full[w], outs[w].at[c], ls.at[w]).start()
-        remote(full[w], outs[w].at[c], cs.at[w], cr.at[w], cn).start()
+        for dst, src in cuts(outs[w], full[w], c, blocks[w]):
+            pltpu.make_async_copy(src, dst, ls.at[w]).start()
+            remote(src, dst, cs.at[w], cr.at[w], cn).start()
 
     lag = 3
     for n in range(len(units) + lag):
@@ -299,6 +331,7 @@
         stage_five(w)
     for k in range(1, groups):
         tails[k - 1].wait()
+    small_o[...] = small_s[z]
     for k in range(1, groups):
         small_o[...] += small_z[k]
     for u in units:
@@ -315,18 +348,21 @@
         for n in range(2):
             c4[w, n].wait_send()
             c5[w, n].wait_send()
-        pltpu.make_async_copy(full[w], outs[w].at[c], ls.at[w]).wait()
-        remote(full[w], outs[w].at[1 - c], cs.at[w], cr.at[w], cn).wait()
+        pltpu.make_async_copy(full[w], full[w], ls.at[w]).wait()
+        remote(full[w], full[w], cs.at[w], cr.at[w], cn).wait()
     finish()
 
 
-def reduce(grads, small, gx, groups):
+def reduce(grads, blocks, small, gx, groups):
     count, clips = len(grads), gx.shape[0]
     dma = pltpu.SemaphoreType.DMA
     tiles = [g.shape[4:] for g in grads]
-    shapes = [jax.ShapeDtypeStruct((2, 4, 2) + t, BF) for t in tiles]
+    shapes = [
+        jax.ShapeDtypeStruct((4, 2, t[0], 2 * t[1]) if b else (2, 4, 2) + t, BF)
+        for t, b in zip(tiles, blocks)
+    ]
     shapes += [
-        jax.ShapeDtypeStruct(small.shape, small.dtype),
+        jax.ShapeDtypeStruct(small.shape[1:], small.dtype),
         jax.ShapeDtypeStruct(gx.shape, gx.dtype),
     ]
     scratch = []
@@ -342,12 +378,16 @@
         (4, 2),
     ):
         scratch += [pltpu.VMEM(lead + t, BF) for t in tiles]
-    scratch += [pltpu.VMEM((3,) + small.shape, F32), pltpu.VMEM((groups,) + small.shape, F32)]
+    scratch += [
+        pltpu.VMEM(small.shape, F32),
+        pltpu.VMEM((3,) + small.shape, F32),
+        pltpu.VMEM(small.shape, F32),
+    ]
     pair = dma((count, groups, 2))
     scratch += [pair] * 5 + [dma((count, groups))] * 2 + [dma((count, 2))] * 4
     scratch += [dma((count,))] * 3 + [dma((2 + groups,))] * 2 + [dma((1, clips))] * 2
     return pl.pallas_call(
-        functools.partial(reduce_body, groups, clips, count),
+        functools.partial(reduce_body, groups, clips, blocks),
         out_shape=shapes,
         in_specs=[ANY] * count + [VM, ANY],
         out_specs=[ANY] * count + [VM, ANY],
@@ -533,31 +573,31 @@
     def pick(value, axis):
         return lax.dynamic_index_in_dim(value, c, axis, keepdims=False)
 
-    halves = [
-        pick(w_qkv.reshape(row, 3, groups, 2, row // 2), 3).reshape(row, 3 * wide),
-        pick(w_out.reshape(2, row // 2, width), 0),
-        pick(w_up.reshape(row, groups, 2, deep // groups), 2).reshape(row, deep),
-        pick(w_down.reshape(2, deep // groups, width), 0),
+    blocks = (3 * groups, 0, groups, 0)
+    raw = [
+        w.reshape(((4, 2) if b else (2, 4, 2)) + (w.shape[0] // (8 if b else 16), w.shape[1]))
+        for w, b in zip((w_qkv, w_out, w_up, w_down), blocks)
     ]
-    halves = [h.reshape(4, 2, h.shape[0] // 8, h.shape[1]) for h in halves]
     bq, bu = b_qkv.shape[0] // row, b_up.shape[0] // row
-    small = jnp.concatenate(
-        [ln1_gain, ln1_bias, b_out, ln2_gain, ln2_bias, b_down, b_qkv, b_up]
-    ).reshape(6 + bq + bu, row)
-    lines = small.shape[0]
-    small = jnp.pad(small, ((0, -lines % 16), (0, 0)))
+    vectors = [ln1_gain, ln1_bias, b_out, ln2_gain, ln2_bias, b_down]
+    vectors += [b_qkv[n * row : (n + 1) * row] for n in range(bq)]
+    vectors += [b_up[n * row : (n + 1) * row] for n in range(bu)]
+    lines = len(vectors)
+    place = lax.broadcasted_iota(jnp.int32, (lines + -lines % 8, row), 0)
+    small = jnp.zeros(place.shape, F32)
+    for n, v in enumerate(vectors):
+        small = jnp.where(place == n, v.astype(F32)[None, :], small)
     pos = jnp.pad(jnp.moveaxis(positions, 0, 1).astype(F32), ((0, 0), (0, 5), (0, 0)))
-    wq, wo, w1, w2, small, x, pos = gather(halves, small, tokens, pos, groups)
+    wq, wo, w1, w2, small, x, pos, dy = gather(raw, blocks, small, tokens, pos, cotangent, groups)
     wq = wq.reshape(width, 3 * wide)
     wo = wo.reshape(wide, width)
     w1 = w1.reshape(width, deep)
     w2 = w2.reshape(deep, width)
-    small = small.astype(F32)
     g1, b1, bo, g2, b2, bd = (small[:, n].reshape(1, width) for n in range(6))
     bq_own = pick(small[:, 6 : 6 + bq].reshape(3, groups, 2, row // 2), 2).reshape(3 * wide, 1)
     bu_own = pick(small[:, 6 + bq : lines].reshape(groups, 2, deep // groups), 1).reshape(1, deep)
 
-    grad_out = move_blocks(cotangent, clips, groups).reshape(own, width)
+    grad_out = dy.reshape(own, width)
     grad_all = both(grad_out)
     grad_f = grad_out.astype(F32)
 
@@ -607,48 +647,22 @@
     gx = (dx2 + norm_back(dh1 * g1, n1, r1)).astype(BF)
 
     mine = (jnp.arange(2) == c).astype(F32)
-    gbq = gbq.reshape(3, groups, 1, row // 2) * mine[None, None, :, None]
+    gbq = gbq.reshape(bq * groups, 1, row // 2) * mine[None, :, None]
     gbu = gbu.reshape(groups, 1, deep // groups) * mine[None, :, None]
-    sums = jnp.concatenate(
-        [
-            gg1,
-            gb1,
-            jnp.sum(low.astype(F32), axis=0),
-            gg2,
-            gb2,
-            jnp.sum(grad_f, axis=0),
-            gbq.reshape(-1),
-            gbu.reshape(-1),
-        ]
-    ).reshape(lines, width)
-    sums = jnp.pad(sums, ((0, -lines % 8), (0, 0)))
+    vectors = (gg1, gb1, jnp.sum(low.astype(F32), axis=0), gg2, gb2, jnp.sum(grad_f, axis=0), gbq, gbu)
+    sums = jnp.concatenate([v.reshape(groups, -1, row) for v in vectors], axis=1)
+    sums = jnp.pad(sums, ((0, 0), (0, -lines % 8), (0, 0)))
     grads = [g.reshape(groups, 2, 2, 2, g.shape[0] // (8 * groups), g.shape[1]) for g in (gwq, gwo, gw1, gw2)]
-    gwq, gwo, gw1, gw2, sums, gx = reduce(grads, sums, gx.reshape(clips, part, width), groups)
-
-    gwq = gwq.reshape(2, row, 3, groups, row // 2)
-    gwq = jnp.transpose(gwq, (1, 2, 3, 0, 4)).reshape(row, 3 * width).astype(F32)
-    gw1 = gw1.reshape(2, row, groups, deep // groups)
-    gw1 = jnp.transpose(gw1, (1, 2, 0, 3)).reshape(row, hidden).astype(F32)
-    gwo = gwo.reshape(row, width).astype(F32)
-    gw2 = gw2.reshape(hidden // groups, width).astype(F32)
-    cut = lambda v: lax.dynamic_index_in_dim(v.reshape(groups, -1), z, 0, keepdims=False)
-    gg1, gb1, gbo, gg2, gb2, gbd = (cut(sums[n]) for n in range(6))
-    return (
-        output,
-        gx,
-        gg1,
-        gb1,
-        gwq,
-        cut(sums[6 : 6 + bq]),
-        gwo,
-        gbo,
-        gg2,
-        gb2,
-        gw1,
-        cut(sums[6 + bq : lines]),
-        gw2,
-        gbd,
-    )
+    gwq, gwo, gw1, gw2, sums, gx = reduce(
+        grads, blocks, sums, gx.reshape(clips, part, width), groups
+    )
+    gwq, gwo, gw1, gw2 = (
+        g.reshape(shard.shape).astype(F32)
+        for g, shard in zip((gwq, gwo, gw1, gw2), (w_qkv, w_out, w_up, w_down))
+    )
+    gg1, gb1, gbo, gg2, gb2, gbd = (sums[n] for n in range(6))
+    gbq, gbu = sums[6 : 6 + bq].reshape(-1), sums[6 + bq : lines].reshape(-1)
+    return (output, gx, gg1, gb1, gwq, gbq, gwo, gbo, gg2, gb2, gw1, gbu, gw2, gbd)
 
 
 def paired_specs():

time: 609 us -> 528 us (0.87)
  local copies, waits for them, and re-layouts: 87.3 us -> 14.1 us
  waiting for transfers between devices: 35.3 us -> 15.8 us
  Pallas kernels: 330 us -> 342 us
  other arithmetic: 27 us -> 37.7 us
  starting transfers between devices: 41.2 us -> 30.7 us
    convert_element_type x6 -> x0, local copies, waits for them, and re-layouts: 31.4 us -> none  [the longest x3 18.5 us: paired(): gw1 = jnp.transpose(gw1, (1, 2, 0, 3)).reshape(row, hidden).astype(F32)]
    ppermute x4 -> x2, waiting for transfers between devices: 30.9 us -> 10.5 us  [move_blocks(): got.append(lax.ppermute(block, ('core', 'grp'), pairs))]
    dynamic_slice x6 -> x2, local copies, waits for them, and re-layouts: 14.3 us -> 0.04 us  [pick(): return lax.dynamic_index_in_dim(value, c, axis, keepdims=False)]
    pallas_call x2, Pallas kernels: 277 us -> 289 us  [the longest x1 168 us: reduce(): pl.pallas_call(functools.partial(reduce_body, groups, clips, blocks), out...]
    convert_element_type x2 -> x11, other arithmetic: 6.35 us -> 14.7 us  [the longest x4 9.96 us: paired(): g.reshape(shard.shape).astype(F32)]
    reshape x5 -> x1, local copies, waits for them, and re-layouts: 7.56 us -> 0.6 us  [paired(): gbq, gbu = (sums[6:6 + bq].reshape(-1), sums[6 + bq:lines].reshape(-1))]
    unnamed x90 -> x55, local copies, waits for them, and re-layouts: 13 us -> 6.39 us
    ppermute x4 -> x2, starting transfers between devices: 13.2 us -> 8.04 us  [move_blocks(): got.append(lax.ppermute(block, ('core', 'grp'), pairs))]
  transfers between devices with their start and end apart: 13 -> 11, of which waited for: 5 -> 5; matrix products, arithmetic and copies ran while one was open for 8% -> 9% of each run, Pallas kernels for 0% -> 0%
where the time goes in v2:
time: 528 us; the launch traced here: 518 us
  Pallas kernels  342 us (65%)
  matrix products  76.7 us (15%)
  other arithmetic  37.7 us (7%)
  starting transfers between devices  30.7 us (6%)
  waiting for transfers between devices  15.8 us (3%)
  local copies, waits for them, and re-layouts  14.1 us (3%)
    pallas_call x1, Pallas kernels, reduce(): pl.pallas_call(functools.partial(reduce_body, groups, clips, blocks), out...  168 us
    pallas_call x1, Pallas kernels, gather(): pl.pallas_call(functools.partial(gather_body, groups, clips, blocks), out...  121 us
    dot_general x12, matrix products, contract(): lax.dot_general(left, right, (((a,), (b,)), ((), ())), preferred_element_...  76.7 us
    pallas_call x1, Pallas kernels, attention_back(): pl.pallas_call(functools.partial(attention_back_body, step), out_shape=[s...  28.1 us
    pallas_call x1, Pallas kernels, attention(): pl.pallas_call(functools.partial(attention_body, step), out_shape=[shape]...  24.8 us
    ppermute x9, starting transfers between devices, swap(): return lax.ppermute(value, 'core', [(0, 1), (1, 0)])  22.7 us
  transfers between devices with their start and end apart: 11, of which 5 were waited for; matrix products, arithmetic and copies ran while one was open for 9% of the time, Pallas kernels for 0%

profile of v2, /device:TPU:9, one launch (start us, length us, event | category | flops | bytes accessed | tf_op | source)
XLA Modules:
  0.0 518.0 jit_solution(16265217385664958778)
XLA Ops:
  7.5 121.1 %gather.1 = (bf16[4,4,2,32,1536]{4,3,2,1,0:T(8,128)(2,1)}, bf16[4,4,2,16,1024]{4,3,2,1,0:T(8,128)(2,1)}, bf16[4,4,2,32,2048]{4,3,2,1,0:T(8,128)(2,1)}, bf16[4,4,...) custom-call(bf16[4,2,32,3072]{3,2,1,0:T(8,128)(2,1)} %bitcast.129, ...), custom_call_target="tpu_custom_call" | custom-call | tf_op jit(solution)/shard_map/gather/pallas_call | solution.py:202
  133.3 20.9 %collective-permute-start = (bf16[512,1024]{1,0:T(8,128)(2,1)S(1)}, bf16[512,1024]{1,0:T(8,128)(2,1)}, u32[]{:S(2)}, u32[]{:S(2)}) collective-permute-start(bf16[512,1024]{1,0:T(8,128)(2,1)S(1)} %fusion.18), channel_id=1, source_target_pairs={{0,4},{4,0},{1,5},{5,1},{2,6},{6,2},{3,7},{7,3},{8,12},{12,8},{9,1... | collective-permute-start | bytes 3145736 | tf_op jit(solution)/shard_map/ppermute | solution.py:510
  158.0 9.1 %convolution_add_fusion.q_ref.k_ref.v_ref = f32[1536,1024]{1,0:T(8,128)} fusion(bf16[1024,1536]{1,0:T(8,128)(2,1)} %bitcast.177, f32[1536]{0:T(1024)S(1)} %add.163, bf16[512,1024]{1,0:T(8,128)(2,1)} %collective-permute-done, bf16[512,1024]{1,0:T(8,128)(2,1)S(1)} %fusion.18), kind=kOutput, calls=%fused_computation.11 | convolution fusion | flops 3226992640 | bytes 11540480 | tf_op jit(solution)/shard_map/dot_general | solution.py:518
  167.1 24.8 %attention.1 = (bf16[512,1024]{1,0:T(8,128)(2,1)}, bf16[512,1024]{1,0:T(8,128)(2,1)}, bf16[512,1024]{1,0:T(8,128)(2,1)}, bf16[512,1024]{1,0:T(8,128)(2,1)}, f32[8,1,1024]{2,1,0:T(1,128)}) custom-call(f32[1536,1024]{1,0:T(8,128)} %convolution_add_fusion.q_ref.k_ref.v_ref, f32[1536,1024]{1,0:T(8,128)} %convolution_add_fusion.q_ref.k_ref.v_ref, ...), custom_call_target="tpu_custom_call" | custom-call | flops 2147483648 | bytes 12582912 | tf_op jit(solution)/shard_map/attention/pallas_call | solution.py:442
  202.6 9.6 %multiply_convert_fusion.1 = (bf16[1024,2048]{1,0:T(8,128)(2,1)}, f32[1024,2048]{1,0:T(8,128)S(1)}) fusion(f32[2048]{0:T(1024)S(1)} %bitcast.164, bf16[1024,2048]{1,0:T(8,128)(2,1)} %bitcast.175, bf16[512,1024]{1,0:T(8,128)(2,1)} %collective-permute-done.3, bf16[512,1024]{1,0:T(8,128)(2,1)} %add_convert_fusion), kind=kOutput, calls=%fused_computation.8 | convolution fusion | flops 4311744512 | bytes 18882560 | tf_op jit(solution)/shard_map/dot_general | solution.py:518
  212.2 10.3 %convert_reduce_fusion = (f32[2048]{0:T(1024)S(1)}, bf16[1024,2048]{1,0:T(8,128)(2,1)}) fusion(f32[1024,2048]{1,0:T(8,128)S(1)} %get-tuple-element.103, f32[2048]{0:T(1024)S(1)} %bitcast.165, bf16[2048,1024]{1,0:T(8,128)(2,1)S(1)} %bitcast.173, bf16[512,1024]{1,0:T(8,128)(2,1)} %collective-permute-done.7, bf16[512,1024]{1,0:T(8,128)(2,1)} %bitcast.28), kind=kOutput, calls=%fused_computation.6 | convolution fusion | flops 4330616832 | bytes 18890752 | tf_op jit(solution)/shard_map/dot_general | solution.py:518
  222.5 7.0 %fusion.50 = f32[1024,1024]{1,0:T(8,128)S(1)} fusion(bf16[1024,2048]{1,0:T(8,128)(2,1)} %get-tuple-element.105, bf16[1024,2048]{1,0:T(8,128)(2,1)S(1)} %bitcast.176), kind=kOutput, calls=%fused_computation.146 | convolution fusion | flops 4294967296 | bytes 12582912 | tf_op jit(solution)/shard_map/dot_general | solution.py:518
  230.1 4.5 fusion.49
  234.9 7.7 %convolution_convert_fusion.2 = bf16[1024,2048]{1,0:T(8,128)(2,1)} fusion(bf16[1024,2048]{1,0:T(8,128)(2,1)S(1)} %copy-done.23, bf16[512,1024]{1,0:T(8,128)(2,1)} %collective-permute-done.3, bf16[512,1024]{1,0:T(8,128)(2,1)} %add_convert_fusion), kind=kOutput, calls=%fused_computation.14 | convolution fusion | flops 4301258752 | bytes 10485760 | tf_op jit(solution)/shard_map/dot_general | solution.py:518
  243.8 3.7 convert_reduce_fusion.4
  247.6 8.0 %collective-permute-start.5 = (bf16[256,1024]{1,0:T(8,128)(2,1)S(1)}, bf16[256,1024]{1,0:T(8,128)(2,1)S(1)}, u32[]{:S(2)}, u32[]{:S(2)}) collective-permute-start(bf16[256,1024]{1,0:T(8,128)(2,1)S(1)} %get-tuple-element.75), channel_id=1, source_target_pairs={{0,0},{1,1},{2,4},{3,5},{4,2},{5,3},{6,6},{7,7},{8,8},{9,9},{10,12... | collective-permute-start | bytes 1572872 | tf_op jit(solution)/shard_map/ppermute | solution.py:536
  255.7 8.2 %convolution_convert_fusion.1 = bf16[2048,1024]{1,0:T(8,128)(2,1)} fusion(bf16[1024,2048]{1,0:T(8,128)(2,1)S(1)} %copy-done.22, bf16[512,1024]{1,0:T(8,128)(2,1)} %collective-permute-done.7, bf16[512,1024]{1,0:T(8,128)(2,1)} %bitcast.28), kind=kOutput, calls=%fused_computation.13 | convolution fusion | flops 4301258752 | bytes 10485760 | tf_op jit(solution)/shard_map/dot_general | solution.py:518
  264.0 3.3 collective-permute-done.5
  267.3 7.2 %collective-permute-done.6 = bf16[256,1024]{1,0:T(8,128)(2,1)S(1)} collective-permute-done((bf16[256,1024]{1,0:T(8,128)(2,1)S(1)}, bf16[256,1024]{1,0:T(8,128)(2,1)S(1)}, u32[]{:S(2)}, u32[]{:S(2)}) %collective-permute-start.6) | collective-permute-done | bytes 524320 | tf_op jit(solution)/shard_map/ppermute | solution.py:536
  276.0 3.8 convolution_convert_fusion.4.g_ref
  279.8 28.1 %attention_back.1 = (bf16[512,1024]{1,0:T(8,128)(2,1)}, bf16[512,1024]{1,0:T(8,128)(2,1)}, bf16[512,1024]{1,0:T(8,128)(2,1)}) custom-call(bf16[512,1024]{1,0:T(8,128)(2,1)} %get-tuple-element.44.q_ref, bf16[512,1024]{1,0:T(8,128)(2,1)} %get-tuple-element.45.k_ref, bf16[512,1024]{1,0:T(8,128)(2,1)} %get-tuple-element.46.v_ref, ...), custom_call_target="tpu_custom_call" | custom-call | flops 5368709120 | bytes 9437184 | tf_op jit(solution)/shard_map/attention_back/pallas_call | solution.py:493
  311.4 3.5 fusion.51
  317.2 3.9 convolution_convert_fusion.3
  321.1 6.5 %convolution_convert_fusion = bf16[1024,1536]{1,0:T(8,128)(2,1)} fusion(bf16[1536,1024]{1,0:T(8,128)(2,1)S(1)} %copy-done.5, bf16[512,1024]{1,0:T(8,128)(2,1)} %collective-permute-done, bf16[512,1024]{1,0:T(8,128)(2,1)S(1)} %copy-done.10), kind=kOutput, calls=%fused_computation.12 | convolution fusion | flops 3226992640 | bytes 8388608 | tf_op jit(solution)/shard_map/dot_general | solution.py:518
  331.2 3.7 fusion.24
  335.0 167.7 %reduce.8 = (bf16[4,2,32,3072]{3,2,1,0:T(8,128)(2,1)}, bf16[2,4,2,16,1024]{4,3,2,1,0:T(8,128)(2,1)}, bf16[4,2,32,4096]{3,2,1,0:T(8,128)(2,1)}, bf16[2,4,2,64,102...) custom-call(bf16[4,2,2,2,32,1536]{5,4,3,2,1,0:T(8,128)(2,1)} %bitcast.126, ...), custom_call_target="tpu_custom_call" | custom-call | tf_op jit(solution)/shard_map/reduce/pallas_call | solution.py:389
  505.6 3.6 bitcast_convert_fusion.2
  510.9 2.6 bitcast_convert_fusion.1
  514.1 2.6 bitcast_convert_fusion
  (147 shorter events, 45.2 us)
Async XLA Ops:
  128.6 4.3 copy-start
  129.7 24.6 %copy-start.18 = (f32[2,8,256]{2,1,0:T(8,128)S(1)}, f32[2,8,256]{2,1,0:T(8,128)}, u32[]{:S(2)}) copy-start(f32[2,8,256]{2,1,0:T(8,128)} %get-tuple-element.39) | copy-start | bytes 49156
  129.7 24.7 %copy-start.17 = (f32[4,16,256]{2,1,0:T(8,128)S(1)}, f32[4,16,256]{2,1,0:T(8,128)}, u32[]{:S(2)}) copy-start(f32[4,16,256]{2,1,0:T(8,128)} %get-tuple-element.38) | copy-start | bytes 196612
  133.3 33.7 %copy-start.9 = (bf16[512,1024]{1,0:T(8,128)(2,1)}, bf16[512,1024]{1,0:T(8,128)(2,1)S(1)}, u32[]{:S(2)}) copy-start(bf16[512,1024]{1,0:T(8,128)(2,1)S(1)} %fusion.18) | copy-start | bytes 3145732
  133.3 24.6 %collective-permute-start = (bf16[512,1024]{1,0:T(8,128)(2,1)S(1)}, bf16[512,1024]{1,0:T(8,128)(2,1)}, u32[]{:S(2)}, u32[]{:S(2)}) collective-permute-start(bf16[512,1024]{1,0:T(8,128)(2,1)S(1)} %fusion.18), channel_id=1, source_target_pairs={{0,4},{4,0},{1,5},{5,1},{2,6},{6,2},{3,7},{7,3},{8,12},{12,8},{9,1... | collective-permute-start | bytes 3145736 | tf_op jit(solution)/shard_map/ppermute | solution.py:510
  154.3 2.4 collective-permute-start.1
  167.1 24.9 %copy-start.14 = (bf16[4,4,2,16,1024]{4,3,2,1,0:T(8,128)(2,1)S(1)}, bf16[4,4,2,16,1024]{4,3,2,1,0:T(8,128)(2,1)}, u32[]{:S(2)}) copy-start(bf16[4,4,2,16,1024]{4,3,2,1,0:T(8,128)(2,1)} %get-tuple-element.41) | copy-start | bytes 3145732
  194.6 2.7 collective-permute-start.2
  199.6 3.0 collective-permute-start.3
  200.0 12.2 %collective-permute-start.7 = (bf16[512,1024]{1,0:T(8,128)(2,1)}, bf16[512,1024]{1,0:T(8,128)(2,1)}, u32[]{:S(2)}, u32[]{:S(2)}) collective-permute-start(bf16[512,1024]{1,0:T(8,128)(2,1)} %bitcast.28), channel_id=1, source_target_pairs={{0,4},{4,0},{1,5},{5,1},{2,6},{6,2},{3,7},{7,3},{8,12},{12,8},{9,1... | collective-permute-start | bytes 3145736 | tf_op jit(solution)/shard_map/ppermute | solution.py:510
  202.6 9.6 %copy-start.19 = (bf16[4,4,2,64,1024]{4,3,2,1,0:T(8,128)(2,1)S(1)}, bf16[4,4,2,64,1024]{4,3,2,1,0:T(8,128)(2,1)}, u32[]{:S(2)}) copy-start(bf16[4,4,2,64,1024]{4,3,2,1,0:T(8,128)(2,1)} %get-tuple-element.43) | copy-start | bytes 12582916
  212.2 10.4 %copy-start.20 = (bf16[4,4,2,32,2048]{4,3,2,1,0:T(8,128)(2,1)S(1)}, bf16[4,4,2,32,2048]{4,3,2,1,0:T(8,128)(2,1)}, u32[]{:S(2)}) copy-start(bf16[4,4,2,32,2048]{4,3,2,1,0:T(8,128)(2,1)} %get-tuple-element.42) | copy-start | bytes 12582916
  222.5 7.6 %copy-start.22 = (bf16[1024,2048]{1,0:T(8,128)(2,1)S(1)}, bf16[1024,2048]{1,0:T(8,128)(2,1)}, u32[]{:S(2)}) copy-start(bf16[1024,2048]{1,0:T(8,128)(2,1)} %get-tuple-element.102) | copy-start | bytes 12582916
  229.6 13.0 %collective-permute-start.8 = (bf16[512,1024]{1,0:T(8,128)(2,1)S(1)}, bf16[512,1024]{1,0:T(8,128)(2,1)S(1)}, u32[]{:S(2)}, u32[]{:S(2)}) collective-permute-start(bf16[512,1024]{1,0:T(8,128)(2,1)S(1)} %slice.199), channel_id=1, source_target_pairs={{0,4},{4,0},{1,5},{5,1},{2,6},{6,2},{3,7},{7,3},{8,12},{12,8},{9,1... | collective-permute-start | bytes 3145736 | tf_op jit(solution)/shard_map/ppermute | solution.py:510
  230.1 4.9 copy-start.23
  234.7 9.0 %collective-permute-start.4 = (bf16[512,1024]{1,0:T(8,128)(2,1)S(1)}, bf16[512,1024]{1,0:T(8,128)(2,1)S(1)}, u32[]{:S(2)}, u32[]{:S(2)}) collective-permute-start(bf16[512,1024]{1,0:T(8,128)(2,1)S(1)} %slice.200), channel_id=1, source_target_pairs={{0,4},{4,0},{1,5},{5,1},{2,6},{6,2},{3,7},{7,3},{8,12},{12,8},{9,1... | collective-permute-start | bytes 3145736 | tf_op jit(solution)/shard_map/ppermute | solution.py:510
  247.6 19.7 %collective-permute-start.5 = (bf16[256,1024]{1,0:T(8,128)(2,1)S(1)}, bf16[256,1024]{1,0:T(8,128)(2,1)S(1)}, u32[]{:S(2)}, u32[]{:S(2)}) collective-permute-start(bf16[256,1024]{1,0:T(8,128)(2,1)S(1)} %get-tuple-element.75), channel_id=1, source_target_pairs={{0,0},{1,1},{2,4},{3,5},{4,2},{5,3},{6,6},{7,7},{8,8},{9,9},{10,12... | collective-permute-start | bytes 1572872 | tf_op jit(solution)/shard_map/ppermute | solution.py:536
  255.5 19.0 %collective-permute-start.6 = (bf16[256,1024]{1,0:T(8,128)(2,1)S(1)}, bf16[256,1024]{1,0:T(8,128)(2,1)S(1)}, u32[]{:S(2)}, u32[]{:S(2)}) collective-permute-start(bf16[256,1024]{1,0:T(8,128)(2,1)S(1)} %get-tuple-element.74), channel_id=1, source_target_pairs={{0,1},{1,0},{2,5},{3,4},{4,3},{5,2},{6,7},{7,6},{8,9},{9,8},{10,13... | collective-permute-start | bytes 1572872 | tf_op jit(solution)/shard_map/ppermute | solution.py:536
  255.6 20.4 %collective-permute-start.9 = (bf16[512,1024]{1,0:T(8,128)(2,1)}, bf16[512,1024]{1,0:T(8,128)(2,1)}, u32[]{:S(2)}, u32[]{:S(2)}) collective-permute-start(bf16[512,1024]{1,0:T(8,128)(2,1)} %get-tuple-element.67), channel_id=1, source_target_pairs={{0,4},{4,0},{1,5},{5,1},{2,6},{6,2},{3,7},{7,3},{8,12},{12,8},{9,1... | collective-permute-start | bytes 3145736 | tf_op jit(solution)/shard_map/ppermute | solution.py:510
  317.1 10.6 %collective-permute-start.10 = (bf16[512,1024]{1,0:T(8,128)(2,1)}, bf16[512,1024]{1,0:T(8,128)(2,1)}, u32[]{:S(2)}, u32[]{:S(2)}) collective-permute-start(bf16[512,1024]{1,0:T(8,128)(2,1)} %slice.198), channel_id=1, source_target_pairs={{0,4},{4,0},{1,5},{5,1},{2,6},{6,2},{3,7},{7,3},{8,12},{12,8},{9,1... | collective-permute-start | bytes 3145736 | tf_op jit(solution)/shard_map/ppermute | solution.py:510
  317.2 4.0 copy-start.5
  321.1 6.6 %copy-start.3 = (f32[1024,1024]{1,0:T(8,128)S(1)}, f32[1024,1024]{1,0:T(8,128)}, u32[]{:S(2)}) copy-start(f32[1024,1024]{1,0:T(8,128)} %copy-done.2) | copy-start | bytes 12582916
  505.6 4.2 copy-start.16
  505.6 5.3 %copy-start.7 = (bf16[4,2,32,4096]{3,2,1,0:T(8,128)(2,1)S(1)}, bf16[4,2,32,4096]{3,2,1,0:T(8,128)(2,1)}, u32[]{:S(2)}) copy-start(bf16[4,2,32,4096]{3,2,1,0:T(8,128)(2,1)} %get-tuple-element.56) | copy-start | bytes 6291460
  (11 other events, 28.2 us)

commit v3 on v2

--- a/solution.py
+++ b/solution.py
@@ -124,62 +124,109 @@
         s.start()
     keep = [pltpu.make_async_copy(small, small_o.at[z], ls.at[count])]
     keep[0].start()
-    first = {}
-    for w in range(count):
+    start_dy, finish_dy = move_tokens((dy,), (dy_o,), us, ur, p, c, z, clips)
+    units = [(w, d, side) for w in range(count) for d in range(1, groups) for side in range(2)]
+
+    def origin(d, side):
+        return z - d if side == 0 else z + d
+
+    def arrives(d, side):
+        return z >= d if side == 0 else z + d < groups
+
+    def leaves(d, side):
+        if side == 0:
+            return jnp.logical_and(z + 1 < groups, z + 1 >= d)
+        return jnp.logical_and(z >= 1, z - 1 + d < groups)
+
+    def hop(w, d, side, src):
+        o = origin(d - 1, side)
+        target = (p, c, lax.rem(z + 1 if side == 0 else z + groups - 1, groups))
+        return remote(src, outs[w].at[o, p], zs.at[w, side, d], zr.at[w, side, d], target)
+
+    def own(w):
         pltpu.make_async_copy(halves[w], halves[w], hs.at[w]).wait()
         keep.append(pltpu.make_async_copy(halves[w], outs[w].at[z], ls.at[w]))
         keep[-1].start()
-        for k in range(1, groups):
-            first[w, k] = remote(
-                halves[w].at[p], outs[w].at[z, p], zs.at[w, k], zr.at[w, k], col[k]
-            )
-            first[w, k].start()
-    start_dy, finish_dy = move_tokens((dy,), (dy_o,), us, ur, p, c, z, clips)
-    start_dy()
-    units = [(w, k) for w in range(count) for k in range(1, groups)]
-    xc, yc, fa, fb = {}, {}, {}, {}
+        for side in range(2):
+
+            @pl.when(leaves(1, side))
+            def _():
+                hop(w, 1, side, halves[w].at[p]).start()
+
+    def links(u):
+        w, d, side = u
+        o = outs[w].at[lax.rem(origin(d, side) + groups, groups)]
+        e, f = xs.at[w, side, d], xr.at[w, side, d]
+        g, h = ys.at[w, side, d], yr.at[w, side, d]
+        a, b = fs.at[w, side, d, 0], fr.at[w, side, d, 0]
+        m, n = fs.at[w, side, d, 1], fr.at[w, side, d, 1]
+        across = lambda q: remote(o.at[q], o.at[q], e, f, xn)
+        along = lambda q: remote(o.at[q], o.at[q], g, h, yn)
+        first = lambda q: remote(o.at[q, 0], o.at[q, 0], a, b, yn)
+        second = lambda q: remote(o.at[q, 1], o.at[q, 1], m, n, xn)
+        return o, across, along, first, second
 
     def plane(u):
-        w, k = u
-        o = outs[w].at[org[k]]
-        remote(halves[w].at[p], o.at[p], zs.at[w, k], zr.at[w, k], col[k]).wait_recv()
-        xc[u] = remote(o.at[p], o.at[p], xs.at[w, k], xr.at[w, k], xn)
-        yc[u] = remote(o.at[p], o.at[p], ys.at[w, k], yr.at[w, k], yn)
-        xc[u].start()
-        yc[u].start()
+        w, d, side = u
+        o, across, along, first, second = links(u)
+
+        @pl.when(arrives(d, side))
+        def _():
+            remote(o.at[p], o.at[p], zs.at[w, side, d], zr.at[w, side, d], xn).wait_recv()
+            if d + 1 < groups:
+
+                @pl.when(leaves(d + 1, side))
+                def _():
+                    hop(w, d + 1, side, o.at[p]).start()
+
+            across(p).start()
+            along(p).start()
 
     def forward(u):
-        w, k = u
-        o = outs[w].at[org[k]]
-        q = p ^ 1
-        remote(o.at[q], o.at[q], xs.at[w, k], xr.at[w, k], xn).wait_recv()
-        fa[u] = remote(o.at[q, 0], o.at[q, 0], fs.at[w, k, 0], fr.at[w, k, 0], yn)
-        fa[u].start()
-        q = p ^ 2
-        remote(o.at[q], o.at[q], ys.at[w, k], yr.at[w, k], yn).wait_recv()
-        fb[u] = remote(o.at[q, 1], o.at[q, 1], fs.at[w, k, 1], fr.at[w, k, 1], xn)
-        fb[u].start()
-
-    lag = 2
+        w, d, side = u
+        o, across, along, first, second = links(u)
+
+        @pl.when(arrives(d, side))
+        def _():
+            across(p ^ 1).wait_recv()
+            first(p ^ 1).start()
+            along(p ^ 2).wait_recv()
+            second(p ^ 2).start()
+
+    def settle(u):
+        w, d, side = u
+        o, across, along, first, second = links(u)
+
+        @pl.when(arrives(d, side))
+        def _():
+            first(p ^ 3).wait_recv()
+            second(p ^ 3).wait_recv()
+            across(p).wait_send()
+            along(p).wait_send()
+            first(p).wait_send()
+            second(p).wait_send()
+
+        @pl.when(leaves(d, side))
+        def _():
+            hop(w, d, side, halves[w].at[p]).wait_send()
+
+    own(0)
+    own(1)
+    lag = 3
     for n in range(len(units) + lag):
         if n < len(units):
             plane(units[n])
+            w, d, side = units[n]
+            if (d, side) == (1, 1) and w + 2 < count:
+                own(w + 2)
+            if n + 1 == len(units):
+                start_dy()
         if n >= lag:
             forward(units[n - lag])
     for u in units:
-        w, k = u
-        q = p ^ 3
-        o = outs[w].at[org[k]]
-        remote(o.at[q, 0], o.at[q, 0], fs.at[w, k, 0], fr.at[w, k, 0], yn).wait_recv()
-        remote(o.at[q, 1], o.at[q, 1], fs.at[w, k, 1], fr.at[w, k, 1], xn).wait_recv()
+        settle(u)
     for k in range(1, groups):
         remote(small, small_o.at[org[k]], ss.at[k], sr.at[k], col[k]).wait_recv()
-    for u in units:
-        first[u].wait_send()
-        xc[u].wait_send()
-        yc[u].wait_send()
-        fa[u].wait_send()
-        fb[u].wait_send()
     for s in smalls:
         s.wait_send()
     for k in keep:
@@ -205,8 +252,8 @@
         in_specs=[ANY] * count + [VM, ANY, ANY, ANY],
         out_specs=[ANY] * len(shapes),
         scratch_shapes=[pltpu.VMEM(h, BF) for h in halves]
-        + [dma((count, groups))] * 6
-        + [dma((count, groups, 2))] * 2
+        + [dma((count, 2, groups))] * 6
+        + [dma((count, 2, groups, 2))] * 2
         + [dma((count,)), dma((count + 1,)), dma((groups,)), dma((groups,))]
         + [dma((2, clips))] * 2
         + [dma((1, clips))] * 2,
@@ -245,53 +292,48 @@
     ]
     for t in tails:
         t.start()
-    units = [(w, k) for w in range(count) for k in range(groups)]
-    load, c1, c2, c3, c4, c5 = {}, {}, {}, {}, {}, {}
-    for u in units:
-        w, k = u
-        g = grads[w].at[k]
-        c1[u, 0] = remote(g.at[:, 1 - lo, 0], one_a[w].at[k], s1.at[w, k, 0], r1.at[w, k, 0], xn)
-        c1[u, 1] = remote(g.at[1 - hi, :, 1], one_b[w].at[k], s1.at[w, k, 1], r1.at[w, k, 1], yn)
-        load[u, 0] = pltpu.make_async_copy(g.at[:, lo, 0], own_a[w].at[k], os.at[w, k, 0])
-        load[u, 1] = pltpu.make_async_copy(g.at[hi, :, 1], own_b[w].at[k], os.at[w, k, 1])
-        c1[u, 0].start()
-        c1[u, 1].start()
-        load[u, 0].start()
-        load[u, 1].start()
+    order = sorted(range(count), key=lambda w: -mine[w].shape[3] * mine[w].shape[2])
+    units = [(w, j) for w in order for j in [*range(1, groups), 0]]
+    load, c1, c2, c4, c5 = {}, {}, {}, {}, {}
+
+    def stage_zero(u):
+        w, j = u
+        g = grads[w].at[lax.rem(z + j, groups)]
+        c1[u, 0] = remote(g.at[:, 1 - lo, 0], one_a[w].at[j], s1.at[w, j, 0], r1.at[w, j, 0], xn)
+        c1[u, 1] = remote(g.at[1 - hi, :, 1], one_b[w].at[j], s1.at[w, j, 1], r1.at[w, j, 1], yn)
+        load[u, 0] = pltpu.make_async_copy(g.at[:, lo, 0], own_a[w].at[j], os.at[w, j, 0])
+        load[u, 1] = pltpu.make_async_copy(g.at[hi, :, 1], own_b[w].at[j], os.at[w, j, 1])
+        for copy in (c1[u, 0], c1[u, 1], load[u, 0], load[u, 1]):
+            copy.start()
 
     def stage_one(u):
-        w, k = u
+        w, j = u
         for n, (own, one, two, side, target) in enumerate(
             ((own_a, one_a, two_a, hi, yn), (own_b, one_b, two_b, lo, xn))
         ):
             load[u, n].wait()
             c1[u, n].wait_recv()
-            o = own[w].at[k]
-            o[...] = (o[...].astype(F32) + one[w][k].astype(F32)).astype(BF)
-            c2[u, n] = remote(o.at[1 - side], two[w].at[k], s2.at[w, k, n], r2.at[w, k, n], target)
+            o = own[w].at[j]
+            o[...] = (o[...].astype(F32) + one[w][j].astype(F32)).astype(BF)
+            c2[u, n] = remote(o.at[1 - side], two[w].at[j], s2.at[w, j, n], r2.at[w, j, n], target)
             c2[u, n].start()
 
+    def third(w, j):
+        return remote(mine[w].at[j], three[w].at[j], s3.at[w, j], r3.at[w, j], col[j])
+
     def stage_two(u):
-        w, k = u
+        w, j = u
         for n, (own, two, side) in enumerate(((own_a, two_a, hi), (own_b, two_b, lo))):
             c2[u, n].wait_recv()
-            mine[w][k, n] = (own[w][k, side].astype(F32) + two[w][k].astype(F32)).astype(BF)
-
-        @pl.when(z != k)
-        def _():
-            remote(
-                mine[w].at[k],
-                three[w].at[lax.rem(k - z + groups, groups)],
-                s3.at[w, k],
-                r3.at[w, lax.rem(k - z + groups, groups)],
-                (p, c, k),
-            ).start()
+            mine[w][j, n] = (own[w][j, side].astype(F32) + two[w][j].astype(F32)).astype(BF)
+        if j:
+            third(w, j).start()
 
     def stage_three(w):
-        total = mine[w][z].astype(F32)
-        for k in range(1, groups):
-            remote(mine[w].at[0], three[w].at[k], s3.at[w, 0], r3.at[w, k], col[k]).wait_recv()
-            total = total + three[w][k].astype(F32)
+        total = mine[w][0].astype(F32)
+        for j in range(1, groups):
+            third(w, j).wait_recv()
+            total = total + three[w][j].astype(F32)
         full[w][p] = total.astype(BF)
         for n, target in enumerate((xn, yn)):
             f = full[w].at[p]
@@ -314,36 +356,31 @@
             pltpu.make_async_copy(src, dst, ls.at[w]).start()
             remote(src, dst, cs.at[w], cr.at[w], cn).start()
 
-    lag = 3
-    for n in range(len(units) + lag):
-        if n < len(units):
-            stage_one(units[n])
-        if n >= lag:
-            stage_two(units[n - lag])
-    for w in range(count):
-        stage_three(w)
-        if w >= 1:
-            stage_four(w - 1)
-        if w >= 2:
-            stage_five(w - 2)
-    stage_four(count - 1)
-    for w in range(max(count - 2, 0), count):
-        stage_five(w)
+    ahead, lag = 2, 2
+    todo = {}
+    for n, u in enumerate(units):
+        todo.setdefault(max(n - ahead, -1), []).append((stage_zero, u))
+        todo.setdefault(n, []).append((stage_one, u))
+        todo.setdefault(n + lag, []).append((stage_two, u))
+    for i, w in enumerate(order):
+        last = (i + 1) * groups - 1 + lag
+        for at, stage in ((2, stage_three), (3, stage_four), (4, stage_five)):
+            todo.setdefault(last + at, []).append((stage, w))
+    for n in sorted(todo):
+        for stage, what in todo[n]:
+            stage(what)
     for k in range(1, groups):
         tails[k - 1].wait()
     small_o[...] = small_s[z]
     for k in range(1, groups):
         small_o[...] += small_z[k]
     for u in units:
-        w, k = u
+        w, j = u
         for n in range(2):
             c1[u, n].wait_send()
             c2[u, n].wait_send()
-
-        @pl.when(z != k)
-        def _():
-            remote(mine[w].at[k], three[w].at[0], s3.at[w, k], r3.at[w, 0], xn).wait_send()
-
+        if j:
+            third(w, j).wait_send()
     for w in range(count):
         for n in range(2):
             c4[w, n].wait_send()

time: 528 us -> 491 us (0.930)
  starting transfers between devices: 30.7 us -> 7.33 us
  Pallas kernels: 342 us -> 328 us
    ppermute x9, starting transfers between devices: 22.7 us -> 1.98 us  [swap(): return lax.ppermute(value, 'core', [(0, 1), (1, 0)])]
    pallas_call x1, Pallas kernels: 168 us -> 150 us  [reduce(): pl.pallas_call(functools.partial(reduce_body, groups, clips, blocks), out...]
  transfers between devices with their start and end apart: 11 -> 11, of which waited for: 5 -> 5; matrix products, arithmetic and copies ran while one was open for 9% -> 10% of each run, Pallas kernels for 0% -> 0%
where the time goes in v3:
time: 491 us; the launch traced here: 482 us
  Pallas kernels  328 us (67%)
  matrix products  76.7 us (16%)
  other arithmetic  37.7 us (8%)
  waiting for transfers between devices  16.3 us (3%)
  local copies, waits for them, and re-layouts  14.1 us (3%)
  starting transfers between devices  7.33 us (1%)
    pallas_call x1, Pallas kernels, reduce(): pl.pallas_call(functools.partial(reduce_body, groups, clips, blocks), out...  150 us
    pallas_call x1, Pallas kernels, gather(): pl.pallas_call(functools.partial(gather_body, groups, clips, blocks), out...  125 us
    dot_general x12, matrix products, contract(): lax.dot_general(left, right, (((a,), (b,)), ((), ())), preferred_element_...  76.7 us
    pallas_call x1, Pallas kernels, attention_back(): pl.pallas_call(functools.partial(attention_back_body, step), out_shape=[s...  28.1 us
    pallas_call x1, Pallas kernels, attention(): pl.pallas_call(functools.partial(attention_body, step), out_shape=[shape]...  24.9 us
    ppermute x2, waiting for transfers between devices, move_blocks(): got.append(lax.ppermute(block, ('core', 'grp'), pairs))  10.8 us
    convert_element_type x4, other arithmetic, paired(): g.reshape(shard.shape).astype(F32)  9.96 us
  transfers between devices with their start and end apart: 11, of which 5 were waited for; matrix products, arithmetic and copies ran while one was open for 10% of the time, Pallas kernels for 0%

profile of v3, /device:TPU:9, one launch (start us, length us, event | category | flops | bytes accessed | tf_op | source)
XLA Modules:
  0.0 481.9 jit_solution(10603143223052396666)
XLA Ops:
  7.5 125.2 %gather.1 = (bf16[4,4,2,32,1536]{4,3,2,1,0:T(8,128)(2,1)}, bf16[4,4,2,16,1024]{4,3,2,1,0:T(8,128)(2,1)}, bf16[4,4,2,32,2048]{4,3,2,1,0:T(8,128)(2,1)}, bf16[4,4,...) custom-call(bf16[4,2,32,3072]{3,2,1,0:T(8,128)(2,1)} %bitcast.129, ...), custom_call_target="tpu_custom_call" | custom-call | tf_op jit(solution)/shard_map/gather/pallas_call | solution.py:249
  141.6 9.1 %convolution_add_fusion.q_ref.k_ref.v_ref = f32[1536,1024]{1,0:T(8,128)} fusion(bf16[1024,1536]{1,0:T(8,128)(2,1)} %bitcast.177, f32[1536]{0:T(1024)S(1)} %add.163, bf16[512,1024]{1,0:T(8,128)(2,1)} %collective-permute-done, bf16[512,1024]{1,0:T(8,128)(2,1)S(1)} %fusion.18), kind=kOutput, calls=%fused_computation.11 | convolution fusion | flops 3226992640 | bytes 11540480 | tf_op jit(solution)/shard_map/dot_general | solution.py:555
  150.7 24.9 %attention.1 = (bf16[512,1024]{1,0:T(8,128)(2,1)}, bf16[512,1024]{1,0:T(8,128)(2,1)}, bf16[512,1024]{1,0:T(8,128)(2,1)}, bf16[512,1024]{1,0:T(8,128)(2,1)}, f32[8,1,1024]{2,1,0:T(1,128)}) custom-call(f32[1536,1024]{1,0:T(8,128)} %convolution_add_fusion.q_ref.k_ref.v_ref, f32[1536,1024]{1,0:T(8,128)} %convolution_add_fusion.q_ref.k_ref.v_ref, ...), custom_call_target="tpu_custom_call" | custom-call | flops 2147483648 | bytes 12582912 | tf_op jit(solution)/shard_map/attention/pallas_call | solution.py:479
  178.5 2.5 collective-permute-done.2
  186.2 9.5 %multiply_convert_fusion.1 = (bf16[1024,2048]{1,0:T(8,128)(2,1)}, f32[1024,2048]{1,0:T(8,128)S(1)}) fusion(f32[2048]{0:T(1024)S(1)} %bitcast.164, bf16[1024,2048]{1,0:T(8,128)(2,1)} %bitcast.175, bf16[512,1024]{1,0:T(8,128)(2,1)} %collective-permute-done.3, bf16[512,1024]{1,0:T(8,128)(2,1)} %add_convert_fusion), kind=kOutput, calls=%fused_computation.8 | convolution fusion | flops 4311744512 | bytes 18882560 | tf_op jit(solution)/shard_map/dot_general | solution.py:555
  195.8 10.4 %convert_reduce_fusion = (f32[2048]{0:T(1024)S(1)}, bf16[1024,2048]{1,0:T(8,128)(2,1)}) fusion(f32[1024,2048]{1,0:T(8,128)S(1)} %get-tuple-element.103, f32[2048]{0:T(1024)S(1)} %bitcast.165, bf16[2048,1024]{1,0:T(8,128)(2,1)S(1)} %bitcast.173, bf16[512,1024]{1,0:T(8,128)(2,1)} %collective-permute-done.7, bf16[512,1024]{1,0:T(8,128)(2,1)} %bitcast.28), kind=kOutput, calls=%fused_computation.6 | convolution fusion | flops 4330616832 | bytes 18890752 | tf_op jit(solution)/shard_map/dot_general | solution.py:555
  206.2 7.2 %fusion.50 = f32[1024,1024]{1,0:T(8,128)S(1)} fusion(bf16[1024,2048]{1,0:T(8,128)(2,1)} %get-tuple-element.105, bf16[1024,2048]{1,0:T(8,128)(2,1)S(1)} %bitcast.176), kind=kOutput, calls=%fused_computation.146 | convolution fusion | flops 4294967296 | bytes 12582912 | tf_op jit(solution)/shard_map/dot_general | solution.py:555
  213.8 4.5 fusion.49
  218.9 7.7 %convolution_convert_fusion.2 = bf16[1024,2048]{1,0:T(8,128)(2,1)} fusion(bf16[1024,2048]{1,0:T(8,128)(2,1)S(1)} %copy-done.23, bf16[512,1024]{1,0:T(8,128)(2,1)} %collective-permute-done.3, bf16[512,1024]{1,0:T(8,128)(2,1)} %add_convert_fusion), kind=kOutput, calls=%fused_computation.14 | convolution fusion | flops 4301258752 | bytes 10485760 | tf_op jit(solution)/shard_map/dot_general | solution.py:555
  227.7 3.7 convert_reduce_fusion.4
  231.5 5.3 %collective-permute-start.5 = (bf16[256,1024]{1,0:T(8,128)(2,1)S(1)}, bf16[256,1024]{1,0:T(8,128)(2,1)S(1)}, u32[]{:S(2)}, u32[]{:S(2)}) collective-permute-start(bf16[256,1024]{1,0:T(8,128)(2,1)S(1)} %get-tuple-element.75), channel_id=1, source_target_pairs={{0,0},{1,1},{2,4},{3,5},{4,2},{5,3},{6,6},{7,7},{8,8},{9,9},{10,12... | collective-permute-start | bytes 1572872 | tf_op jit(solution)/shard_map/ppermute | solution.py:573
  236.9 7.9 %convolution_convert_fusion.1 = bf16[2048,1024]{1,0:T(8,128)(2,1)} fusion(bf16[1024,2048]{1,0:T(8,128)(2,1)S(1)} %copy-done.22, bf16[512,1024]{1,0:T(8,128)(2,1)} %collective-permute-done.7, bf16[512,1024]{1,0:T(8,128)(2,1)} %bitcast.28), kind=kOutput, calls=%fused_computation.13 | convolution fusion | flops 4301258752 | bytes 10485760 | tf_op jit(solution)/shard_map/dot_general | solution.py:555
  245.0 4.9 %collective-permute-done.5 = bf16[256,1024]{1,0:T(8,128)(2,1)S(1)} collective-permute-done((bf16[256,1024]{1,0:T(8,128)(2,1)S(1)}, bf16[256,1024]{1,0:T(8,128)(2,1)S(1)}, u32[]{:S(2)}, u32[]{:S(2)}) %collective-permute-start.5) | collective-permute-done | bytes 524320 | tf_op jit(solution)/shard_map/ppermute | solution.py:573
  249.9 5.9 %collective-permute-done.6 = bf16[256,1024]{1,0:T(8,128)(2,1)S(1)} collective-permute-done((bf16[256,1024]{1,0:T(8,128)(2,1)S(1)}, bf16[256,1024]{1,0:T(8,128)(2,1)S(1)}, u32[]{:S(2)}, u32[]{:S(2)}) %collective-permute-start.6) | collective-permute-done | bytes 524320 | tf_op jit(solution)/shard_map/ppermute | solution.py:573
  257.2 3.8 convolution_convert_fusion.4.g_ref
  261.0 28.1 %attention_back.1 = (bf16[512,1024]{1,0:T(8,128)(2,1)}, bf16[512,1024]{1,0:T(8,128)(2,1)}, bf16[512,1024]{1,0:T(8,128)(2,1)}) custom-call(bf16[512,1024]{1,0:T(8,128)(2,1)} %get-tuple-element.44.q_ref, bf16[512,1024]{1,0:T(8,128)(2,1)} %get-tuple-element.45.k_ref, bf16[512,1024]{1,0:T(8,128)(2,1)} %get-tuple-element.46.v_ref, ...), custom_call_target="tpu_custom_call" | custom-call | flops 5368709120 | bytes 9437184 | tf_op jit(solution)/shard_map/attention_back/pallas_call | solution.py:530
  292.6 3.5 fusion.51
  298.5 3.9 convolution_convert_fusion.3
  302.4 6.6 %convolution_convert_fusion = bf16[1024,1536]{1,0:T(8,128)(2,1)} fusion(bf16[1536,1024]{1,0:T(8,128)(2,1)S(1)} %copy-done.5, bf16[512,1024]{1,0:T(8,128)(2,1)} %collective-permute-done, bf16[512,1024]{1,0:T(8,128)(2,1)S(1)} %copy-done.10), kind=kOutput, calls=%fused_computation.12 | convolution fusion | flops 3226992640 | bytes 8388608 | tf_op jit(solution)/shard_map/dot_general | solution.py:555
  312.6 3.7 fusion.24
  316.3 150.2 %reduce.8 = (bf16[4,2,32,3072]{3,2,1,0:T(8,128)(2,1)}, bf16[2,4,2,16,1024]{4,3,2,1,0:T(8,128)(2,1)}, bf16[4,2,32,4096]{3,2,1,0:T(8,128)(2,1)}, bf16[2,4,2,64,102...) custom-call(bf16[4,2,2,2,32,1536]{5,4,3,2,1,0:T(8,128)(2,1)} %bitcast.126, ...), custom_call_target="tpu_custom_call" | custom-call | tf_op jit(solution)/shard_map/reduce/pallas_call | solution.py:426
  469.5 3.6 bitcast_convert_fusion.2
  474.8 2.6 bitcast_convert_fusion.1
  478.0 2.6 bitcast_convert_fusion
  (147 shorter events, 43.1 us)
Async XLA Ops:
  132.7 4.3 copy-start
  133.8 4.2 copy-start.17
  137.4 13.3 %copy-start.9 = (bf16[512,1024]{1,0:T(8,128)(2,1)}, bf16[512,1024]{1,0:T(8,128)(2,1)S(1)}, u32[]{:S(2)}) copy-start(bf16[512,1024]{1,0:T(8,128)(2,1)S(1)} %fusion.18) | copy-start | bytes 3145732
  137.4 4.1 collective-permute-start
  137.5 2.8 collective-permute-start.1
  150.7 24.9 %copy-start.14 = (bf16[4,4,2,16,1024]{4,3,2,1,0:T(8,128)(2,1)S(1)}, bf16[4,4,2,16,1024]{4,3,2,1,0:T(8,128)(2,1)}, u32[]{:S(2)}) copy-start(bf16[4,4,2,16,1024]{4,3,2,1,0:T(8,128)(2,1)} %get-tuple-element.41) | copy-start | bytes 3145732
  178.3 2.7 collective-permute-start.2
  183.2 3.0 collective-permute-start.3
  183.4 12.4 %collective-permute-start.7 = (bf16[512,1024]{1,0:T(8,128)(2,1)}, bf16[512,1024]{1,0:T(8,128)(2,1)}, u32[]{:S(2)}, u32[]{:S(2)}) collective-permute-start(bf16[512,1024]{1,0:T(8,128)(2,1)} %bitcast.28), channel_id=1, source_target_pairs={{0,4},{4,0},{1,5},{5,1},{2,6},{6,2},{3,7},{7,3},{8,12},{12,8},{9,1... | collective-permute-start | bytes 3145736 | tf_op jit(solution)/shard_map/ppermute | solution.py:547
  186.2 9.6 %copy-start.19 = (bf16[4,4,2,64,1024]{4,3,2,1,0:T(8,128)(2,1)S(1)}, bf16[4,4,2,64,1024]{4,3,2,1,0:T(8,128)(2,1)}, u32[]{:S(2)}) copy-start(bf16[4,4,2,64,1024]{4,3,2,1,0:T(8,128)(2,1)} %get-tuple-element.43) | copy-start | bytes 12582916
  195.8 10.4 %copy-start.20 = (bf16[4,4,2,32,2048]{4,3,2,1,0:T(8,128)(2,1)S(1)}, bf16[4,4,2,32,2048]{4,3,2,1,0:T(8,128)(2,1)}, u32[]{:S(2)}) copy-start(bf16[4,4,2,32,2048]{4,3,2,1,0:T(8,128)(2,1)} %get-tuple-element.42) | copy-start | bytes 12582916
  206.2 7.6 %copy-start.22 = (bf16[1024,2048]{1,0:T(8,128)(2,1)S(1)}, bf16[1024,2048]{1,0:T(8,128)(2,1)}, u32[]{:S(2)}) copy-start(bf16[1024,2048]{1,0:T(8,128)(2,1)} %get-tuple-element.102) | copy-start | bytes 12582916
  213.6 13.0 %collective-permute-start.8 = (bf16[512,1024]{1,0:T(8,128)(2,1)S(1)}, bf16[512,1024]{1,0:T(8,128)(2,1)S(1)}, u32[]{:S(2)}, u32[]{:S(2)}) collective-permute-start(bf16[512,1024]{1,0:T(8,128)(2,1)S(1)} %slice.199), channel_id=1, source_target_pairs={{0,4},{4,0},{1,5},{5,1},{2,6},{6,2},{3,7},{7,3},{8,12},{12,8},{9,1... | collective-permute-start | bytes 3145736 | tf_op jit(solution)/shard_map/ppermute | solution.py:547
  213.8 5.1 %copy-start.23 = (bf16[1024,2048]{1,0:T(8,128)(2,1)S(1)}, bf16[1024,2048]{1,0:T(8,128)(2,1)}, u32[]{:S(2)}) copy-start(bf16[1024,2048]{1,0:T(8,128)(2,1)} %get-tuple-element.105) | copy-start | bytes 12582916
  218.4 9.3 %collective-permute-start.4 = (bf16[512,1024]{1,0:T(8,128)(2,1)S(1)}, bf16[512,1024]{1,0:T(8,128)(2,1)S(1)}, u32[]{:S(2)}, u32[]{:S(2)}) collective-permute-start(bf16[512,1024]{1,0:T(8,128)(2,1)S(1)} %slice.200), channel_id=1, source_target_pairs={{0,4},{4,0},{1,5},{5,1},{2,6},{6,2},{3,7},{7,3},{8,12},{12,8},{9,1... | collective-permute-start | bytes 3145736 | tf_op jit(solution)/shard_map/ppermute | solution.py:547
  231.5 18.4 %collective-permute-start.5 = (bf16[256,1024]{1,0:T(8,128)(2,1)S(1)}, bf16[256,1024]{1,0:T(8,128)(2,1)S(1)}, u32[]{:S(2)}, u32[]{:S(2)}) collective-permute-start(bf16[256,1024]{1,0:T(8,128)(2,1)S(1)} %get-tuple-element.75), channel_id=1, source_target_pairs={{0,0},{1,1},{2,4},{3,5},{4,2},{5,3},{6,6},{7,7},{8,8},{9,9},{10,12... | collective-permute-start | bytes 1572872 | tf_op jit(solution)/shard_map/ppermute | solution.py:573
  236.8 19.0 %collective-permute-start.6 = (bf16[256,1024]{1,0:T(8,128)(2,1)S(1)}, bf16[256,1024]{1,0:T(8,128)(2,1)S(1)}, u32[]{:S(2)}, u32[]{:S(2)}) collective-permute-start(bf16[256,1024]{1,0:T(8,128)(2,1)S(1)} %get-tuple-element.74), channel_id=1, source_target_pairs={{0,1},{1,0},{2,5},{3,4},{4,3},{5,2},{6,7},{7,6},{8,9},{9,8},{10,13... | collective-permute-start | bytes 1572872 | tf_op jit(solution)/shard_map/ppermute | solution.py:573
  236.9 20.4 %collective-permute-start.9 = (bf16[512,1024]{1,0:T(8,128)(2,1)}, bf16[512,1024]{1,0:T(8,128)(2,1)}, u32[]{:S(2)}, u32[]{:S(2)}) collective-permute-start(bf16[512,1024]{1,0:T(8,128)(2,1)} %get-tuple-element.67), channel_id=1, source_target_pairs={{0,4},{4,0},{1,5},{5,1},{2,6},{6,2},{3,7},{7,3},{8,12},{12,8},{9,1... | collective-permute-start | bytes 3145736 | tf_op jit(solution)/shard_map/ppermute | solution.py:547
  298.4 10.6 %collective-permute-start.10 = (bf16[512,1024]{1,0:T(8,128)(2,1)}, bf16[512,1024]{1,0:T(8,128)(2,1)}, u32[]{:S(2)}, u32[]{:S(2)}) collective-permute-start(bf16[512,1024]{1,0:T(8,128)(2,1)} %slice.198), channel_id=1, source_target_pairs={{0,4},{4,0},{1,5},{5,1},{2,6},{6,2},{3,7},{7,3},{8,12},{12,8},{9,1... | collective-permute-start | bytes 3145736 | tf_op jit(solution)/shard_map/ppermute | solution.py:547
  298.4 4.0 copy-start.5
  298.5 4.0 copy-start.10
  302.4 6.6 %copy-start.3 = (f32[1024,1024]{1,0:T(8,128)S(1)}, f32[1024,1024]{1,0:T(8,128)}, u32[]{:S(2)}) copy-start(f32[1024,1024]{1,0:T(8,128)} %copy-done.2) | copy-start | bytes 12582916
  469.5 4.2 copy-start.16
  469.5 5.3 %copy-start.7 = (bf16[4,2,32,4096]{3,2,1,0:T(8,128)(2,1)S(1)}, bf16[4,2,32,4096]{3,2,1,0:T(8,128)(2,1)}, u32[]{:S(2)}) copy-start(bf16[4,2,32,4096]{3,2,1,0:T(8,128)(2,1)} %get-tuple-element.56) | copy-start | bytes 6291460
  (11 other events, 28.0 us)

commit v4 on v3

--- a/solution.py
+++ b/solution.py
@@ -262,91 +262,129 @@
     )(*raw, small, x, pos, dy)
 
 
-def reduce_body(groups, clips, blocks, *refs):
+def turn(u, cosine, sine):
+    half = HEAD // 2
+    first, second = u[:half], u[half:]
+    return jnp.concatenate(
+        [first * cosine - second * sine, first * sine + second * cosine], axis=0
+    )
+
+
+def dot(a, b):
+    return jnp.dot(a, b, preferred_element_type=F32)
+
+
+def dot_t(a, b):
+    return lax.dot_general(a, b, (((1,), (1,)), ((), ())), preferred_element_type=F32)
+
+
+def tile(i, size):
+    return pl.ds(pl.multiple_of(i * size, size), size)
+
+
+def backward_body(groups, clips, blocks, *refs):
     count = len(blocks)
-    grads, (small, gx) = refs[:count], refs[count : count + 2]
-    outs = refs[count + 2 : 2 * count + 2]
-    small_o, gx_o = refs[2 * count + 2 : 2 * count + 4]
-    scratch = refs[2 * count + 4 :]
-    own_a, own_b, one_a, one_b, two_a, two_b, mine, three, full = (
-        scratch[i * count : (i + 1) * count] for i in range(9)
-    )
-    small_s, small_r, small_z = scratch[9 * count : 9 * count + 3]
-    (os, s1, r1, s2, r2, s3, r3, s4, r4, s5, r5, cs, cr, ls, ss, sr, ts, tr) = scratch[9 * count + 3 :]
+    (gw2, gw1, gu, w1, wo, wq, mix, qs, kr, vb, h1, x2, x, dy, base, rest) = refs[:16]
+    (lse, cosine, sine, g1, g2, gbu) = refs[16:22]
+    outs = refs[22 : 22 + count]
+    small_o, gx_o, y_o = refs[22 + count : 25 + count]
+    (gu_b, w1_b, wo_b, mix_b, qs_b, kr_b, vb_b, h1_b, x2_b, x_b, dy_b) = refs[25 + count : 36 + count]
+    (own_f, give, take, y_take, dx2, low, da, gwo, gwq, ak, av, dq2, dk2, acc, gx) = refs[
+        36 + count : 51 + count
+    ]
+    ld, es, er = refs[51 + count : 54 + count]
+    grads = (gwq, gwo, gw1, gw2)
+    scratch = refs[54 + count :]
+    own_a, own_b, one_a, one_b, two_a, two_b, three, full = (
+        scratch[i * count : (i + 1) * count] for i in range(8)
+    )
+    small_s, small_r, small_z = scratch[8 * count : 8 * count + 3]
+    (os, s1, r1, s2, r2, s3, r3, s4, r4, s5, r5, cs, cr, ls, ss, sr, ts, tr, us, ur) = scratch[
+        8 * count + 3 :
+    ]
+    own, width = own_f.shape
+    inner = mix_b.shape[0]
+    third_width = wq.shape[1]
+    pairs = ((gu, gu_b), (w1, w1_b), (wo, wo_b), (mix, mix_b), (qs, qs_b), (kr, kr_b), (vb, vb_b))
+    pairs += ((h1, h1_b), (x2, x2_b), (x, x_b), (dy, dy_b))
+    loads = [pltpu.make_async_copy(a, b, ld.at[n]) for n, (a, b) in enumerate(pairs)]
+    for copy in loads:
+        copy.start()
     p, c, z = where_am_i()
     hi, lo = lax.div(p, 2), lax.rem(p, 2)
     enter(p, c, z, groups)
     col = [(p, c, lax.rem(z + k, groups)) for k in range(groups)]
     xn, yn, cn = (p ^ 1, c, z), (p ^ 2, c, z), (p, c ^ 1, z)
-    start, finish = move_tokens((gx,), (gx_o,), ts, tr, p, c, z, clips)
-    start()
-    small_s[...] = small[...]
-    for n, target in enumerate((cn, xn, yn)):
-        copy = remote(small_s, small_r.at[n], ss.at[n], sr.at[n], target)
-        copy.start()
-        copy.wait()
-        small_s[...] += small_r[n]
-    tails = [
-        remote(small_s.at[col[k][2]], small_z.at[k], ss.at[2 + k], sr.at[2 + k], col[k])
-        for k in range(1, groups)
-    ]
-    for t in tails:
-        t.start()
-    order = sorted(range(count), key=lambda w: -mine[w].shape[3] * mine[w].shape[2])
+    order = (3, 2, 1, 0)
     units = [(w, j) for w in order for j in [*range(1, groups), 0]]
-    load, c1, c2, c4, c5 = {}, {}, {}, {}, {}
-
-    def stage_zero(u):
+    sides = ((own_a, one_a, two_a, hi, yn), (own_b, one_b, two_b, lo, xn))
+
+    def c1(u, n):
         w, j = u
         g = grads[w].at[lax.rem(z + j, groups)]
-        c1[u, 0] = remote(g.at[:, 1 - lo, 0], one_a[w].at[j], s1.at[w, j, 0], r1.at[w, j, 0], xn)
-        c1[u, 1] = remote(g.at[1 - hi, :, 1], one_b[w].at[j], s1.at[w, j, 1], r1.at[w, j, 1], yn)
-        load[u, 0] = pltpu.make_async_copy(g.at[:, lo, 0], own_a[w].at[j], os.at[w, j, 0])
-        load[u, 1] = pltpu.make_async_copy(g.at[hi, :, 1], own_b[w].at[j], os.at[w, j, 1])
-        for copy in (c1[u, 0], c1[u, 1], load[u, 0], load[u, 1]):
-            copy.start()
+        src, target = (g.at[:, 1 - lo, 0], xn) if n == 0 else (g.at[1 - hi, :, 1], yn)
+        return remote(src, sides[n][1][w].at[j], s1.at[w, j, n], r1.at[w, j, n], target)
+
+    def load(u, n):
+        w, j = u
+        g = grads[w].at[lax.rem(z + j, groups)]
+        src = g.at[:, lo, 0] if n == 0 else g.at[hi, :, 1]
+        return pltpu.make_async_copy(src, sides[n][0][w].at[j], os.at[w, j, n])
+
+    def c2(u, n):
+        w, j = u
+        own, one, two, side, target = sides[n]
+        return remote(own[w].at[j, 1 - side], two[w].at[j], s2.at[w, j, n], r2.at[w, j, n], target)
+
+    def c3(u, n):
+        w, j = u
+        src = sides[n][0][w].at[j, sides[n][3]]
+        return remote(src, three[w].at[j, n], s3.at[w, j, n], r3.at[w, j, n], col[j])
+
+    def c4(w, n):
+        f = full[w].at[p]
+        return remote(f, f, s4.at[w, n], r4.at[w, n], (xn, yn)[n])
+
+    def c5(w, n):
+        f = full[w].at[(p ^ 1, p ^ 2)[n], n]
+        return remote(f, f, s5.at[w, n], r5.at[w, n], (yn, xn)[n])
+
+    def stage_zero(u):
+        for n in range(2):
+            c1(u, n).start()
+            load(u, n).start()
 
     def stage_one(u):
         w, j = u
-        for n, (own, one, two, side, target) in enumerate(
-            ((own_a, one_a, two_a, hi, yn), (own_b, one_b, two_b, lo, xn))
-        ):
-            load[u, n].wait()
-            c1[u, n].wait_recv()
-            o = own[w].at[j]
-            o[...] = (o[...].astype(F32) + one[w][j].astype(F32)).astype(BF)
-            c2[u, n] = remote(o.at[1 - side], two[w].at[j], s2.at[w, j, n], r2.at[w, j, n], target)
-            c2[u, n].start()
-
-    def third(w, j):
-        return remote(mine[w].at[j], three[w].at[j], s3.at[w, j], r3.at[w, j], col[j])
+        for n, (own, one, two, side, target) in enumerate(sides):
+            load(u, n).wait()
+            c1(u, n).wait_recv()
+            own[w][j] = (own[w][j].astype(F32) + one[w][j].astype(F32)).astype(BF)
+            c2(u, n).start()
 
     def stage_two(u):
         w, j = u
-        for n, (own, two, side) in enumerate(((own_a, two_a, hi), (own_b, two_b, lo))):
-            c2[u, n].wait_recv()
-            mine[w][j, n] = (own[w][j, side].astype(F32) + two[w][j].astype(F32)).astype(BF)
-        if j:
-            third(w, j).start()
+        for n, (own, one, two, side, target) in enumerate(sides):
+            c2(u, n).wait_recv()
+            own[w][j, side] = (own[w][j, side].astype(F32) + two[w][j].astype(F32)).astype(BF)
+            if j:
+                c3(u, n).start()
 
     def stage_three(w):
-        total = mine[w][0].astype(F32)
-        for j in range(1, groups):
-            third(w, j).wait_recv()
-            total = total + three[w][j].astype(F32)
-        full[w][p] = total.astype(BF)
-        for n, target in enumerate((xn, yn)):
-            f = full[w].at[p]
-            c4[w, n] = remote(f, f, s4.at[w, n], r4.at[w, n], target)
-            c4[w, n].start()
+        for n, (own, one, two, side, target) in enumerate(sides):
+            total = own[w][0, side].astype(F32)
+            for j in range(1, groups):
+                c3((w, j), n).wait_recv()
+                total = total + three[w][j, n].astype(F32)
+            full[w][p, n] = total.astype(BF)
+        for n in range(2):
+            c4(w, n).start()
 
     def stage_four(w):
-        for n, (q, target) in enumerate(((p ^ 1, yn), (p ^ 2, xn))):
-            f = full[w].at[q]
+        for n, target in enumerate((yn, xn)):
+            f = full[w].at[(p ^ 1, p ^ 2)[n]]
             remote(f, f, s4.at[w, n], r4.at[w, n], target).wait_recv()
-            f = full[w].at[q, n]
-            c5[w, n] = remote(f, f, s5.at[w, n], r5.at[w, n], target)
-            c5[w, n].start()
+            c5(w, n).start()
 
     def stage_five(w):
         for n in range(2):
@@ -356,7 +394,7 @@
             pltpu.make_async_copy(src, dst, ls.at[w]).start()
             remote(src, dst, cs.at[w], cr.at[w], cn).start()
 
-    ahead, lag = 2, 2
+    ahead, lag = 3, 2
     todo = {}
     for n, u in enumerate(units):
         todo.setdefault(max(n - ahead, -1), []).append((stage_zero, u))
@@ -366,9 +404,202 @@
         last = (i + 1) * groups - 1 + lag
         for at, stage in ((2, stage_three), (3, stage_four), (4, stage_five)):
             todo.setdefault(last + at, []).append((stage, w))
-    for n in sorted(todo):
-        for stage, what in todo[n]:
+    steps = sorted(todo)
+
+    def run(step):
+        for stage, what in todo[step]:
             stage(what)
+
+    def tick():
+        run(steps.pop(0))
+
+    def half_sum(n, left, right, depth):
+        def other(i, carry):
+            part = dot_t(left[own:, :depth], right[tile(i, 256), :depth])
+            give[:, tile(i, 256)] = part.astype(BF)
+            return carry
+
+        def self(i, carry):
+            own_f[:, tile(i, 256)] = dot_t(left[:own, :depth], right[tile(i, 256), :depth])
+            return carry
+
+        lax.fori_loop(0, width // 256, other, 0)
+        copy = remote(give, take, es.at[n], er.at[n], cn)
+        copy.start()
+        lax.fori_loop(0, width // 256, self, 0)
+        return copy
+
+    def part(i):
+        per = own // clips // 128
+        return lax.div(i, per), tile(lax.rem(i, per), 128)
+
+    def norm_step(i, field, gain, grad, row):
+        at = tile(i, 128)
+        d = own_f[at] + take[at].astype(F32)
+        v = field[at].astype(F32)
+        v = v - jnp.mean(v, axis=1, keepdims=True)
+        r = lax.rsqrt(jnp.mean(v * v, axis=1, keepdims=True) + EPS)
+        v = v * r
+        acc[row : row + 1] += jnp.sum(d * v, axis=0, keepdims=True)
+        acc[row + 1 : row + 2] += jnp.sum(d, axis=0, keepdims=True)
+        e = d * gain[...]
+        mean = jnp.mean(e, axis=1, keepdims=True)
+        e = e - mean - v * jnp.mean(e * v, axis=1, keepdims=True)
+        return grad + r * e
+
+    tick()
+    y_copy = remote(rest, y_take, es.at[3], er.at[3], cn)
+    y_copy.start()
+    acc[...] = jnp.zeros_like(acc)
+    loads[0].wait()
+    loads[1].wait()
+    swap = half_sum(0, gu_b, w1_b, w1.shape[1])
+    wq_b = w1_b.at[:, :third_width]
+    dqkv = gu_b.at[:, :third_width]
+    late = pltpu.make_async_copy(wq, wq_b, ld.at[len(loads)])
+    late.start()
+    tick()
+    for copy in loads[2:]:
+        copy.wait()
+    swap.wait()
+
+    def second_norm(i, carry):
+        at = tile(i, 128)
+        g = dy_b[part(i)].astype(F32)
+        d = norm_step(i, x2_b, g2, g, 3)
+        dx2[at] = d
+        acc[5:6] += jnp.sum(g, axis=0, keepdims=True)
+        low[at] = d.astype(BF)
+        acc[2:3] += jnp.sum(d.astype(BF).astype(F32), axis=0, keepdims=True)
+        return carry
+
+    lax.fori_loop(0, own // 128, second_norm, 0)
+    swap = remote(low.at[:own], low.at[own:], es.at[1], er.at[1], cn)
+    swap.start()
+    y_base = pltpu.make_async_copy(base, x2_b, ld.at[len(loads) + 1])
+    y_base.start()
+    tick()
+    swap.wait()
+
+    def out_grad(i, carry):
+        at = tile(i, 256)
+        gwo[..., at] = dot(mix_b[...], low[:, at]).astype(BF).reshape(gwo.shape[:-1] + (256,))
+        return carry
+
+    lax.fori_loop(0, width // 256, out_grad, 0)
+
+    def attn_grad(i, carry):
+        at = tile(i, 256)
+        da[:, at] = dot_t(wo_b[...], low[at]).astype(BF)
+        return carry
+
+    lax.fori_loop(0, 2 * own // 256, attn_grad, 0)
+    tick()
+
+    def head(h, side):
+        rows = tile(h, HEAD)
+        place = tile(side, HEAD)
+        co, si = cosine[...], sine[...]
+        kt = kr_b[rows]
+        keys, values = kt.T, vb_b[rows].T
+        queries, outer_grads = qs_b[rows].T, da[rows].T
+        step = 256
+        for i in range(0, 2 * own, step):
+            s = slice(i, i + step)
+            g = da[rows, s]
+            p = jnp.exp(dot(keys, qs_b[rows, s]) - lse[h, :, s])
+            delta = jnp.sum(mix_b[rows, s].astype(F32) * g.astype(F32), axis=0, keepdims=True)
+            ds = (p * (dot(values, g) - delta)).astype(BF)
+            dq2[place, s] = turn(dot(kt, ds) * SCALE, co[:, s], -si[:, s]).astype(BF)
+            dv = dot(p.astype(BF), outer_grads[s])
+            dk = dot(ds, queries[s])
+            if i == 0:
+                ak[...] = dk
+                av[side] = dv
+            else:
+                ak[...] += dk
+                av[side] += dv
+        dk2[place] = turn(ak[...].T, co, -si).astype(BF)
+
+    heads = inner // HEAD
+    during = [steps.pop(0) for _ in range(4)]
+
+    def two_heads(i, carry):
+        lax.fori_loop(0, 2, lambda side, _: head(2 * i + side, side), None)
+        for n, value in enumerate(
+            (dq2[...].T, dk2[...].T, jnp.concatenate([av[0], av[1]], axis=1).astype(BF))
+        ):
+            at = pl.ds(pl.multiple_of(n * inner + i * 2 * HEAD, 2 * HEAD), 2 * HEAD)
+            dqkv[:, at] = value
+        for n, step in enumerate(during):
+            pl.when(i == n * heads // 8)(functools.partial(run, step))
+        return carry
+
+    lax.fori_loop(0, heads // 2, two_heads, 0)
+    y_base.wait()
+    y_copy.wait()
+
+    def last_add(i, carry):
+        at = tile(i, 128)
+        dy_b[part(i)] = (x2_b[at] + y_take[at].astype(F32)).astype(BF)
+        return carry
+
+    lax.fori_loop(0, own // 128, last_add, 0)
+    y_start, y_finish = move_tokens((dy_b,), (y_o,), us, ur, p, c, z, clips)
+    y_start()
+    row = width // groups
+    for g in range(groups):
+        left = h1_b[:, g * row : (g + 1) * row].T
+
+        def in_grad(i, carry):
+            at = tile(i, 512)
+            gwq[g, ..., at] = dot(left, dqkv[:, at]).astype(BF).reshape(gwq.shape[1:-1] + (512,))
+            return carry
+
+        lax.fori_loop(0, third_width // 512, in_grad, 0)
+    tick()
+    late.wait()
+    swap = half_sum(2, dqkv, wq_b, third_width)
+    tick()
+    swap.wait()
+
+    def first_norm(i, carry):
+        gx[part(i)] = norm_step(i, x_b, g1, dx2[tile(i, 128)], 0).astype(BF)
+        return carry
+
+    lax.fori_loop(0, own // 128, first_norm, 0)
+    start, finish = move_tokens((gx,), (gx_o,), ts, tr, p, c, z, clips)
+    start()
+    tick()
+    small_s[...] = jnp.zeros_like(small_s)
+    for n in range(6):
+        for g in range(groups):
+            small_s[g, n : n + 1] = acc[n : n + 1, g * row : (g + 1) * row]
+    half = row // 2
+    mine_at = pl.ds(pl.multiple_of(c * half, half), half)
+    for b in range(3 * groups):
+        line = jnp.sum(dqkv[:, b * half : (b + 1) * half].astype(F32), axis=0, keepdims=True)
+        small_s[b // 3, 6 + b % 3 : 7 + b % 3, mine_at] = line
+    deep = gbu.shape[1] // groups
+    for g in range(groups):
+        for n in range(deep // row):
+            at = pl.ds(9 + c * (deep // row) + n, 1)
+            small_s[g, at] = gbu[:, g * deep + n * row : g * deep + (n + 1) * row]
+    tick()
+    for n, target in enumerate((cn, xn, yn)):
+        copy = remote(small_s, small_r.at[n], ss.at[n], sr.at[n], target)
+        copy.start()
+        tick()
+        copy.wait()
+        small_s[...] += small_r[n]
+    tails = [
+        remote(small_s.at[col[k][2]], small_z.at[k], ss.at[2 + k], sr.at[2 + k], col[k])
+        for k in range(1, groups)
+    ]
+    for t in tails:
+        t.start()
+    while steps:
+        tick()
     for k in range(1, groups):
         tails[k - 1].wait()
     small_o[...] = small_s[z]
@@ -377,32 +608,46 @@
     for u in units:
         w, j = u
         for n in range(2):
-            c1[u, n].wait_send()
-            c2[u, n].wait_send()
-        if j:
-            third(w, j).wait_send()
+            c1(u, n).wait_send()
+            c2(u, n).wait_send()
+            if j:
+                c3(u, n).wait_send()
     for w in range(count):
         for n in range(2):
-            c4[w, n].wait_send()
-            c5[w, n].wait_send()
+            c4(w, n).wait_send()
+            c5(w, n).wait_send()
         pltpu.make_async_copy(full[w], full[w], ls.at[w]).wait()
         remote(full[w], full[w], cs.at[w], cr.at[w], cn).wait()
     finish()
-
-
-def reduce(grads, blocks, small, gx, groups):
-    count, clips = len(grads), gx.shape[0]
+    y_finish()
+
+
+def backward(gw2, gw1, arrays, tables, lines, groups, blocks):
+    gu, w1, wo, wq, mix, qs, kr, vb, h1, x2, x, dy, base, rest = arrays
+    (own, width), clips = x.shape, dy.shape[0]
+    small = jax.ShapeDtypeStruct((groups, lines + -lines % 8, width // groups), F32)
+    count = len(blocks)
     dma = pltpu.SemaphoreType.DMA
-    tiles = [g.shape[4:] for g in grads]
+    split = lambda v: (groups, 2, 2, 2, v.shape[0] // (8 * groups), v.shape[1])
+    tiles = [split(wq)[4:], split(wo)[4:], gw1.shape[4:], gw2.shape[4:]]
     shapes = [
         jax.ShapeDtypeStruct((4, 2, t[0], 2 * t[1]) if b else (2, 4, 2) + t, BF)
         for t, b in zip(tiles, blocks)
     ]
     shapes += [
-        jax.ShapeDtypeStruct(small.shape[1:], small.dtype),
-        jax.ShapeDtypeStruct(gx.shape, gx.dtype),
+        jax.ShapeDtypeStruct(small.shape[1:], F32),
+        jax.ShapeDtypeStruct(dy.shape, BF),
+        jax.ShapeDtypeStruct(dy.shape, BF),
     ]
-    scratch = []
+    scratch = [pltpu.VMEM(v.shape, v.dtype) for v in (gu, w1, wo, mix, qs, kr, vb, h1, x2, x, dy)]
+    half, low = (own, width), pltpu.VMEM((2 * own, width), BF)
+    scratch += [pltpu.VMEM(half, F32)] + [pltpu.VMEM(half, BF)] * 3
+    scratch += [pltpu.VMEM(half, F32), low, pltpu.VMEM(mix.shape, BF)]
+    scratch += [pltpu.VMEM(split(wo), BF), pltpu.VMEM(split(wq), BF)]
+    scratch += [pltpu.VMEM((2 * own, HEAD), F32), pltpu.VMEM((2, 2 * own, HEAD), F32)]
+    scratch += [pltpu.VMEM((2 * HEAD, 2 * own), BF)] * 2
+    scratch += [pltpu.VMEM((8, width), F32), pltpu.VMEM(dy.shape, BF)]
+    scratch += [dma((13,)), dma((4,)), dma((4,))]
     for lead in (
         (groups, 2),
         (groups, 2),
@@ -410,7 +655,6 @@
         (groups, 2),
         (groups,),
         (groups,),
-        (groups, 2),
         (groups, 2),
         (4, 2),
     ):
@@ -421,31 +665,19 @@
         pltpu.VMEM(small.shape, F32),
     ]
     pair = dma((count, groups, 2))
-    scratch += [pair] * 5 + [dma((count, groups))] * 2 + [dma((count, 2))] * 4
-    scratch += [dma((count,))] * 3 + [dma((2 + groups,))] * 2 + [dma((1, clips))] * 2
+    scratch += [pair] * 7 + [dma((count, 2))] * 4
+    scratch += [dma((count,))] * 3 + [dma((2 + groups,))] * 2 + [dma((1, clips))] * 4
     return pl.pallas_call(
-        functools.partial(reduce_body, groups, clips, blocks),
+        functools.partial(backward_body, groups, clips, blocks),
         out_shape=shapes,
-        in_specs=[ANY] * count + [VM, ANY],
-        out_specs=[ANY] * count + [VM, ANY],
+        in_specs=[ANY] * (2 + len(arrays)) + [VM] * len(tables),
+        out_specs=[ANY] * count + [VM, ANY, ANY],
         scratch_shapes=scratch,
         compiler_params=pltpu.CompilerParams(
-            collective_id=1, has_side_effects=True, vmem_limit_bytes=60 * 1024 * 1024
+            collective_id=1, has_side_effects=True, vmem_limit_bytes=67043328
         ),
-        name="reduce",
-    )(*grads, small, gx)
-
-
-def turn(u, cosine, sine):
-    half = HEAD // 2
-    first, second = u[:half], u[half:]
-    return jnp.concatenate(
-        [first * cosine - second * sine, first * sine + second * cosine], axis=0
-    )
-
-
-def dot(a, b):
-    return jnp.dot(a, b, preferred_element_type=F32)
+        name="backward",
+    )(gw2, gw1, *arrays, *tables)
 
 
 def attention_body(step, q_ref, k_ref, v_ref, cos_ref, sin_ref, qs_ref, kr_ref, vb_ref, o_ref, l_ref):
@@ -491,58 +723,6 @@
     )(qkv, qkv, qkv, cosine, sine)
 
 
-def attention_back_body(
-    step, q_ref, k_ref, v_ref, o_ref, l_ref, g_ref, cos_ref, sin_ref, dq_ref, dk_ref, dv_ref, ak, av
-):
-    cosine, sine = cos_ref[...], sin_ref[...]
-    length = cosine.shape[1]
-    kt, keys, values = k_ref[...], k_ref[...].T, v_ref[...].T
-    queries, grads = q_ref[...].T, g_ref[...].T
-    for i in range(0, length, step):
-        s = slice(i, i + step)
-        g = g_ref[:, s]
-        scores = dot(keys, q_ref[:, s])
-        p = jnp.exp(scores - l_ref[0, :, s])
-        dp = dot(values, g)
-        delta = jnp.sum(o_ref[:, s].astype(F32) * g.astype(F32), axis=0, keepdims=True)
-        ds = (p * (dp - delta)).astype(BF)
-        dq = dot(kt, ds) * SCALE
-        dq_ref[:, s] = turn(dq, cosine[:, s], -sine[:, s]).astype(BF)
-        dv = dot(p.astype(BF), grads[s])
-        dk = dot(ds, queries[s])
-        if i == 0:
-            ak[...] = dk
-            av[...] = dv
-        else:
-            ak[...] += dk
-            av[...] += dv
-    dk_ref[...] = turn(ak[...].T, cosine, -sine).astype(BF)
-    dv_ref[...] = av[...].T.astype(BF)
-
-
-def attention_back(qs, kr, vb, out, lse, grad, cosine, sine, step=256):
-    width, length = qs.shape
-    heads = width // HEAD
-    row = pl.BlockSpec((HEAD, length), lambda h: (h, 0))
-    table = pl.BlockSpec((HEAD // 2, length), lambda h: (0, 0))
-    line = pl.BlockSpec((1, 1, length), lambda h: (h, 0, 0))
-    shape = jax.ShapeDtypeStruct((width, length), BF)
-    return pl.pallas_call(
-        functools.partial(attention_back_body, step),
-        out_shape=[shape] * 3,
-        grid=(heads,),
-        in_specs=[row] * 4 + [line, row, table, table],
-        out_specs=[row] * 3,
-        scratch_shapes=[pltpu.VMEM((length, HEAD), F32)] * 2,
-        cost_estimate=pl.CostEstimate(
-            flops=10 * width * length * length,
-            transcendentals=heads * length * length,
-            bytes_accessed=width * length * 18,
-        ),
-        name="attention_back",
-    )(qs, kr, vb, out, lse, grad, cosine, sine)
-
-
 def swap(value):
     return lax.ppermute(value, "core", [(0, 1), (1, 0)])
 
@@ -558,26 +738,6 @@
 def own_sum(partial):
     half = partial.shape[0] // 2
     return partial[:half] + swap(partial[half:].astype(BF)).astype(F32)
-
-
-def move_blocks(x, clips, groups):
-    c, z = lax.axis_index("core"), lax.axis_index("grp")
-    got = []
-    for t in range(clips):
-        pairs = []
-        for cc in range(2):
-            for zz in range(groups):
-                i = (t + zz) % clips
-                pairs.append((cc * groups + zz, (zz // clips) * groups + cc * clips + i))
-        block = lax.dynamic_index_in_dim(x, lax.rem(t + z, clips), 0, keepdims=False)
-        got.append(lax.ppermute(block, ("core", "grp"), pairs))
-    stacked = jnp.stack(got)
-    return jnp.stack(
-        [
-            lax.dynamic_index_in_dim(stacked, lax.rem(z - m + clips, clips), 0, keepdims=False)
-            for m in range(clips)
-        ]
-    )
 
 
 def paired(
@@ -636,7 +796,6 @@
 
     grad_out = dy.reshape(own, width)
     grad_all = both(grad_out)
-    grad_f = grad_out.astype(F32)
 
     pos = jnp.moveaxis(pos[:, :3], 1, 0).reshape(3, own)
     pos = jnp.concatenate([pos, swap(pos)], axis=1)
@@ -650,49 +809,30 @@
     angles = chosen * freq[:, None]
     cosine, sine = jnp.cos(angles), jnp.sin(angles)
 
-    x = x.reshape(own, width).astype(F32)
-    n1, r1 = normalize(x)
-    h1 = both((n1 * g1 + b1).astype(BF))
+    tokens = x.reshape(own, width)
+    x = tokens.astype(F32)
+    h1 = both((normalize(x)[0] * g1 + b1).astype(BF))
     qkv = contract(wq, h1, 0, 1) + bq_own
     qs, kr, vb, mixed, lse = attention(qkv, cosine, sine)
     x2 = x + own_sum(contract(mixed, wo, 0, 0)) + bo
-    n2, r2 = normalize(x2)
-    h2 = both((n2 * g2 + b2).astype(BF))
+    h2 = both((normalize(x2)[0] * g2 + b2).astype(BF))
     u = contract(h2, w1, 1, 0) + bu_own
     cdf = 0.5 * (1.0 + lax.erf(u * F32(0.7071067811865476)))
     act = (u * cdf).astype(BF)
     slope = (cdf + u * jnp.exp(-0.5 * u * u) * F32(0.3989422804014327)).astype(BF)
-    result = (x2 + own_sum(contract(act, w2, 1, 0)) + bd).astype(BF)
-    output = move_blocks(result.reshape(clips, part, width), clips, groups)
+    result = contract(act, w2, 1, 0)
+    base, rest = x2 + result[:own] + bd, result[own:].astype(BF)
 
     gw2 = contract(act, grad_all, 0, 0).astype(BF)
     gu = (contract(grad_all, w2, 1, 1) * slope.astype(F32)).astype(BF)
     gw1 = contract(h2, gu, 0, 0).astype(BF)
     gbu = jnp.sum(gu.astype(F32), axis=0)
-    dh2 = own_sum(contract(gu, w1, 1, 1))
-    gg2, gb2 = jnp.sum(dh2 * n2, axis=0), jnp.sum(dh2, axis=0)
-    dx2 = grad_f + norm_back(dh2 * g2, n2, r2)
-    low = dx2.astype(BF)
-    low_all = both(low)
-    gwo = contract(mixed, low_all, 1, 0).astype(BF)
-    da = contract(wo, low_all, 1, 1).astype(BF)
-    dqkv = jnp.concatenate(attention_back(qs, kr, vb, mixed, lse, da, cosine, sine), axis=0)
-    gwq = contract(h1, dqkv, 0, 1).astype(BF)
-    gbq = jnp.sum(dqkv.astype(F32), axis=1)
-    dh1 = own_sum(contract(dqkv, wq, 0, 1))
-    gg1, gb1 = jnp.sum(dh1 * n1, axis=0), jnp.sum(dh1, axis=0)
-    gx = (dx2 + norm_back(dh1 * g1, n1, r1)).astype(BF)
-
-    mine = (jnp.arange(2) == c).astype(F32)
-    gbq = gbq.reshape(bq * groups, 1, row // 2) * mine[None, :, None]
-    gbu = gbu.reshape(groups, 1, deep // groups) * mine[None, :, None]
-    vectors = (gg1, gb1, jnp.sum(low.astype(F32), axis=0), gg2, gb2, jnp.sum(grad_f, axis=0), gbq, gbu)
-    sums = jnp.concatenate([v.reshape(groups, -1, row) for v in vectors], axis=1)
-    sums = jnp.pad(sums, ((0, 0), (0, -lines % 8), (0, 0)))
-    grads = [g.reshape(groups, 2, 2, 2, g.shape[0] // (8 * groups), g.shape[1]) for g in (gwq, gwo, gw1, gw2)]
-    gwq, gwo, gw1, gw2, sums, gx = reduce(
-        grads, blocks, sums, gx.reshape(clips, part, width), groups
-    )
+    gw2, gw1 = (
+        g.reshape(groups, 2, 2, 2, g.shape[0] // (8 * groups), g.shape[1]) for g in (gw2, gw1)
+    )
+    arrays = (gu, w1, wo, wq, mixed, qs, kr, vb, h1, x2, tokens, dy, base, rest)
+    tables = (lse, cosine, sine, g1, g2, gbu.reshape(1, deep))
+    gwq, gwo, gw1, gw2, sums, gx, output = backward(gw2, gw1, arrays, tables, lines, groups, blocks)
     gwq, gwo, gw1, gw2 = (
         g.reshape(shard.shape).astype(F32)
         for g, shard in zip((gwq, gwo, gw1, gw2), (w_qkv, w_out, w_up, w_down))

time: 491 us -> 420 us (0.86)
  matrix products: 76.7 us -> 50.4 us
  waiting for transfers between devices: 16.3 us -> 4.56 us
  Pallas kernels: 328 us -> 317 us
  other arithmetic: 37.7 us -> 30.1 us
  starting transfers between devices: 7.33 us -> 1.26 us
    dot_general x12 -> x7, matrix products: 76.7 us -> 50.4 us  [contract(): lax.dot_general(left, right, (((a,), (b,)), ((), ())), preferred_element_...]
    pallas_call x2 -> x1, Pallas kernels: 178 us -> 167 us  [backward(): pl.pallas_call(functools.partial(backward_body, groups, clips, blocks), o...]
    ppermute x2 -> x0, waiting for transfers between devices: 10.8 us -> none  [move_blocks(): got.append(lax.ppermute(block, ('core', 'grp'), pairs))]
    reduce_sum x5 -> x0, other arithmetic: 9.16 us -> none  [the longest x1 3.71 us: paired(): jnp.sum(low.astype(F32), axis=0)]
    ppermute x2 -> x0, starting transfers between devices: 5.35 us -> none  [move_blocks(): got.append(lax.ppermute(block, ('core', 'grp'), pairs))]
  transfers between devices with their start and end apart: 11 -> 5, of which waited for: 5 -> 2; matrix products, arithmetic and copies ran while one was open for 10% -> 5% of each run, Pallas kernels for 0% -> 0%
where the time goes in v4:
time: 420 us; the launch traced here: 414 us
  Pallas kernels  317 us (75%)
  matrix products  50.4 us (12%)
  other arithmetic  30.1 us (7%)
  local copies, waits for them, and re-layouts  9.37 us (2%)
  waiting for transfers between devices  4.56 us (1%)
    pallas_call x1, Pallas kernels, backward(): pl.pallas_call(functools.partial(backward_body, groups, clips, blocks), o...  167 us
    pallas_call x1, Pallas kernels, gather(): pl.pallas_call(functools.partial(gather_body, groups, clips, blocks), out...  125 us
    dot_general x7, matrix products, contract(): lax.dot_general(left, right, (((a,), (b,)), ((), ())), preferred_element_...  50.4 us
    pallas_call x1, Pallas kernels, attention(): pl.pallas_call(functools.partial(attention_body, step), out_shape=[shape]...  24.6 us
    convert_element_type x4, other arithmetic, paired(): g.reshape(shard.shape).astype(F32)  10.8 us
  transfers between devices with their start and end apart: 5, of which 2 were waited for; matrix products, arithmetic and copies ran while one was open for 5% of the time, Pallas kernels for 0%

profile of v4, /device:TPU:9, one launch (start us, length us, event | category | flops | bytes accessed | tf_op | source)
XLA Modules:
  0.0 413.9 jit_solution(1204673675652529781)
XLA Ops:
  7.5 125.2 %gather.1 = (bf16[4,4,2,32,1536]{4,3,2,1,0:T(8,128)(2,1)}, bf16[4,4,2,16,1024]{4,3,2,1,0:T(8,128)(2,1)}, bf16[4,4,2,32,2048]{4,3,2,1,0:T(8,128)(2,1)}, bf16[4,4,...) custom-call(bf16[4,2,32,3072]{3,2,1,0:T(8,128)(2,1)} %bitcast.82, ...), custom_call_target="tpu_custom_call" | custom-call | tf_op jit(solution)/shard_map/gather/pallas_call | solution.py:249
  132.7 1.5 convert_reduce_fusion.1
  134.2 1.6 fusion.11
  137.0 1.7 fusion.8
  139.4 2.0 collective-permute-done.1
  141.4 1.3 fusion.14
  142.7 9.0 %convolution_add_fusion.q_ref.k_ref.v_ref = f32[1536,1024]{1,0:T(8,128)} fusion(bf16[1024,1536]{1,0:T(8,128)(2,1)} %bitcast.78, f32[1536]{0:T(1024)S(1)} %add.125, bf16[512,1024]{1,0:T(8,128)(2,1)S(1)} %collective-permute-done, bf16[512,1024]{1,0:T(8,128)(2,1)S(1)} %fusion.8), kind=kOutput, calls=%fused_computation.10 | convolution fusion | flops 3226992640 | bytes 11540480 | tf_op jit(solution)/shard_map/dot_general | solution.py:735
  151.7 24.6 %attention.1 = (bf16[512,1024]{1,0:T(8,128)(2,1)}, bf16[512,1024]{1,0:T(8,128)(2,1)}, bf16[512,1024]{1,0:T(8,128)(2,1)}, bf16[512,1024]{1,0:T(8,128)(2,1)}, f32[8,1,1024]{2,1,0:T(1,128)}) custom-call(f32[1536,1024]{1,0:T(8,128)} %convolution_add_fusion.q_ref.k_ref.v_ref, f32[1536,1024]{1,0:T(8,128)} %convolution_add_fusion.q_ref.k_ref.v_ref, ...), custom_call_target="tpu_custom_call" | custom-call | flops 2147483648 | bytes 12582912 | tf_op jit(solution)/shard_map/attention/pallas_call | solution.py:711
  176.4 2.6 fusion.28
  179.4 2.5 collective-permute-done.2
  182.8 1.4 add_convert_fusion
  184.8 2.9 pad_maximum_fusion.refs_10_
  187.7 7.7 %multiply_convert_fusion.1 = (bf16[1024,2048]{1,0:T(8,128)(2,1)S(1)}, f32[1024,2048]{1,0:T(8,128)S(1)}) fusion(f32[2048]{0:T(1024)S(1)} %bitcast.98, bf16[1024,2048]{1,0:T(8,128)(2,1)S(1)} %bitcast.73, bf16[512,1024]{1,0:T(8,128)(2,1)} %collective-permute-done.3, bf16[512,1024]{1,0:T(8,128)(2,1)} %add_convert_fusion), kind=kOutput, calls=%fused_computation.8 | convolution fusion | flops 4311744512 | bytes 18882560 | tf_op jit(solution)/shard_map/dot_general | solution.py:735
  195.4 4.5 %fusion.29 = f32[1024,1024]{1,0:T(8,128)S(1)} fusion(bf16[1024,2048]{1,0:T(8,128)(2,1)S(1)} %get-tuple-element.82, bf16[2048,1024]{1,0:T(8,128)(2,1)S(1)} %bitcast.109), kind=kOutput, calls=%fused_computation.91 | convolution fusion | flops 4294967296 | bytes 12582912 | tf_op jit(solution)/shard_map/dot_general | solution.py:735
  201.1 1.8 fusion.12.refs_14_
  202.9 7.7 %convolution_convert_fusion.1 = bf16[2048,1024]{1,0:T(8,128)(2,1)} fusion(bf16[1024,2048]{1,0:T(8,128)(2,1)S(1)} %get-tuple-element.82, bf16[512,1024]{1,0:T(8,128)(2,1)} %collective-permute-done.4, bf16[512,1024]{1,0:T(8,128)(2,1)} %bitcast.21), kind=kOutput, calls=%fused_computation.12 | convolution fusion | flops 4301258752 | bytes 10485760 | tf_op jit(solution)/shard_map/dot_general | solution.py:735
  210.6 9.5 %convert_reduce_fusion = (f32[2048]{0:T(1024)}, bf16[1024,2048]{1,0:T(8,128)(2,1)S(1)}) fusion(f32[1024,2048]{1,0:T(8,128)S(1)} %get-tuple-element.83, f32[2048]{0:T(1024)S(1)} %bitcast.99, bf16[2048,1024]{1,0:T(8,128)(2,1)S(1)} %bitcast.110, bf16[512,1024]{1,0:T(8,128)(2,1)} %collective-permute-done.4, bf16[512,1024]{1,0:T(8,128)(2,1)} %bitcast.21), kind=kOutput, calls=%fused_computation.6 | convolution fusion | flops 4330616832 | bytes 18890752 | tf_op jit(solution)/shard_map/dot_general | solution.py:735
  220.1 9.3 %convolution_convert_fusion = bf16[1024,2048]{1,0:T(8,128)(2,1)} fusion(bf16[1024,2048]{1,0:T(8,128)(2,1)S(1)} %get-tuple-element.85.refs_2_, bf16[512,1024]{1,0:T(8,128)(2,1)} %collective-permute-done.3, bf16[512,1024]{1,0:T(8,128)(2,1)} %add_convert_fusion), kind=kOutput, calls=%fused_computation.11 | convolution fusion | flops 4301258752 | bytes 10485760 | tf_op jit(solution)/shard_map/dot_general | solution.py:735
  229.4 167.2 %backward.1 = (bf16[4,2,32,3072]{3,2,1,0:T(8,128)(2,1)}, bf16[2,4,2,16,1024]{4,3,2,1,0:T(8,128)(2,1)}, bf16[4,2,32,4096]{3,2,1,0:T(8,128)(2,1)}, bf16[2,4,2,64,1...) custom-call(bf16[4,2,2,2,64,1024]{5,4,3,2,1,0:T(8,128)(2,1)} %bitcast., ...), custom_call_target="tpu_custom_call" | custom-call | tf_op jit(solution)/shard_map/backward/pallas_call | solution.py:670
  398.2 1.5 fusion.27
  400.9 2.1 bitcast_convert_fusion.3
  403.0 3.4 bitcast_convert_fusion.2
  406.5 2.6 bitcast_convert_fusion.1
  409.1 2.6 bitcast_convert_fusion
  (87 shorter events, 16.3 us)
Async XLA Ops:
  132.7 6.1 %copy-start.15 = (f32[2,8,256]{2,1,0:T(8,128)S(1)}, f32[2,8,256]{2,1,0:T(8,128)}, u32[]{:S(2)}) copy-start(f32[2,8,256]{2,1,0:T(8,128)} %get-tuple-element.37) | copy-start | bytes 49156
  132.7 6.6 %copy-start.12 = (f32[4,16,256]{2,1,0:T(8,128)S(1)}, f32[4,16,256]{2,1,0:T(8,128)}, u32[]{:S(2)}) copy-start(f32[4,16,256]{2,1,0:T(8,128)} %get-tuple-element.36) | copy-start | bytes 196612
  137.0 14.7 %copy-start.14 = (f32[4,1,256]{2,1,0:T(1,128)}, f32[4,1,256]{2,1,0:T(1,128)S(1)}, u32[]{:S(2)}) copy-start(f32[4,1,256]{2,1,0:T(1,128)S(1)} %get-tuple-element.61) | copy-start | bytes 12292
  137.0 45.8 %copy-start.13 = (f32[4,1,256]{2,1,0:T(1,128)}, f32[4,1,256]{2,1,0:T(1,128)S(1)}, u32[]{:S(2)}) copy-start(f32[4,1,256]{2,1,0:T(1,128)S(1)} %get-tuple-element.58) | copy-start | bytes 12292
  138.7 13.0 %copy-start.4 = (bf16[512,1024]{1,0:T(8,128)(2,1)}, bf16[512,1024]{1,0:T(8,128)(2,1)S(1)}, u32[]{:S(2)}) copy-start(bf16[512,1024]{1,0:T(8,128)(2,1)S(1)} %fusion.8) | copy-start | bytes 3145732
  138.7 4.0 collective-permute-start
  138.8 2.6 collective-permute-start.1
  142.7 9.0 %copy-start.11 = (bf16[512,1024]{1,0:T(8,128)(2,1)}, bf16[512,1024]{1,0:T(8,128)(2,1)S(1)}, u32[]{:S(2)}) copy-start(bf16[512,1024]{1,0:T(8,128)(2,1)S(1)} %collective-permute-done) | copy-start | bytes 3145732
  151.7 24.7 %copy-start.6 = (bf16[4,4,2,16,1024]{4,3,2,1,0:T(8,128)(2,1)S(1)}, bf16[4,4,2,16,1024]{4,3,2,1,0:T(8,128)(2,1)}, u32[]{:S(2)}) copy-start(bf16[4,4,2,16,1024]{4,3,2,1,0:T(8,128)(2,1)} %get-tuple-element.39) | copy-start | bytes 3145732
  176.4 5.5 %copy-start.1 = (bf16[2,256,1024]{2,1,0:T(8,128)(2,1)S(1)}, bf16[2,256,1024]{2,1,0:T(8,128)(2,1)}, u32[]{:S(2)}) copy-start(bf16[2,256,1024]{2,1,0:T(8,128)(2,1)} %get-tuple-element.34) | copy-start | bytes 3145732
  179.2 2.7 collective-permute-start.2
  182.4 18.6 %copy-start = (f32[512,1024]{1,0:T(8,128)}, f32[512,1024]{1,0:T(8,128)S(1)}, u32[]{:S(2)}) copy-start(f32[512,1024]{1,0:T(8,128)S(1)} %get-tuple-element.55.refs_11_) | copy-start | bytes 6291460
  182.4 2.3 copy-start.5
  184.2 3.5 collective-permute-start.3
  184.3 18.5 %collective-permute-start.4 = (bf16[512,1024]{1,0:T(8,128)(2,1)}, bf16[512,1024]{1,0:T(8,128)(2,1)}, u32[]{:S(2)}, u32[]{:S(2)}) collective-permute-start(bf16[512,1024]{1,0:T(8,128)(2,1)} %bitcast.21), channel_id=1, source_target_pairs={{0,4},{4,0},{1,5},{5,1},{2,6},{6,2},{3,7},{7,3},{8,12},{12,8},{9,1... | collective-permute-start | bytes 3145736 | tf_op jit(solution)/shard_map/ppermute | solution.py:727
  184.7 2.9 copy-start.2
  187.7 7.7 %copy-start.16 = (bf16[4,4,2,64,1024]{4,3,2,1,0:T(8,128)(2,1)S(1)}, bf16[4,4,2,64,1024]{4,3,2,1,0:T(8,128)(2,1)}, u32[]{:S(2)}) copy-start(bf16[4,4,2,64,1024]{4,3,2,1,0:T(8,128)(2,1)} %get-tuple-element.42) | copy-start | bytes 12582916
  220.1 9.3 %copy-start.3 = (bf16[1024,2048]{1,0:T(8,128)(2,1)}, bf16[1024,2048]{1,0:T(8,128)(2,1)S(1)}, u32[]{:S(2)}) copy-start(bf16[1024,2048]{1,0:T(8,128)(2,1)S(1)} %get-tuple-element.85.refs_2_) | copy-start | bytes 12582916
  396.6 9.8 %copy-start.8 = (bf16[4,2,32,4096]{3,2,1,0:T(8,128)(2,1)S(1)}, bf16[4,2,32,4096]{3,2,1,0:T(8,128)(2,1)}, u32[]{:S(2)}) copy-start(bf16[4,2,32,4096]{3,2,1,0:T(8,128)(2,1)} %get-tuple-element.52) | copy-start | bytes 6291460
  406.5 2.7 copy-start.7
  409.1 2.6 copy-start.10
  409.1 3.6 copy-start.9

commit v5 on v4

--- a/solution.py
+++ b/solution.py
@@ -56,19 +56,27 @@
     def here(i):
         return jnp.logical_and(core == c, c * clips + i == z)
 
-    def start():
+    def start(k, pieces):
         for n, (src, dst) in enumerate(zip(refs, outs)):
+            rows = src.shape[1] // pieces
+            rows = pl.ds(k * rows, rows)
             for i in range(clips):
                 tc, tz = route(i)
 
                 @pl.when(here(i))
                 def _():
-                    pltpu.make_async_copy(src.at[i], dst.at[slot], recv.at[n, slot]).start()
+                    pltpu.make_async_copy(
+                        src.at[i, rows], dst.at[slot, rows], recv.at[n, slot]
+                    ).start()
 
                 @pl.when(jnp.logical_not(here(i)))
                 def _():
                     remote(
-                        src.at[i], dst.at[slot], send.at[n, i], recv.at[n, slot], (p, tc, tz)
+                        src.at[i, rows],
+                        dst.at[slot, rows],
+                        send.at[n, i],
+                        recv.at[n, slot],
+                        (p, tc, tz),
                     ).start()
 
     def finish():
@@ -106,7 +114,9 @@
     outs = refs[count + 4 : 2 * count + 4]
     small_o, x_o, pos_o, dy_o = refs[2 * count + 4 : 2 * count + 8]
     halves = refs[2 * count + 8 : 3 * count + 8]
-    zs, zr, xs, xr, ys, yr, fs, fr, hs, ls, ss, sr, ts, tr, us, ur = refs[3 * count + 8 :]
+    zs, zr, xs, xr, ys, yr, fs, fr, hs, ls, ss, sr, ts, tr, us, ur, vs, vr = refs[
+        3 * count + 8 :
+    ]
     p, c, z = where_am_i()
     for w in range(count):
         for src, dst in cuts(raw[w], halves[w], c, blocks[w]):
@@ -115,8 +125,8 @@
     col = [(p, c, lax.rem(z + k, groups)) for k in range(groups)]
     org = [lax.rem(z + groups - k, groups) for k in range(groups)]
     xn, yn = (p ^ 1, c, z), (p ^ 2, c, z)
-    start, finish = move_tokens((x, pos), (x_o, pos_o), ts, tr, p, c, z, clips)
-    start()
+    start_pos, finish_pos = move_tokens((pos,), (pos_o,), vs, vr, p, c, z, clips)
+    start_x, finish_x = move_tokens((x,), (x_o,), ts, tr, p, c, z, clips)
     smalls = [
         remote(small, small_o.at[z], ss.at[k], sr.at[k], col[k]) for k in range(1, groups)
     ]
@@ -211,7 +221,10 @@
             hop(w, d, side, halves[w].at[p]).wait_send()
 
     own(0)
+    start_pos(0, 1)
     own(1)
+    moves = {2 * k: (start_x, k) for k in range(4)}
+    moves.update({10 + 3 * k: (start_dy, k) for k in range(4)})
     lag = 3
     for n in range(len(units) + lag):
         if n < len(units):
@@ -219,8 +232,8 @@
             w, d, side = units[n]
             if (d, side) == (1, 1) and w + 2 < count:
                 own(w + 2)
-            if n + 1 == len(units):
-                start_dy()
+            if n in moves:
+                moves[n][0](moves[n][1], 4)
         if n >= lag:
             forward(units[n - lag])
     for u in units:
@@ -231,7 +244,8 @@
         s.wait_send()
     for k in keep:
         k.wait()
-    finish()
+    finish_pos()
+    finish_x()
     finish_dy()
 
 
@@ -255,8 +269,7 @@
         + [dma((count, 2, groups))] * 6
         + [dma((count, 2, groups, 2))] * 2
         + [dma((count,)), dma((count + 1,)), dma((groups,)), dma((groups,))]
-        + [dma((2, clips))] * 2
-        + [dma((1, clips))] * 2,
+        + [dma((1, clips))] * 6,
         compiler_params=pltpu.CompilerParams(collective_id=0, has_side_effects=True),
         name="gather",
     )(*raw, small, x, pos, dy)
@@ -450,6 +463,8 @@
     tick()
     y_copy = remote(rest, y_take, es.at[3], er.at[3], cn)
     y_copy.start()
+    y_base = pltpu.make_async_copy(base, dx2, ld.at[len(loads) + 1])
+    y_base.start()
     acc[...] = jnp.zeros_like(acc)
     loads[0].wait()
     loads[1].wait()
@@ -459,6 +474,18 @@
     late = pltpu.make_async_copy(wq, wq_b, ld.at[len(loads)])
     late.start()
     tick()
+    y_base.wait()
+    y_copy.wait()
+
+    def last_add(i, carry):
+        at = tile(i, 128)
+        gx[part(i)] = (dx2[at] + y_take[at].astype(F32)).astype(BF)
+        return carry
+
+    lax.fori_loop(0, own // 128, last_add, 0)
+    y_start, y_finish = move_tokens((gx,), (y_o,), us, ur, p, c, z, clips)
+    y_start(0, 2)
+    y_start(1, 2)
     for copy in loads[2:]:
         copy.wait()
     swap.wait()
@@ -476,8 +503,6 @@
     lax.fori_loop(0, own // 128, second_norm, 0)
     swap = remote(low.at[:own], low.at[own:], es.at[1], er.at[1], cn)
     swap.start()
-    y_base = pltpu.make_async_copy(base, x2_b, ld.at[len(loads) + 1])
-    y_base.start()
     tick()
     swap.wait()
 
@@ -536,17 +561,6 @@
         return carry
 
     lax.fori_loop(0, heads // 2, two_heads, 0)
-    y_base.wait()
-    y_copy.wait()
-
-    def last_add(i, carry):
-        at = tile(i, 128)
-        dy_b[part(i)] = (x2_b[at] + y_take[at].astype(F32)).astype(BF)
-        return carry
-
-    lax.fori_loop(0, own // 128, last_add, 0)
-    y_start, y_finish = move_tokens((dy_b,), (y_o,), us, ur, p, c, z, clips)
-    y_start()
     row = width // groups
     for g in range(groups):
         left = h1_b[:, g * row : (g + 1) * row].T
@@ -562,6 +576,7 @@
     swap = half_sum(2, dqkv, wq_b, third_width)
     tick()
     swap.wait()
+    y_finish()
 
     def first_norm(i, carry):
         gx[part(i)] = norm_step(i, x_b, g1, dx2[tile(i, 128)], 0).astype(BF)
@@ -569,7 +584,7 @@
 
     lax.fori_loop(0, own // 128, first_norm, 0)
     start, finish = move_tokens((gx,), (gx_o,), ts, tr, p, c, z, clips)
-    start()
+    start(0, 4)
     tick()
     small_s[...] = jnp.zeros_like(small_s)
     for n in range(6):
@@ -589,7 +604,9 @@
     for n, target in enumerate((cn, xn, yn)):
         copy = remote(small_s, small_r.at[n], ss.at[n], sr.at[n], target)
         copy.start()
-        tick()
+        start(n + 1, 4)
+        for _ in range(1 if n == 0 else 3):
+            tick()
         copy.wait()
         small_s[...] += small_r[n]
     tails = [
@@ -619,7 +636,6 @@
         pltpu.make_async_copy(full[w], full[w], ls.at[w]).wait()
         remote(full[w], full[w], cs.at[w], cr.at[w], cn).wait()
     finish()
-    y_finish()
 
 
 def backward(gw2, gw1, arrays, tables, lines, groups, blocks):

time: 420 us -> 400 us (0.952)
  Pallas kernels: 317 us -> 295 us
    pallas_call x1, Pallas kernels: 125 us -> 106 us  [gather(): pl.pallas_call(functools.partial(gather_body, groups, clips, blocks), out...]
where the time goes in v5:
time: 400 us; the launch traced here: 395 us
  Pallas kernels  295 us (74%)
  matrix products  50.4 us (13%)
  other arithmetic  30.1 us (8%)
  local copies, waits for them, and re-layouts  9.37 us (2%)
  starting transfers between devices  4.38 us (1%)
  waiting for transfers between devices  4.37 us (1%)
    pallas_call x1, Pallas kernels, backward(): pl.pallas_call(functools.partial(backward_body, groups, clips, blocks), o...  164 us
    pallas_call x1, Pallas kernels, gather(): pl.pallas_call(functools.partial(gather_body, groups, clips, blocks), out...  106 us
    dot_general x7, matrix products, contract(): lax.dot_general(left, right, (((a,), (b,)), ((), ())), preferred_element_...  50.4 us
    pallas_call x1, Pallas kernels, attention(): pl.pallas_call(functools.partial(attention_body, step), out_shape=[shape]...  24.6 us
    convert_element_type x4, other arithmetic, paired(): g.reshape(shard.shape).astype(F32)  10.8 us
  transfers between devices with their start and end apart: 5, of which 2 were waited for; matrix products, arithmetic and copies ran while one was open for 5% of the time, Pallas kernels for 0%

profile of v5, /device:TPU:9, one launch (start us, length us, event | category | flops | bytes accessed | tf_op | source)
XLA Modules:
  0.0 394.7 jit_solution(13156258218339660607)
XLA Ops:
  7.5 105.8 %gather.1 = (bf16[4,4,2,32,1536]{4,3,2,1,0:T(8,128)(2,1)}, bf16[4,4,2,16,1024]{4,3,2,1,0:T(8,128)(2,1)}, bf16[4,4,2,32,2048]{4,3,2,1,0:T(8,128)(2,1)}, bf16[4,4,...) custom-call(bf16[4,2,32,3072]{3,2,1,0:T(8,128)(2,1)} %bitcast.82, ...), custom_call_target="tpu_custom_call" | custom-call | tf_op jit(solution)/shard_map/gather/pallas_call | solution.py:263
  113.4 1.5 convert_reduce_fusion.1
  114.8 1.6 fusion.11
  117.6 1.7 fusion.8
  119.3 3.3 collective-permute-start
  122.9 2.1 collective-permute-done.1
  126.3 9.0 %convolution_add_fusion.q_ref.k_ref.v_ref = f32[1536,1024]{1,0:T(8,128)} fusion(bf16[1024,1536]{1,0:T(8,128)(2,1)} %bitcast.78, f32[1536]{0:T(1024)S(1)} %add.125, bf16[512,1024]{1,0:T(8,128)(2,1)S(1)} %collective-permute-done, bf16[512,1024]{1,0:T(8,128)(2,1)S(1)} %fusion.8), kind=kOutput, calls=%fused_computation.10 | convolution fusion | flops 3226992640 | bytes 11540480 | tf_op jit(solution)/shard_map/dot_general | solution.py:751
  135.3 24.6 %attention.1 = (bf16[512,1024]{1,0:T(8,128)(2,1)}, bf16[512,1024]{1,0:T(8,128)(2,1)}, bf16[512,1024]{1,0:T(8,128)(2,1)}, bf16[512,1024]{1,0:T(8,128)(2,1)}, f32[8,1,1024]{2,1,0:T(1,128)}) custom-call(f32[1536,1024]{1,0:T(8,128)} %convolution_add_fusion.q_ref.k_ref.v_ref, f32[1536,1024]{1,0:T(8,128)} %convolution_add_fusion.q_ref.k_ref.v_ref, ...), custom_call_target="tpu_custom_call" | custom-call | flops 2147483648 | bytes 12582912 | tf_op jit(solution)/shard_map/attention/pallas_call | solution.py:727
  159.9 2.6 fusion.28
  163.1 2.3 collective-permute-done.2
  166.4 1.4 add_convert_fusion
  168.3 2.9 pad_maximum_fusion.refs_10_
  171.2 7.7 %multiply_convert_fusion.1 = (bf16[1024,2048]{1,0:T(8,128)(2,1)S(1)}, f32[1024,2048]{1,0:T(8,128)S(1)}) fusion(f32[2048]{0:T(1024)S(1)} %bitcast.98, bf16[1024,2048]{1,0:T(8,128)(2,1)S(1)} %bitcast.73, bf16[512,1024]{1,0:T(8,128)(2,1)} %collective-permute-done.3, bf16[512,1024]{1,0:T(8,128)(2,1)} %add_convert_fusion), kind=kOutput, calls=%fused_computation.8 | convolution fusion | flops 4311744512 | bytes 18882560 | tf_op jit(solution)/shard_map/dot_general | solution.py:751
  178.9 4.5 %fusion.29 = f32[1024,1024]{1,0:T(8,128)S(1)} fusion(bf16[1024,2048]{1,0:T(8,128)(2,1)S(1)} %get-tuple-element.82, bf16[2048,1024]{1,0:T(8,128)(2,1)S(1)} %bitcast.109), kind=kOutput, calls=%fused_computation.91 | convolution fusion | flops 4294967296 | bytes 12582912 | tf_op jit(solution)/shard_map/dot_general | solution.py:751
  184.6 1.8 fusion.12.refs_14_
  186.4 7.7 %convolution_convert_fusion.1 = bf16[2048,1024]{1,0:T(8,128)(2,1)} fusion(bf16[1024,2048]{1,0:T(8,128)(2,1)S(1)} %get-tuple-element.82, bf16[512,1024]{1,0:T(8,128)(2,1)} %collective-permute-done.4, bf16[512,1024]{1,0:T(8,128)(2,1)} %bitcast.21), kind=kOutput, calls=%fused_computation.12 | convolution fusion | flops 4301258752 | bytes 10485760 | tf_op jit(solution)/shard_map/dot_general | solution.py:751
  194.1 9.5 %convert_reduce_fusion = (f32[2048]{0:T(1024)}, bf16[1024,2048]{1,0:T(8,128)(2,1)S(1)}) fusion(f32[1024,2048]{1,0:T(8,128)S(1)} %get-tuple-element.83, f32[2048]{0:T(1024)S(1)} %bitcast.99, bf16[2048,1024]{1,0:T(8,128)(2,1)S(1)} %bitcast.110, bf16[512,1024]{1,0:T(8,128)(2,1)} %collective-permute-done.4, bf16[512,1024]{1,0:T(8,128)(2,1)} %bitcast.21), kind=kOutput, calls=%fused_computation.6 | convolution fusion | flops 4330616832 | bytes 18890752 | tf_op jit(solution)/shard_map/dot_general | solution.py:751
  203.7 9.3 %convolution_convert_fusion = bf16[1024,2048]{1,0:T(8,128)(2,1)} fusion(bf16[1024,2048]{1,0:T(8,128)(2,1)S(1)} %get-tuple-element.85.refs_2_, bf16[512,1024]{1,0:T(8,128)(2,1)} %collective-permute-done.3, bf16[512,1024]{1,0:T(8,128)(2,1)} %add_convert_fusion), kind=kOutput, calls=%fused_computation.11 | convolution fusion | flops 4301258752 | bytes 10485760 | tf_op jit(solution)/shard_map/dot_general | solution.py:751
  212.9 164.5 %backward.1 = (bf16[4,2,32,3072]{3,2,1,0:T(8,128)(2,1)}, bf16[2,4,2,16,1024]{4,3,2,1,0:T(8,128)(2,1)}, bf16[4,2,32,4096]{3,2,1,0:T(8,128)(2,1)}, bf16[2,4,2,64,1...) custom-call(bf16[4,2,2,2,64,1024]{5,4,3,2,1,0:T(8,128)(2,1)} %bitcast., ...), custom_call_target="tpu_custom_call" | custom-call | tf_op jit(solution)/shard_map/backward/pallas_call | solution.py:686
  379.0 1.5 fusion.27
  381.7 2.1 bitcast_convert_fusion.3
  383.8 3.4 bitcast_convert_fusion.2
  387.3 2.6 bitcast_convert_fusion.1
  389.9 2.6 bitcast_convert_fusion
  (87 shorter events, 17.4 us)
Async XLA Ops:
  113.3 9.3 %copy-start.15 = (f32[2,8,256]{2,1,0:T(8,128)S(1)}, f32[2,8,256]{2,1,0:T(8,128)}, u32[]{:S(2)}) copy-start(f32[2,8,256]{2,1,0:T(8,128)} %get-tuple-element.37) | copy-start | bytes 49156
  113.4 9.4 %copy-start.12 = (f32[4,16,256]{2,1,0:T(8,128)S(1)}, f32[4,16,256]{2,1,0:T(8,128)}, u32[]{:S(2)}) copy-start(f32[4,16,256]{2,1,0:T(8,128)} %get-tuple-element.36) | copy-start | bytes 196612
  117.6 17.6 %copy-start.14 = (f32[4,1,256]{2,1,0:T(1,128)}, f32[4,1,256]{2,1,0:T(1,128)S(1)}, u32[]{:S(2)}) copy-start(f32[4,1,256]{2,1,0:T(1,128)S(1)} %get-tuple-element.61) | copy-start | bytes 12292
  117.6 48.7 %copy-start.13 = (f32[4,1,256]{2,1,0:T(1,128)}, f32[4,1,256]{2,1,0:T(1,128)S(1)}, u32[]{:S(2)}) copy-start(f32[4,1,256]{2,1,0:T(1,128)S(1)} %get-tuple-element.58) | copy-start | bytes 12292
  119.3 15.9 %copy-start.4 = (bf16[512,1024]{1,0:T(8,128)(2,1)}, bf16[512,1024]{1,0:T(8,128)(2,1)S(1)}, u32[]{:S(2)}) copy-start(bf16[512,1024]{1,0:T(8,128)(2,1)S(1)} %fusion.8) | copy-start | bytes 3145732
  119.3 6.9 %collective-permute-start = (bf16[512,1024]{1,0:T(8,128)(2,1)S(1)}, bf16[512,1024]{1,0:T(8,128)(2,1)S(1)}, u32[]{:S(2)}, u32[]{:S(2)}) collective-permute-start(bf16[512,1024]{1,0:T(8,128)(2,1)S(1)} %fusion.8), channel_id=1, source_target_pairs={{0,4},{4,0},{1,5},{5,1},{2,6},{6,2},{3,7},{7,3},{8,12},{12,8},{9,1... | collective-permute-start | bytes 3145736 | tf_op jit(solution)/shard_map/ppermute | solution.py:743
  122.7 2.3 collective-permute-start.1
  126.3 9.0 %copy-start.11 = (bf16[512,1024]{1,0:T(8,128)(2,1)}, bf16[512,1024]{1,0:T(8,128)(2,1)S(1)}, u32[]{:S(2)}) copy-start(bf16[512,1024]{1,0:T(8,128)(2,1)S(1)} %collective-permute-done) | copy-start | bytes 3145732
  135.3 24.7 %copy-start.6 = (bf16[4,4,2,16,1024]{4,3,2,1,0:T(8,128)(2,1)S(1)}, bf16[4,4,2,16,1024]{4,3,2,1,0:T(8,128)(2,1)}, u32[]{:S(2)}) copy-start(bf16[4,4,2,16,1024]{4,3,2,1,0:T(8,128)(2,1)} %get-tuple-element.39) | copy-start | bytes 3145732
  159.9 5.5 %copy-start.1 = (bf16[2,256,1024]{2,1,0:T(8,128)(2,1)S(1)}, bf16[2,256,1024]{2,1,0:T(8,128)(2,1)}, u32[]{:S(2)}) copy-start(bf16[2,256,1024]{2,1,0:T(8,128)(2,1)} %get-tuple-element.34) | copy-start | bytes 3145732
  162.7 2.7 collective-permute-start.2
  166.0 18.6 %copy-start = (f32[512,1024]{1,0:T(8,128)}, f32[512,1024]{1,0:T(8,128)S(1)}, u32[]{:S(2)}) copy-start(f32[512,1024]{1,0:T(8,128)S(1)} %get-tuple-element.55.refs_11_) | copy-start | bytes 6291460
  166.0 2.3 copy-start.5
  167.7 3.5 collective-permute-start.3
  168.1 18.3 %collective-permute-start.4 = (bf16[512,1024]{1,0:T(8,128)(2,1)}, bf16[512,1024]{1,0:T(8,128)(2,1)}, u32[]{:S(2)}, u32[]{:S(2)}) collective-permute-start(bf16[512,1024]{1,0:T(8,128)(2,1)} %bitcast.21), channel_id=1, source_target_pairs={{0,4},{4,0},{1,5},{5,1},{2,6},{6,2},{3,7},{7,3},{8,12},{12,8},{9,1... | collective-permute-start | bytes 3145736 | tf_op jit(solution)/shard_map/ppermute | solution.py:743
  168.3 2.9 copy-start.2
  171.2 7.7 %copy-start.16 = (bf16[4,4,2,64,1024]{4,3,2,1,0:T(8,128)(2,1)S(1)}, bf16[4,4,2,64,1024]{4,3,2,1,0:T(8,128)(2,1)}, u32[]{:S(2)}) copy-start(bf16[4,4,2,64,1024]{4,3,2,1,0:T(8,128)(2,1)} %get-tuple-element.42) | copy-start | bytes 12582916
  203.7 9.3 %copy-start.3 = (bf16[1024,2048]{1,0:T(8,128)(2,1)}, bf16[1024,2048]{1,0:T(8,128)(2,1)S(1)}, u32[]{:S(2)}) copy-start(bf16[1024,2048]{1,0:T(8,128)(2,1)S(1)} %get-tuple-element.85.refs_2_) | copy-start | bytes 12582916
  377.4 9.8 %copy-start.8 = (bf16[4,2,32,4096]{3,2,1,0:T(8,128)(2,1)S(1)}, bf16[4,2,32,4096]{3,2,1,0:T(8,128)(2,1)}, u32[]{:S(2)}) copy-start(bf16[4,2,32,4096]{3,2,1,0:T(8,128)(2,1)} %get-tuple-element.52) | copy-start | bytes 6291460
  387.2 2.7 copy-start.7
  389.9 2.6 copy-start.10
  389.9 3.6 copy-start.9

commit v6 on v5

--- a/solution.py
+++ b/solution.py
@@ -79,7 +79,7 @@
                         (p, tc, tz),
                     ).start()
 
-    def finish():
+    def sent():
         for n, (src, dst) in enumerate(zip(refs, outs)):
             for i in range(clips):
 
@@ -89,10 +89,36 @@
                         src.at[i], dst.at[slot], send.at[n, i], recv.at[n, slot], (p, c ^ 1, z)
                     ).wait_send()
 
+    def arrive():
+        for n, (src, dst) in enumerate(zip(refs, outs)):
             for m in range(clips):
                 pltpu.make_async_copy(src.at[0], dst.at[m], recv.at[n, m]).wait()
 
-    return start, finish
+    def finish():
+        sent()
+        arrive()
+
+    return start, finish, sent, arrive
+
+
+def turn(u, cosine, sine):
+    half = HEAD // 2
+    first, second = u[:half], u[half:]
+    return jnp.concatenate(
+        [first * cosine - second * sine, first * sine + second * cosine], axis=0
+    )
+
+
+def dot(a, b):
+    return jnp.dot(a, b, preferred_element_type=F32)
+
+
+def dot_t(a, b):
+    return lax.dot_general(a, b, (((1,), (1,)), ((), ())), preferred_element_type=F32)
+
+
+def tile(i, size):
+    return pl.ds(pl.multiple_of(i * size, size), size)
 
 
 def cuts(whole, half, c, blocks):
@@ -108,15 +134,19 @@
     ]
 
 
-def gather_body(groups, clips, blocks, *refs):
+def forward_body(groups, clips, blocks, *refs):
     count = len(blocks)
-    raw, (small, x, pos, dy) = refs[:count], refs[count : count + 4]
-    outs = refs[count + 4 : 2 * count + 4]
-    small_o, x_o, pos_o, dy_o = refs[2 * count + 4 : 2 * count + 8]
-    halves = refs[2 * count + 8 : 3 * count + 8]
-    zs, zr, xs, xr, ys, yr, fs, fr, hs, ls, ss, sr, ts, tr, us, ur, vs, vr = refs[
-        3 * count + 8 :
+    raw, (small, x, tab, dy) = refs[:count], refs[count : count + 4]
+    (wq_o, *outs) = refs[count + 4 : 2 * count + 4]
+    (small_o, x_o, tab_o, dy_o, h1_o, qs_o, kr_o, vb_o, mix_o, lse_o) = refs[2 * count + 4 : 2 * count + 14]
+    halves = refs[2 * count + 14 : 3 * count + 14]
+    (wq_v, small_v, x_v, tab_v, tab_w, h1, qs, kr, vb, mix, qkv, gain, bias) = refs[
+        3 * count + 14 : 3 * count + 27
     ]
+    (zs, zr, xs, xr, ys, yr, fs, fr, hs, ls, ss, sr, ts, tr, us, ur, vs, vr, es, er, ks) = refs[
+        3 * count + 27 :
+    ]
+    outs = [wq_v, *outs]
     p, c, z = where_am_i()
     for w in range(count):
         for src, dst in cuts(raw[w], halves[w], c, blocks[w]):
@@ -124,17 +154,17 @@
     enter(p, c, z, groups)
     col = [(p, c, lax.rem(z + k, groups)) for k in range(groups)]
     org = [lax.rem(z + groups - k, groups) for k in range(groups)]
-    xn, yn = (p ^ 1, c, z), (p ^ 2, c, z)
-    start_pos, finish_pos = move_tokens((pos,), (pos_o,), vs, vr, p, c, z, clips)
-    start_x, finish_x = move_tokens((x,), (x_o,), ts, tr, p, c, z, clips)
+    xn, yn, cn = (p ^ 1, c, z), (p ^ 2, c, z), (p, c ^ 1, z)
     smalls = [
-        remote(small, small_o.at[z], ss.at[k], sr.at[k], col[k]) for k in range(1, groups)
+        remote(small, small_v.at[z], ss.at[k], sr.at[k], col[k]) for k in range(1, groups)
     ]
     for s in smalls:
         s.start()
-    keep = [pltpu.make_async_copy(small, small_o.at[z], ls.at[count])]
+    keep = [pltpu.make_async_copy(small, small_v.at[z], ls.at[count])]
     keep[0].start()
-    start_dy, finish_dy = move_tokens((dy,), (dy_o,), us, ur, p, c, z, clips)
+    start_tab, _, sent_tab, arrive_tab = move_tokens((tab,), (tab_v,), vs, vr, p, c, z, clips)
+    start_x, _, sent_x, arrive_x = move_tokens((x,), (x_v,), ts, tr, p, c, z, clips)
+    start_dy, finish_dy, *_ = move_tokens((dy,), (dy_o,), us, ur, p, c, z, clips)
     units = [(w, d, side) for w in range(count) for d in range(1, groups) for side in range(2)]
 
     def origin(d, side):
@@ -203,7 +233,7 @@
             along(p ^ 2).wait_recv()
             second(p ^ 2).start()
 
-    def settle(u):
+    def complete(u):
         w, d, side = u
         o, across, along, first, second = links(u)
 
@@ -211,6 +241,13 @@
         def _():
             first(p ^ 3).wait_recv()
             second(p ^ 3).wait_recv()
+
+    def settle(u):
+        w, d, side = u
+        o, across, along, first, second = links(u)
+
+        @pl.when(arrives(d, side))
+        def _():
             across(p).wait_send()
             along(p).wait_send()
             first(p).wait_send()
@@ -221,12 +258,13 @@
             hop(w, d, side, halves[w].at[p]).wait_send()
 
     own(0)
-    start_pos(0, 1)
+    start_tab(0, 1)
     own(1)
     moves = {2 * k: (start_x, k) for k in range(4)}
     moves.update({10 + 3 * k: (start_dy, k) for k in range(4)})
     lag = 3
-    for n in range(len(units) + lag):
+
+    def step(n):
         if n < len(units):
             plane(units[n])
             w, d, side = units[n]
@@ -236,16 +274,124 @@
                 moves[n][0](moves[n][1], 4)
         if n >= lag:
             forward(units[n - lag])
+
+    steps = list(range(len(units) + lag))
+    early = 2 * (groups - 1) + lag
+    for _ in range(early):
+        step(steps.pop(0))
+    for k in range(1, groups):
+        remote(small, small_v.at[org[k]], ss.at[k], sr.at[k], col[k]).wait_recv()
+    keep[0].wait()
+    row = small_v.shape[2]
+    half = row // 2
+    mine = pl.ds(pl.multiple_of(c * half, half), half)
+    for g in range(groups):
+        gain[0:2, g * row : (g + 1) * row] = small_v[g, 0:2]
+        for r in range(3):
+            bias[3 * g + r : 3 * g + r + 1] = small_v[g, 6 + r : 7 + r, mine]
+    small_o[...] = small_v[...]
+    own_count = h1.shape[0] // 2
+    arrive_x()
+    saves = [pltpu.make_async_copy(x_v, x_o, ks.at[0])]
+    saves[0].start()
+
+    def norm(i, carry):
+        per = own_count // clips // 128
+        v = x_v[lax.div(i, per), tile(lax.rem(i, per), 128)].astype(F32)
+        v = v - jnp.mean(v, axis=1, keepdims=True)
+        v = v * lax.rsqrt(jnp.mean(v * v, axis=1, keepdims=True) + EPS)
+        h1[tile(i, 128)] = (v * gain[0:1] + gain[1:2]).astype(BF)
+        return carry
+
+    lax.fori_loop(0, own_count // 128, norm, 0)
+    swap = remote(h1.at[:own_count], h1.at[own_count:], es.at[0], er.at[0], cn)
+    swap.start()
+    arrive_tab()
+    swap_tab = remote(tab_v, tab_w, es.at[1], er.at[1], cn)
+    swap_tab.start()
+    step(steps.pop(0))
+    swap_tab.wait()
+    part = tab_v.shape[2]
+    for m in range(clips):
+        tab_o[:, m * part : (m + 1) * part] = tab_v[m]
+        tab_o[:, own_count + m * part : own_count + (m + 1) * part] = tab_w[m]
+    for u in units[: 2 * (groups - 1)]:
+        complete(u)
+    keep[1].wait()
+    saves.append(pltpu.make_async_copy(wq_v, wq_o, ks.at[1]))
+    saves[1].start()
+    swap.wait()
+    saves.append(pltpu.make_async_copy(h1, h1_o, ks.at[2]))
+    saves[2].start()
+    inner = qs.shape[0]
+    heads = inner // HEAD
+    pairs = heads // 2
+
+    def head(h, side):
+        rows, place = tile(h, HEAD), tile(side, HEAD)
+        co, si = tab_o[: HEAD // 2], tab_o[HEAD // 2 :]
+        k = turn(qkv[1, place], co, si).astype(BF)
+        v = qkv[2, place].astype(BF)
+        q = (turn(qkv[0, place], co, si).astype(BF).astype(F32) * SCALE).astype(BF)
+        kr[rows] = k
+        vb[rows] = v
+        qs[rows] = q
+        keys = k.T
+        size = 256
+        for i in range(0, 2 * own_count, size):
+            scores = dot(keys, q[:, i : i + size])
+            top = jnp.max(scores, axis=0, keepdims=True)
+            e = jnp.exp(scores - top)
+            total = jnp.sum(e, axis=0, keepdims=True)
+            mixed = dot(v, e.astype(BF))
+            mix[rows, i : i + size] = (mixed / total).astype(BF)
+            lse_o[h, :, i : i + size] = top + jnp.log(total)
+
+    during = [steps.pop(0) for _ in range(heads + heads // 2)]
+
+    def two_heads(i, carry):
+        def project(n, carry):
+            at = pl.ds(pl.multiple_of(n * inner + i * 2 * HEAD, 2 * HEAD), 2 * HEAD)
+            w = wq_v[..., at].reshape(h1.shape[1], 2 * HEAD)
+            qkv[n] = (dot(h1[...], w) + bias[pl.ds(n * pairs + i, 1)]).T
+            return carry
+
+        lax.fori_loop(0, 3, project, 0)
+        for n in range(pairs):
+
+            @pl.when(i == n)
+            def _():
+                step(during[3 * n])
+
+        def one(side, carry):
+            head(2 * i + side, side)
+            for n in range(heads):
+
+                @pl.when(2 * i + side == n)
+                def _():
+                    step(during[3 * (n // 2) + 1 + n % 2])
+
+            return carry
+
+        lax.fori_loop(0, 2, one, 0)
+        return carry
+
+    lax.fori_loop(0, pairs, two_heads, 0)
+    for n, (a, b) in enumerate(((qs, qs_o), (kr, kr_o), (vb, vb_o), (mix, mix_o))):
+        saves.append(pltpu.make_async_copy(a, b, ks.at[3 + n]))
+        saves[-1].start()
+    while steps:
+        step(steps.pop(0))
+    for u in units[2 * (groups - 1) :]:
+        complete(u)
     for u in units:
         settle(u)
-    for k in range(1, groups):
-        remote(small, small_o.at[org[k]], ss.at[k], sr.at[k], col[k]).wait_recv()
     for s in smalls:
         s.wait_send()
-    for k in keep:
+    for k in keep[2:] + saves:
         k.wait()
-    finish_pos()
-    finish_x()
+    sent_tab()
+    sent_x()
     finish_dy()
 
 
@@ -253,46 +399,40 @@
     return raw.shape[1:] if blocks == 0 else raw.shape[:3] + (raw.shape[3] // 2,)
 
 
-def gather(raw, blocks, small, x, pos, dy, groups):
+def forward(raw, blocks, small, x, tab, dy, groups):
     count, clips = len(raw), x.shape[0]
+    own, width = clips * x.shape[1], x.shape[2]
+    halves = [half_shape(r, b) for r, b in zip(raw, blocks)]
+    inner = halves[0][-1] // 3
     dma = pltpu.SemaphoreType.DMA
-    halves = [half_shape(r, b) for r, b in zip(raw, blocks)]
-    shapes = [jax.ShapeDtypeStruct((groups,) + h, BF) for h in halves]
-    shapes += [jax.ShapeDtypeStruct((groups,) + small.shape, small.dtype)]
-    shapes += [jax.ShapeDtypeStruct(v.shape, v.dtype) for v in (x, pos, dy)]
+    of = jax.ShapeDtypeStruct
+    feature = (inner, 2 * own)
+    shapes = [of((groups,) + h, BF) for h in halves]
+    shapes += [of((groups,) + small.shape, F32), of(x.shape, BF), of((HEAD, 2 * own), F32)]
+    shapes += [of(x.shape, BF), of((2 * own, width), BF)] + [of(feature, BF)] * 4
+    shapes += [of((inner // HEAD, 1, 2 * own), F32)]
+    vm = pltpu.VMEM
+    scratch = [vm(h, BF) for h in halves]
+    scratch += [vm((groups,) + halves[0], BF), vm((groups,) + small.shape, F32), vm(x.shape, BF)]
+    scratch += [vm(tab.shape, F32)] * 2 + [vm((2 * own, width), BF)] + [vm(feature, BF)] * 4
+    scratch += [vm((3, 2 * HEAD, 2 * own), F32), vm((8, width), F32)]
+    scratch += [vm((3 * groups + -3 * groups % 8, width // groups // 2), F32)]
     return pl.pallas_call(
-        functools.partial(gather_body, groups, clips, blocks),
+        functools.partial(forward_body, groups, clips, blocks),
         out_shape=shapes,
         in_specs=[ANY] * count + [VM, ANY, ANY, ANY],
-        out_specs=[ANY] * len(shapes),
-        scratch_shapes=[pltpu.VMEM(h, BF) for h in halves]
+        out_specs=[ANY] * count + [VM, ANY, VM] + [ANY] * 6 + [VM],
+        scratch_shapes=scratch
         + [dma((count, 2, groups))] * 6
         + [dma((count, 2, groups, 2))] * 2
         + [dma((count,)), dma((count + 1,)), dma((groups,)), dma((groups,))]
-        + [dma((1, clips))] * 6,
-        compiler_params=pltpu.CompilerParams(collective_id=0, has_side_effects=True),
-        name="gather",
-    )(*raw, small, x, pos, dy)
-
-
-def turn(u, cosine, sine):
-    half = HEAD // 2
-    first, second = u[:half], u[half:]
-    return jnp.concatenate(
-        [first * cosine - second * sine, first * sine + second * cosine], axis=0
-    )
-
-
-def dot(a, b):
-    return jnp.dot(a, b, preferred_element_type=F32)
-
-
-def dot_t(a, b):
-    return lax.dot_general(a, b, (((1,), (1,)), ((), ())), preferred_element_type=F32)
-
-
-def tile(i, size):
-    return pl.ds(pl.multiple_of(i * size, size), size)
+        + [dma((1, clips))] * 6
+        + [dma((2,)), dma((2,)), dma((7,))],
+        compiler_params=pltpu.CompilerParams(
+            collective_id=0, has_side_effects=True, vmem_limit_bytes=60 * 1024 * 1024
+        ),
+        name="forward",
+    )(*raw, small, x, tab, dy)
 
 
 def backward_body(groups, clips, blocks, *refs):
@@ -483,7 +623,7 @@
         return carry
 
     lax.fori_loop(0, own // 128, last_add, 0)
-    y_start, y_finish = move_tokens((gx,), (y_o,), us, ur, p, c, z, clips)
+    y_start, y_finish, *_ = move_tokens((gx,), (y_o,), us, ur, p, c, z, clips)
     y_start(0, 2)
     y_start(1, 2)
     for copy in loads[2:]:
@@ -583,7 +723,7 @@
         return carry
 
     lax.fori_loop(0, own // 128, first_norm, 0)
-    start, finish = move_tokens((gx,), (gx_o,), ts, tr, p, c, z, clips)
+    start, finish, *_ = move_tokens((gx,), (gx_o,), ts, tr, p, c, z, clips)
     start(0, 4)
     tick()
     small_s[...] = jnp.zeros_like(small_s)
@@ -696,49 +836,6 @@
     )(gw2, gw1, *arrays, *tables)
 
 
-def attention_body(step, q_ref, k_ref, v_ref, cos_ref, sin_ref, qs_ref, kr_ref, vb_ref, o_ref, l_ref):
-    cosine, sine = cos_ref[...], sin_ref[...]
-    length = cosine.shape[1]
-    kr = turn(k_ref[...], cosine, sine).astype(BF)
-    vb = v_ref[...].astype(BF)
-    qs = (turn(q_ref[...], cosine, sine).astype(BF).astype(F32) * SCALE).astype(BF)
-    kr_ref[...] = kr
-    vb_ref[...] = vb
-    qs_ref[...] = qs
-    keys = kr.T
-    for i in range(0, length, step):
-        scores = dot(keys, qs[:, i : i + step])
-        top = jnp.max(scores, axis=0, keepdims=True)
-        e = jnp.exp(scores - top)
-        total = jnp.sum(e, axis=0, keepdims=True)
-        mixed = dot(vb, e.astype(BF))
-        o_ref[:, i : i + step] = (mixed / total).astype(BF)
-        l_ref[0, :, i : i + step] = top + jnp.log(total)
-
-
-def attention(qkv, cosine, sine, step=256):
-    rows, length = qkv.shape
-    width = rows // 3
-    heads = width // HEAD
-    block = [pl.BlockSpec((HEAD, length), lambda h, n=n: (n * heads + h, 0)) for n in range(3)]
-    table = pl.BlockSpec((HEAD // 2, length), lambda h: (0, 0))
-    out = pl.BlockSpec((HEAD, length), lambda h: (h, 0))
-    shape = jax.ShapeDtypeStruct((width, length), BF)
-    return pl.pallas_call(
-        functools.partial(attention_body, step),
-        out_shape=[shape] * 4 + [jax.ShapeDtypeStruct((heads, 1, length), F32)],
-        grid=(heads,),
-        in_specs=block + [table, table],
-        out_specs=[out] * 4 + [pl.BlockSpec((1, 1, length), lambda h: (h, 0, 0))],
-        cost_estimate=pl.CostEstimate(
-            flops=4 * width * length * length,
-            transcendentals=heads * length * length,
-            bytes_accessed=width * length * 24,
-        ),
-        name="attention",
-    )(qkv, qkv, qkv, cosine, sine)
-
-
 def swap(value):
     return lax.ppermute(value, "core", [(0, 1), (1, 0)])
 
@@ -800,36 +897,30 @@
     small = jnp.zeros(place.shape, F32)
     for n, v in enumerate(vectors):
         small = jnp.where(place == n, v.astype(F32)[None, :], small)
-    pos = jnp.pad(jnp.moveaxis(positions, 0, 1).astype(F32), ((0, 0), (0, 5), (0, 0)))
-    wq, wo, w1, w2, small, x, pos, dy = gather(raw, blocks, small, tokens, pos, cotangent, groups)
+    pair = jnp.arange(HEAD // 2)
+    band = (pair >= 10).astype(jnp.int32) + (pair >= 21).astype(jnp.int32)
+    begin = jnp.where(band == 0, 0, jnp.where(band == 1, 10, 21))
+    number = jnp.where(band == 0, 10, 11)
+    freq = jnp.power(F32(10000.0), -(pair - begin).astype(F32) / number.astype(F32))
+    pos = positions.astype(F32)[:, :, None, :]
+    band = band[None, :, None]
+    chosen = jnp.where(band == 0, pos[0], jnp.where(band == 1, pos[1], pos[2]))
+    angles = chosen * freq[None, :, None]
+    tab = jnp.concatenate([jnp.cos(angles), jnp.sin(angles)], axis=1)
+    wq, wo, w1, w2, small, x, tab, dy, h1, qs, kr, vb, mixed, lse = forward(
+        raw, blocks, small, tokens, tab, cotangent, groups
+    )
+    cosine, sine = tab[: HEAD // 2], tab[HEAD // 2 :]
     wq = wq.reshape(width, 3 * wide)
     wo = wo.reshape(wide, width)
     w1 = w1.reshape(width, deep)
     w2 = w2.reshape(deep, width)
     g1, b1, bo, g2, b2, bd = (small[:, n].reshape(1, width) for n in range(6))
-    bq_own = pick(small[:, 6 : 6 + bq].reshape(3, groups, 2, row // 2), 2).reshape(3 * wide, 1)
     bu_own = pick(small[:, 6 + bq : lines].reshape(groups, 2, deep // groups), 1).reshape(1, deep)
-
     grad_out = dy.reshape(own, width)
     grad_all = both(grad_out)
-
-    pos = jnp.moveaxis(pos[:, :3], 1, 0).reshape(3, own)
-    pos = jnp.concatenate([pos, swap(pos)], axis=1)
-    pair = jnp.arange(HEAD // 2)
-    band = (pair >= 10).astype(jnp.int32) + (pair >= 21).astype(jnp.int32)
-    begin = jnp.where(band == 0, 0, jnp.where(band == 1, 10, 21))
-    count = jnp.where(band == 0, 10, 11)
-    freq = jnp.power(F32(10000.0), -(pair - begin).astype(F32) / count.astype(F32))
-    band = band[:, None]
-    chosen = jnp.where(band == 0, pos[0:1], jnp.where(band == 1, pos[1:2], pos[2:3]))
-    angles = chosen * freq[:, None]
-    cosine, sine = jnp.cos(angles), jnp.sin(angles)
-
     tokens = x.reshape(own, width)
     x = tokens.astype(F32)
-    h1 = both((normalize(x)[0] * g1 + b1).astype(BF))
-    qkv = contract(wq, h1, 0, 1) + bq_own
-    qs, kr, vb, mixed, lse = attention(qkv, cosine, sine)
     x2 = x + own_sum(contract(mixed, wo, 0, 0)) + bo
     h2 = both((normalize(x2)[0] * g2 + b2).astype(BF))
     u = contract(h2, w1, 1, 0) + bu_own

time: 400 us -> 368 us (0.920)
  Pallas kernels: 295 us -> 285 us
  matrix products: 50.4 us -> 41.3 us
  other arithmetic: 30.1 us -> 22.1 us
    pallas_call x2 -> x1, Pallas kernels: 130 us -> 121 us  [forward(): pl.pallas_call(functools.partial(forward_body, groups, clips, blocks), ou...]
    dot_general x7 -> x6, matrix products: 50.4 us -> 41.3 us  [contract(): lax.dot_general(left, right, (((a,), (b,)), ((), ())), preferred_element_...]
  transfers between devices with their start and end apart: 5 -> 3, of which waited for: 2 -> 2; matrix products, arithmetic and copies ran while one was open for 5% -> 5% of each run, Pallas kernels for 0% -> 0%
where the time goes in v6:
time: 368 us; the launch traced here: 364 us
  Pallas kernels  285 us (77%)
  matrix products  41.3 us (11%)
  other arithmetic  22.1 us (6%)
  local copies, waits for them, and re-layouts  8.91 us (2%)
    pallas_call x1, Pallas kernels, backward(): pl.pallas_call(functools.partial(backward_body, groups, clips, blocks), o...  164 us
    pallas_call x1, Pallas kernels, forward(): pl.pallas_call(functools.partial(forward_body, groups, clips, blocks), ou...  121 us
    dot_general x6, matrix products, contract(): lax.dot_general(left, right, (((a,), (b,)), ((), ())), preferred_element_...  41.3 us
    convert_element_type x4, other arithmetic, paired(): g.reshape(shard.shape).astype(F32)  10.8 us
  transfers between devices with their start and end apart: 3, of which 2 were waited for; matrix products, arithmetic and copies ran while one was open for 5% of the time, Pallas kernels for 0%

profile of v6, /device:TPU:9, one launch (start us, length us, event | category | flops | bytes accessed | tf_op | source)
XLA Modules:
  0.0 364.0 jit_solution(10276895429276183284)
XLA Ops:
  5.4 0.8 slice_convert_fusion.4
  7.9 121.4 %forward.1 = (bf16[4,4,2,32,1536]{4,3,2,1,0:T(8,128)(2,1)}, bf16[4,4,2,16,1024]{4,3,2,1,0:T(8,128)(2,1)}, bf16[4,4,2,32,2048]{4,3,2,1,0:T(8,128)(2,1)}, bf16[4,4...) custom-call(bf16[4,2,32,3072]{3,2,1,0:T(8,128)(2,1)} %bitcast.67, ...), custom_call_target="tpu_custom_call" | custom-call | tf_op jit(solution)/shard_map/forward/pallas_call | solution.py:420
  129.3 2.9 fusion.22
  132.4 1.4 collective-permute-start
  134.4 1.7 collective-permute-done
  137.0 1.4 add_convert_fusion
  139.0 0.7 fusion.19
  139.8 1.6 collective-permute-done.1
  141.4 8.1 %multiply_convert_fusion.1 = (bf16[1024,2048]{1,0:T(8,128)(2,1)S(1)}, f32[1024,2048]{1,0:T(8,128)S(1)}) fusion(f32[2048]{0:T(1024)S(1)} %bitcast.79, bf16[1024,2048]{1,0:T(8,128)(2,1)} %bitcast.57, bf16[512,1024]{1,0:T(8,128)(2,1)} %collective-permute-done.1, bf16[512,1024]{1,0:T(8,128)(2,1)} %add_convert_fusion), kind=kOutput, calls=%fused_computation.8 | convolution fusion | flops 4311744512 | bytes 18882560 | tf_op jit(solution)/shard_map/dot_general | solution.py:848
  149.5 4.5 %fusion.23 = f32[1024,1024]{1,0:T(8,128)S(1)} fusion(bf16[1024,2048]{1,0:T(8,128)(2,1)S(1)} %get-tuple-element.83, bf16[2048,1024]{1,0:T(8,128)(2,1)S(1)} %bitcast.88), kind=kOutput, calls=%fused_computation.76 | convolution fusion | flops 4294967296 | bytes 12582912 | tf_op jit(solution)/shard_map/dot_general | solution.py:848
  154.0 1.1 slice.153.refs_15_
  155.2 1.8 fusion.5.refs_14_
  156.9 7.7 %convolution_convert_fusion.1 = bf16[2048,1024]{1,0:T(8,128)(2,1)} fusion(bf16[1024,2048]{1,0:T(8,128)(2,1)S(1)} %get-tuple-element.83, bf16[512,1024]{1,0:T(8,128)(2,1)} %collective-permute-done.2, bf16[512,1024]{1,0:T(8,128)(2,1)S(1)} %bitcast.69), kind=kOutput, calls=%fused_computation.11 | convolution fusion | flops 4301258752 | bytes 10485760 | tf_op jit(solution)/shard_map/dot_general | solution.py:848
  164.6 8.9 %convert_reduce_fusion = (f32[2048]{0:T(1024)}, bf16[1024,2048]{1,0:T(8,128)(2,1)S(1)}) fusion(f32[1024,2048]{1,0:T(8,128)S(1)} %get-tuple-element.84, f32[2048]{0:T(1024)S(1)} %bitcast.80, bf16[2048,1024]{1,0:T(8,128)(2,1)S(1)} %bitcast.89, bf16[512,1024]{1,0:T(8,128)(2,1)} %collective-permute-done.2, bf16[512,1024]{1,0:T(8,128)(2,1)S(1)} %bitcast.70), kind=kOutput, calls=%fused_computation.6 | convolution fusion | flops 4330616832 | bytes 18890752 | tf_op jit(solution)/shard_map/dot_general | solution.py:848
  173.5 9.3 %convolution_convert_fusion = bf16[1024,2048]{1,0:T(8,128)(2,1)} fusion(bf16[1024,2048]{1,0:T(8,128)(2,1)S(1)} %get-tuple-element.86.refs_2_, bf16[512,1024]{1,0:T(8,128)(2,1)} %collective-permute-done.1, bf16[512,1024]{1,0:T(8,128)(2,1)} %add_convert_fusion), kind=kOutput, calls=%fused_computation.10 | convolution fusion | flops 4301258752 | bytes 10485760 | tf_op jit(solution)/shard_map/dot_general | solution.py:848
  182.7 163.7 %backward.1 = (bf16[4,2,32,3072]{3,2,1,0:T(8,128)(2,1)}, bf16[2,4,2,16,1024]{4,3,2,1,0:T(8,128)(2,1)}, bf16[4,2,32,4096]{3,2,1,0:T(8,128)(2,1)}, bf16[2,4,2,64,1...) custom-call(bf16[4,2,2,2,64,1024]{5,4,3,2,1,0:T(8,128)(2,1)} %bitcast., ...), custom_call_target="tpu_custom_call" | custom-call | tf_op jit(solution)/shard_map/backward/pallas_call | solution.py:826
  346.5 0.9 slice.119
  348.0 1.5 fusion.21
  350.7 2.1 bitcast_convert_fusion.3
  352.9 3.4 bitcast_convert_fusion.2
  356.3 2.6 bitcast_convert_fusion.1
  359.0 2.6 bitcast_convert_fusion
  361.6 1.0 copy.35
  362.6 1.0 copy.36
  (59 shorter events, 10.6 us)
Async XLA Ops:
  129.3 4.5 %copy-start.10 = (f32[4,16,256]{2,1,0:T(8,128)S(1)}, f32[4,16,256]{2,1,0:T(8,128)}, u32[]{:S(2)}) copy-start(f32[4,16,256]{2,1,0:T(8,128)} %get-tuple-element.38) | copy-start | bytes 196612
  129.3 6.7 %copy-start.2 = (bf16[2,256,1024]{2,1,0:T(8,128)(2,1)S(1)}, bf16[2,256,1024]{2,1,0:T(8,128)(2,1)}, u32[]{:S(2)}) copy-start(bf16[2,256,1024]{2,1,0:T(8,128)(2,1)} %get-tuple-element.35) | copy-start | bytes 3145732
  132.4 3.6 collective-permute-start
  134.4 2.6 copy-start.9
  136.6 18.6 %copy-start = (f32[512,1024]{1,0:T(8,128)}, f32[512,1024]{1,0:T(8,128)S(1)}, u32[]{:S(2)}) copy-start(f32[512,1024]{1,0:T(8,128)S(1)} %get-tuple-element.57.refs_11_) | copy-start | bytes 6291460
  136.6 2.1 copy-start.5
  136.6 2.4 copy-start.8
  138.4 3.0 collective-permute-start.1
  138.8 18.2 %collective-permute-start.2 = (bf16[512,1024]{1,0:T(8,128)(2,1)S(1)}, bf16[512,1024]{1,0:T(8,128)(2,1)}, u32[]{:S(2)}, u32[]{:S(2)}) collective-permute-start(bf16[512,1024]{1,0:T(8,128)(2,1)S(1)} %bitcast.68), channel_id=1, source_target_pairs={{0,4},{4,0},{1,5},{5,1},{2,6},{6,2},{3,7},{7,3},{8,12},{12,8},{9,1... | collective-permute-start | bytes 3145736 | tf_op jit(solution)/shard_map/ppermute | solution.py:840
  141.4 8.1 %copy-start.11 = (bf16[4,4,2,64,1024]{4,3,2,1,0:T(8,128)(2,1)S(1)}, bf16[4,4,2,64,1024]{4,3,2,1,0:T(8,128)(2,1)}, u32[]{:S(2)}) copy-start(bf16[4,4,2,64,1024]{4,3,2,1,0:T(8,128)(2,1)} %get-tuple-element.41) | copy-start | bytes 12582916
  173.5 9.3 %copy-start.1 = (bf16[1024,2048]{1,0:T(8,128)(2,1)}, bf16[1024,2048]{1,0:T(8,128)(2,1)S(1)}, u32[]{:S(2)}) copy-start(bf16[1024,2048]{1,0:T(8,128)(2,1)S(1)} %get-tuple-element.86.refs_2_) | copy-start | bytes 12582916
  346.5 9.8 %copy-start.4 = (bf16[4,2,32,4096]{3,2,1,0:T(8,128)(2,1)S(1)}, bf16[4,2,32,4096]{3,2,1,0:T(8,128)(2,1)}, u32[]{:S(2)}) copy-start(bf16[4,2,32,4096]{3,2,1,0:T(8,128)(2,1)} %get-tuple-element.54) | copy-start | bytes 6291460
  356.3 2.7 copy-start.3
  359.0 2.6 copy-start.7
  359.0 3.6 copy-start.6

commit v7 on v6

--- a/solution.py
+++ b/solution.py
@@ -437,17 +437,18 @@
 
 def backward_body(groups, clips, blocks, *refs):
     count = len(blocks)
-    (gw2, gw1, gu, w1, wo, wq, mix, qs, kr, vb, h1, x2, x, dy, base, rest) = refs[:16]
-    (lse, cosine, sine, g1, g2, gbu) = refs[16:22]
-    outs = refs[22 : 22 + count]
-    small_o, gx_o, y_o = refs[22 + count : 25 + count]
-    (gu_b, w1_b, wo_b, mix_b, qs_b, kr_b, vb_b, h1_b, x2_b, x_b, dy_b) = refs[25 + count : 36 + count]
+    (gw2, act, slope, w2, w1, wo, wq, mix, qs, kr, vb, h1, h2, x2, x, dy, dy_all) = refs[:17]
+    (lse, cosine, sine, g1, g2, bd) = refs[17:23]
+    outs = refs[23 : 23 + count]
+    gw1, small_o, gx_o, y_o = refs[23 + count : 27 + count]
+    (gu_b, w1_b, wo_b, mix_b, qs_b, kr_b, vb_b, h1_b, x2_b, x_b, dy_b) = refs[27 + count : 38 + count]
     (own_f, give, take, y_take, dx2, low, da, gwo, gwq, ak, av, dq2, dk2, acc, gx) = refs[
-        36 + count : 51 + count
+        38 + count : 53 + count
     ]
-    ld, es, er = refs[51 + count : 54 + count]
+    (sl, gbu, stage_b) = refs[53 + count : 56 + count]
+    ld, es, er, sls = refs[56 + count : 60 + count]
     grads = (gwq, gwo, gw1, gw2)
-    scratch = refs[54 + count :]
+    scratch = refs[60 + count :]
     own_a, own_b, one_a, one_b, two_a, two_b, three, full = (
         scratch[i * count : (i + 1) * count] for i in range(8)
     )
@@ -458,10 +459,17 @@
     own, width = own_f.shape
     inner = mix_b.shape[0]
     third_width = wq.shape[1]
-    pairs = ((gu, gu_b), (w1, w1_b), (wo, wo_b), (mix, mix_b), (qs, qs_b), (kr, kr_b), (vb, vb_b))
-    pairs += ((h1, h1_b), (x2, x2_b), (x, x_b), (dy, dy_b))
+
+    upper, lower = w1_b.at[:, :width], w1_b.at[:, width:]
+    pairs = ((w2.at[:width], upper), (w2.at[width:], lower), (dy_all, low), (h2, h1_b))
+    pairs += ((x2, x2_b), (dy, dy_b), (mix, mix_b), (wo, wo_b))
+    pairs += ((qs, qs_b), (kr, kr_b), (vb, vb_b), (x, x_b))
+    pairs += ((w1, w1_b), (h1, h1_b), (act, gu_b), (w2.at[:width], upper), (w2.at[width:], lower))
+    pairs += ((wq, w1_b.at[:, :third_width]),)
     loads = [pltpu.make_async_copy(a, b, ld.at[n]) for n, (a, b) in enumerate(pairs)]
-    for copy in loads:
+    first_tile = pltpu.make_async_copy(slope.at[:, :256], sl.at[0], sls.at[0])
+    first_tile.start()
+    for copy in loads[:12]:
         copy.start()
     p, c, z = where_am_i()
     hi, lo = lax.div(p, 2), lax.rem(p, 2)
@@ -601,32 +609,71 @@
         return grad + r * e
 
     tick()
-    y_copy = remote(rest, y_take, es.at[3], er.at[3], cn)
-    y_copy.start()
-    y_base = pltpu.make_async_copy(base, dx2, ld.at[len(loads) + 1])
-    y_base.start()
     acc[...] = jnp.zeros_like(acc)
-    loads[0].wait()
-    loads[1].wait()
-    swap = half_sum(0, gu_b, w1_b, w1.shape[1])
-    wq_b = w1_b.at[:, :third_width]
-    dqkv = gu_b.at[:, :third_width]
-    late = pltpu.make_async_copy(wq, wq_b, ld.at[len(loads)])
-    late.start()
+    for copy in loads[:3]:
+        copy.wait()
+    deep = slope.shape[1]
+    sides_of = deep // width
+
+    def hidden_grad(side, i):
+        n = side * (width // 256) + i
+        slot = lax.rem(n, 2)
+        pltpu.make_async_copy(slope.at[:, :256], sl.at[slot], sls.at[slot]).wait()
+
+        @pl.when(n + 1 < deep // 256)
+        def _():
+            src = slope.at[:, tile(n + 1, 256)]
+            pltpu.make_async_copy(src, sl.at[1 - slot], sls.at[1 - slot]).start()
+
+        right = w1_b[tile(i, 256), side * width : (side + 1) * width]
+        line = jnp.zeros((1, 256), F32)
+        for r in range(2):
+            rows = slice(r * own, (r + 1) * own)
+            g = dot_t(low[rows], right) * sl[slot, rows].astype(F32)
+            g = g.astype(BF)
+            gu_b[rows, tile(n, 256)] = g
+            line = line + jnp.sum(g.astype(F32), axis=0, keepdims=True)
+        gbu[:, tile(n, 256)] = line
+
+    for side in range(sides_of):
+
+        def columns(i, carry):
+            hidden_grad(side, i)
+            return carry
+
+        lax.fori_loop(0, width // 256, columns, 0)
+        if side == 0:
+            tick()
+    loads[12].start()
+    loads[3].wait()
+    row = width // groups
+
+    def up_grad(j, carry):
+        k = lax.rem(z + j, groups)
+        left = h1_b[:, tile(k, row)].T
+
+        def columns(i, carry):
+            at = tile(i, 512)
+            stage_b[..., at] = dot(left, gu_b[:, at]).astype(BF).reshape(stage_b.shape[:-1] + (512,))
+            return carry
+
+        lax.fori_loop(0, deep // 512, columns, 0)
+        copy = pltpu.make_async_copy(stage_b, gw1.at[k], ld.at[18])
+        copy.start()
+        copy.wait()
+        return carry
+
+    lax.fori_loop(1, 3, up_grad, 0)
     tick()
-    y_base.wait()
-    y_copy.wait()
-
-    def last_add(i, carry):
-        at = tile(i, 128)
-        gx[part(i)] = (dx2[at] + y_take[at].astype(F32)).astype(BF)
-        return carry
-
-    lax.fori_loop(0, own // 128, last_add, 0)
-    y_start, y_finish, *_ = move_tokens((gx,), (y_o,), us, ur, p, c, z, clips)
-    y_start(0, 2)
-    y_start(1, 2)
-    for copy in loads[2:]:
+    lax.fori_loop(3, groups + 1, up_grad, 0)
+    loads[13].start()
+    tick()
+    loads[12].wait()
+    swap = half_sum(0, gu_b, w1_b, deep)
+    for copy in loads[14:17]:
+        copy.start()
+    tick()
+    for copy in loads[4:12]:
         copy.wait()
     swap.wait()
 
@@ -660,6 +707,39 @@
 
     lax.fori_loop(0, 2 * own // 256, attn_grad, 0)
     tick()
+
+    for copy in loads[14:17]:
+        copy.wait()
+
+    def down(rows, i):
+        left = dot(gu_b[rows, :width], w1_b[:, tile(i, 256)])
+        at = pl.ds(pl.multiple_of(width + i * 256, 256), 256)
+        return left + dot(gu_b[rows, width:], w1_b[:, at])
+
+    def down_other(i, carry):
+        give[:, tile(i, 256)] = down(slice(own, 2 * own), i).astype(BF)
+        return carry
+
+    def down_self(i, carry):
+        own_f[:, tile(i, 256)] = down(slice(0, own), i)
+        return carry
+
+    lax.fori_loop(0, width // 256, down_other, 0)
+    y_copy = remote(give, y_take, es.at[3], er.at[3], cn)
+    y_copy.start()
+    lax.fori_loop(0, width // 256, down_self, 0)
+    loads[17].start()
+    y_copy.wait()
+
+    def last_add(i, carry):
+        at = tile(i, 128)
+        gx[part(i)] = (x2_b[at] + own_f[at] + bd[...] + y_take[at].astype(F32)).astype(BF)
+        return carry
+
+    lax.fori_loop(0, own // 128, last_add, 0)
+    y_start, y_finish, *_ = move_tokens((gx,), (y_o,), us, ur, p, c, z, clips)
+    y_start(0, 4)
+    dqkv = gu_b.at[:, :third_width]
 
     def head(h, side):
         rows = tile(h, HEAD)
@@ -687,7 +767,7 @@
         dk2[place] = turn(ak[...].T, co, -si).astype(BF)
 
     heads = inner // HEAD
-    during = [steps.pop(0) for _ in range(4)]
+    during = [steps.pop(0) for _ in range(3)]
 
     def two_heads(i, carry):
         lax.fori_loop(0, 2, lambda side, _: head(2 * i + side, side), None)
@@ -698,10 +778,11 @@
             dqkv[:, at] = value
         for n, step in enumerate(during):
             pl.when(i == n * heads // 8)(functools.partial(run, step))
+            pl.when(i == n * heads // 8)(functools.partial(y_start, n + 1, 4))
         return carry
 
     lax.fori_loop(0, heads // 2, two_heads, 0)
-    row = width // groups
+    loads[13].wait()
     for g in range(groups):
         left = h1_b[:, g * row : (g + 1) * row].T
 
@@ -712,8 +793,8 @@
 
         lax.fori_loop(0, third_width // 512, in_grad, 0)
     tick()
-    late.wait()
-    swap = half_sum(2, dqkv, wq_b, third_width)
+    loads[17].wait()
+    swap = half_sum(2, dqkv, w1_b, third_width)
     tick()
     swap.wait()
     y_finish()
@@ -735,11 +816,11 @@
     for b in range(3 * groups):
         line = jnp.sum(dqkv[:, b * half : (b + 1) * half].astype(F32), axis=0, keepdims=True)
         small_s[b // 3, 6 + b % 3 : 7 + b % 3, mine_at] = line
-    deep = gbu.shape[1] // groups
+    share = deep // groups
     for g in range(groups):
-        for n in range(deep // row):
-            at = pl.ds(9 + c * (deep // row) + n, 1)
-            small_s[g, at] = gbu[:, g * deep + n * row : g * deep + (n + 1) * row]
+        for n in range(share // row):
+            at = pl.ds(9 + c * (share // row) + n, 1)
+            small_s[g, at] = gbu[:, g * share + n * row : g * share + (n + 1) * row]
     tick()
     for n, target in enumerate((cn, xn, yn)):
         copy = remote(small_s, small_r.at[n], ss.at[n], sr.at[n], target)
@@ -778,24 +859,25 @@
     finish()
 
 
-def backward(gw2, gw1, arrays, tables, lines, groups, blocks):
-    gu, w1, wo, wq, mix, qs, kr, vb, h1, x2, x, dy, base, rest = arrays
+def backward(gw2, arrays, tables, lines, groups, blocks):
+    act, slope, w2, w1, wo, wq, mix, qs, kr, vb, h1, h2, x2, x, dy, dy_all = arrays
     (own, width), clips = x.shape, dy.shape[0]
     small = jax.ShapeDtypeStruct((groups, lines + -lines % 8, width // groups), F32)
     count = len(blocks)
     dma = pltpu.SemaphoreType.DMA
     split = lambda v: (groups, 2, 2, 2, v.shape[0] // (8 * groups), v.shape[1])
-    tiles = [split(wq)[4:], split(wo)[4:], gw1.shape[4:], gw2.shape[4:]]
+    tiles = [split(v)[4:] for v in (wq, wo, w1, w2)]
     shapes = [
         jax.ShapeDtypeStruct((4, 2, t[0], 2 * t[1]) if b else (2, 4, 2) + t, BF)
         for t, b in zip(tiles, blocks)
     ]
     shapes += [
+        jax.ShapeDtypeStruct(split(w1), BF),
         jax.ShapeDtypeStruct(small.shape[1:], F32),
         jax.ShapeDtypeStruct(dy.shape, BF),
         jax.ShapeDtypeStruct(dy.shape, BF),
     ]
-    scratch = [pltpu.VMEM(v.shape, v.dtype) for v in (gu, w1, wo, mix, qs, kr, vb, h1, x2, x, dy)]
+    scratch = [pltpu.VMEM(v.shape, v.dtype) for v in (act, w1, wo, mix, qs, kr, vb, h1, x2, x, dy)]
     half, low = (own, width), pltpu.VMEM((2 * own, width), BF)
     scratch += [pltpu.VMEM(half, F32)] + [pltpu.VMEM(half, BF)] * 3
     scratch += [pltpu.VMEM(half, F32), low, pltpu.VMEM(mix.shape, BF)]
@@ -803,7 +885,9 @@
     scratch += [pltpu.VMEM((2 * own, HEAD), F32), pltpu.VMEM((2, 2 * own, HEAD), F32)]
     scratch += [pltpu.VMEM((2 * HEAD, 2 * own), BF)] * 2
     scratch += [pltpu.VMEM((8, width), F32), pltpu.VMEM(dy.shape, BF)]
-    scratch += [dma((13,)), dma((4,)), dma((4,))]
+    scratch += [pltpu.VMEM((2, 2 * own, 256), BF), pltpu.VMEM((1, act.shape[1]), F32)]
+    scratch += [pltpu.VMEM(split(w1)[1:], BF)]
+    scratch += [dma((19,)), dma((4,)), dma((4,)), dma((2,))]
     for lead in (
         (groups, 2),
         (groups, 2),
@@ -826,14 +910,14 @@
     return pl.pallas_call(
         functools.partial(backward_body, groups, clips, blocks),
         out_shape=shapes,
-        in_specs=[ANY] * (2 + len(arrays)) + [VM] * len(tables),
-        out_specs=[ANY] * count + [VM, ANY, ANY],
+        in_specs=[ANY] * (1 + len(arrays)) + [VM] * len(tables),
+        out_specs=[ANY] * (count + 1) + [VM, ANY, ANY],
         scratch_shapes=scratch,
         compiler_params=pltpu.CompilerParams(
             collective_id=1, has_side_effects=True, vmem_limit_bytes=67043328
         ),
         name="backward",
-    )(gw2, gw1, *arrays, *tables)
+    )(gw2, *arrays, *tables)
 
 
 def swap(value):
@@ -927,19 +1011,12 @@
     cdf = 0.5 * (1.0 + lax.erf(u * F32(0.7071067811865476)))
     act = (u * cdf).astype(BF)
     slope = (cdf + u * jnp.exp(-0.5 * u * u) * F32(0.3989422804014327)).astype(BF)
-    result = contract(act, w2, 1, 0)
-    base, rest = x2 + result[:own] + bd, result[own:].astype(BF)
 
     gw2 = contract(act, grad_all, 0, 0).astype(BF)
-    gu = (contract(grad_all, w2, 1, 1) * slope.astype(F32)).astype(BF)
-    gw1 = contract(h2, gu, 0, 0).astype(BF)
-    gbu = jnp.sum(gu.astype(F32), axis=0)
-    gw2, gw1 = (
-        g.reshape(groups, 2, 2, 2, g.shape[0] // (8 * groups), g.shape[1]) for g in (gw2, gw1)
-    )
-    arrays = (gu, w1, wo, wq, mixed, qs, kr, vb, h1, x2, tokens, dy, base, rest)
-    tables = (lse, cosine, sine, g1, g2, gbu.reshape(1, deep))
-    gwq, gwo, gw1, gw2, sums, gx, output = backward(gw2, gw1, arrays, tables, lines, groups, blocks)
+    gw2 = gw2.reshape(groups, 2, 2, 2, gw2.shape[0] // (8 * groups), width)
+    arrays = (act, slope, w2, w1, wo, wq, mixed, qs, kr, vb, h1, h2, x2, tokens, dy, grad_all)
+    tables = (lse, cosine, sine, g1, g2, bd)
+    gwq, gwo, gw1, gw2, _, sums, gx, output = backward(gw2, arrays, tables, lines, groups, blocks)
     gwq, gwo, gw1, gw2 = (
         g.reshape(shard.shape).astype(F32)
         for g, shard in zip((gwq, gwo, gw1, gw2), (w_qkv, w_out, w_up, w_down))

time: 368 us -> 352 us (0.957)
  matrix products: 41.3 us -> 18.5 us
  Pallas kernels: 285 us -> 296 us
    dot_general x6 -> x3, matrix products: 41.3 us -> 18.5 us  [contract(): lax.dot_general(left, right, (((a,), (b,)), ((), ())), preferred_element_...]
    pallas_call x1, Pallas kernels: 164 us -> 174 us  [backward(): pl.pallas_call(functools.partial(backward_body, groups, clips, blocks), o...]
    concatenate x0 -> x2, other arithmetic: none -> 4.69 us  [both(): return jnp.concatenate([value, swap(value)], axis=0)]
  transfers between devices with their start and end apart: 3 -> 3, of which waited for: 2 -> 1; matrix products, arithmetic and copies ran while one was open for 5% -> 1% of each run, Pallas kernels for 0% -> 0%
where the time goes in v7:
time: 352 us; the launch traced here: 351 us
  Pallas kernels  296 us (84%)
  other arithmetic  24 us (7%)
  matrix products  18.5 us (5%)
  local copies, waits for them, and re-layouts  8.72 us (2%)
    pallas_call x1, Pallas kernels, backward(): pl.pallas_call(functools.partial(backward_body, groups, clips, blocks), o...  174 us
    pallas_call x1, Pallas kernels, forward(): pl.pallas_call(functools.partial(forward_body, groups, clips, blocks), ou...  121 us
    dot_general x3, matrix products, contract(): lax.dot_general(left, right, (((a,), (b,)), ((), ())), preferred_element_...  18.5 us
    convert_element_type x4, other arithmetic, paired(): g.reshape(shard.shape).astype(F32)  10.8 us
  transfers between devices with their start and end apart: 3, of which 1 were waited for; matrix products, arithmetic and copies ran while one was open for 1% of the time, Pallas kernels for 0%

profile of v7, /device:TPU:9, one launch (start us, length us, event | category | flops | bytes accessed | tf_op | source)
XLA Modules:
  0.0 351.2 jit_solution(12881488497061322965)
XLA Ops:
  4.7 0.7 convert_element_type.148
  5.4 0.8 slice_convert_fusion.3
  6.6 0.7 pad_maximum_fusion.2.refs_6_
  7.2 0.7 select_select_fusion.refs_4_
  7.9 121.4 %forward.1 = (bf16[4,4,2,32,1536]{4,3,2,1,0:T(8,128)(2,1)}, bf16[4,4,2,16,1024]{4,3,2,1,0:T(8,128)(2,1)}, bf16[4,4,2,32,2048]{4,3,2,1,0:T(8,128)(2,1)}, bf16[4,4...) custom-call(bf16[4,2,32,3072]{3,2,1,0:T(8,128)(2,1)} %bitcast.64, ...), custom_call_target="tpu_custom_call" | custom-call | tf_op jit(solution)/shard_map/forward/pallas_call | solution.py:420
  129.3 3.0 fusion.17
  132.5 1.4 collective-permute-start
  134.5 1.6 collective-permute-done
  137.0 0.9 copy-done
  138.9 0.7 fusion.14
  139.6 1.6 pad_maximum_fusion.1.refs_16_
  141.2 3.1 pad_maximum_fusion.refs_12_
  144.3 9.2 %fusion.4 = (bf16[1024,2048]{1,0:T(8,128)(2,1)}, bf16[1024,2048]{1,0:T(8,128)(2,1)S(1)}) fusion(f32[2048]{0:T(1024)S(1)} %bitcast.72, bf16[1024,2048]{1,0:T(8,128)(2,1)S(1)} %bitcast.52, bf16[512,1024]{1,0:T(8,128)(2,1)} %collective-permute-done.1, bf16[512,1024]{1,0:T(8,128)(2,1)S(1)} %add_convert_fusion), kind=kOutput, calls=%fused_computation.5 | convolution fusion | flops 4324327424 | bytes 14688256 | tf_op jit(solution)/shard_map/dot_general | solution.py:932
  153.6 6.2 %convolution_convert_fusion = bf16[2048,1024]{1,0:T(8,128)(2,1)} fusion(bf16[1024,2048]{1,0:T(8,128)(2,1)S(1)} %get-tuple-element.59.refs_1_, bf16[512,1024]{1,0:T(8,128)(2,1)S(1)} %collective-permute-done.2, bf16[512,1024]{1,0:T(8,128)(2,1)S(1)} %bitcast.58), kind=kOutput, calls=%fused_computation.8 | convolution fusion | flops 4301258752 | bytes 10485760 | tf_op jit(solution)/shard_map/dot_general | solution.py:932
  159.8 174.3 %backward.1 = (bf16[4,2,32,3072]{3,2,1,0:T(8,128)(2,1)}, bf16[2,4,2,16,1024]{4,3,2,1,0:T(8,128)(2,1)}, bf16[4,2,32,4096]{3,2,1,0:T(8,128)(2,1)}, bf16[2,4,2,64,1...) custom-call(bf16[4,2,2,2,64,1024]{5,4,3,2,1,0:T(8,128)(2,1)} %bitcas, ...), custom_call_target="tpu_custom_call" | custom-call | tf_op jit(solution)/shard_map/backward/pallas_call | solution.py:910
  334.1 0.9 slice.110
  335.0 0.7 slice_bitcast_fusion
  335.7 1.5 fusion.16
  338.4 2.1 bitcast_convert_fusion.3
  340.5 3.4 bitcast_convert_fusion.2
  344.0 2.6 bitcast_convert_fusion.1
  346.6 2.6 bitcast_convert_fusion
  349.2 1.0 copy.35
  350.2 1.0 copy.36
  (56 shorter events, 8.2 us)
Async XLA Ops:
  129.3 4.5 %copy-start.4 = (bf16[2,256,1024]{2,1,0:T(8,128)(2,1)S(1)}, bf16[2,256,1024]{2,1,0:T(8,128)(2,1)}, u32[]{:S(2)}) copy-start(bf16[2,256,1024]{2,1,0:T(8,128)(2,1)} %get-tuple-element.40.refs_15_) | copy-start | bytes 3145732
  129.3 4.6 %copy-start.11 = (f32[4,16,256]{2,1,0:T(8,128)S(1)}, f32[4,16,256]{2,1,0:T(8,128)}, u32[]{:S(2)}) copy-start(f32[4,16,256]{2,1,0:T(8,128)} %get-tuple-element.38) | copy-start | bytes 196612
  129.3 6.8 %copy-start.3 = (bf16[2,256,1024]{2,1,0:T(8,128)(2,1)S(1)}, bf16[2,256,1024]{2,1,0:T(8,128)(2,1)}, u32[]{:S(2)}) copy-start(bf16[2,256,1024]{2,1,0:T(8,128)(2,1)} %get-tuple-element.35) | copy-start | bytes 3145732
  132.5 3.6 %collective-permute-start = (bf16[512,1024]{1,0:T(8,128)(2,1)S(1)}, bf16[512,1024]{1,0:T(8,128)(2,1)S(1)}, u32[]{:S(2)}, u32[]{:S(2)}) collective-permute-start(bf16[512,1024]{1,0:T(8,128)(2,1)S(1)} %slice.138), channel_id=1, source_target_pairs={{0,4},{4,0},{1,5},{5,1},{2,6},{6,2},{3,7},{7,3},{8,12},{12,8},{9,1... | collective-permute-start | bytes 3145736 | tf_op jit(solution)/shard_map/ppermute | solution.py:924
  133.8 5.8 %collective-permute-start.2 = (bf16[512,1024]{1,0:T(8,128)(2,1)S(1)}, bf16[512,1024]{1,0:T(8,128)(2,1)S(1)}, u32[]{:S(2)}, u32[]{:S(2)}) collective-permute-start(bf16[512,1024]{1,0:T(8,128)(2,1)S(1)} %bitcast.56), channel_id=1, source_target_pairs={{0,4},{4,0},{1,5},{5,1},{2,6},{6,2},{3,7},{7,3},{8,12},{12,8},{9,1... | collective-permute-start | bytes 3145736 | tf_op jit(solution)/shard_map/ppermute | solution.py:924
  134.5 2.5 copy-start.10
  136.6 1.3 copy-start
  136.6 2.2 copy-start.9
  138.4 2.9 collective-permute-start.1
  139.6 4.7 %copy-start.1 = (bf16[4,4,2,32,2048]{4,3,2,1,0:T(8,128)(2,1)S(1)}, bf16[4,4,2,32,2048]{4,3,2,1,0:T(8,128)(2,1)}, u32[]{:S(2)}) copy-start(bf16[4,4,2,32,2048]{4,3,2,1,0:T(8,128)(2,1)} %get-tuple-element.39) | copy-start | bytes 12582916
  153.6 6.3 %copy-start.2 = (bf16[1024,2048]{1,0:T(8,128)(2,1)}, bf16[1024,2048]{1,0:T(8,128)(2,1)S(1)}, u32[]{:S(2)}) copy-start(bf16[1024,2048]{1,0:T(8,128)(2,1)S(1)} %get-tuple-element.59.refs_1_) | copy-start | bytes 12582916
  334.1 9.8 %copy-start.6 = (bf16[4,2,32,4096]{3,2,1,0:T(8,128)(2,1)S(1)}, bf16[4,2,32,4096]{3,2,1,0:T(8,128)(2,1)}, u32[]{:S(2)}) copy-start(bf16[4,2,32,4096]{3,2,1,0:T(8,128)(2,1)} %get-tuple-element.54) | copy-start | bytes 6291460
  344.0 2.7 copy-start.5
  346.6 2.6 copy-start.8
  346.6 3.6 %copy-start.7 = (bf16[2,256,1024]{2,1,0:T(8,128)(2,1)S(1)}, bf16[2,256,1024]{2,1,0:T(8,128)(2,1)}, u32[]{:S(2)}) copy-start(bf16[2,256,1024]{2,1,0:T(8,128)(2,1)} %get-tuple-element.118) | copy-start | bytes 3145732

commit v8 on v7

--- a/solution.py
+++ b/solution.py
@@ -137,16 +137,19 @@
 def forward_body(groups, clips, blocks, *refs):
     count = len(blocks)
     raw, (small, x, tab, dy) = refs[:count], refs[count : count + 4]
-    (wq_o, *outs) = refs[count + 4 : 2 * count + 4]
-    (small_o, x_o, tab_o, dy_o, h1_o, qs_o, kr_o, vb_o, mix_o, lse_o) = refs[2 * count + 4 : 2 * count + 14]
-    halves = refs[2 * count + 14 : 3 * count + 14]
+    (wq_o, wo_o, *outs) = refs[count + 4 : 2 * count + 4]
+    (small_o, x_o, tab_o, dy_o, h1_o, qs_o, kr_o, vb_o, mix_o, lse_o, x2_o, h2_o) = refs[
+        2 * count + 4 : 2 * count + 16
+    ]
+    halves = refs[2 * count + 16 : 3 * count + 16]
     (wq_v, small_v, x_v, tab_v, tab_w, h1, qs, kr, vb, mix, qkv, gain, bias) = refs[
-        3 * count + 14 : 3 * count + 27
+        3 * count + 16 : 3 * count + 29
     ]
+    (wo_v, own_f, give, take, h2) = refs[3 * count + 29 : 3 * count + 34]
     (zs, zr, xs, xr, ys, yr, fs, fr, hs, ls, ss, sr, ts, tr, us, ur, vs, vr, es, er, ks) = refs[
-        3 * count + 27 :
+        3 * count + 34 :
     ]
-    outs = [wq_v, *outs]
+    outs = [wq_v, wo_v, *outs]
     p, c, z = where_am_i()
     for w in range(count):
         for src, dst in cuts(raw[w], halves[w], c, blocks[w]):
@@ -164,7 +167,7 @@
     keep[0].start()
     start_tab, _, sent_tab, arrive_tab = move_tokens((tab,), (tab_v,), vs, vr, p, c, z, clips)
     start_x, _, sent_x, arrive_x = move_tokens((x,), (x_v,), ts, tr, p, c, z, clips)
-    start_dy, finish_dy, *_ = move_tokens((dy,), (dy_o,), us, ur, p, c, z, clips)
+    start_dy, _, sent_dy, arrive_dy = move_tokens((dy,), (dy_o.at[:clips],), us, ur, p, c, z, clips)
     units = [(w, d, side) for w in range(count) for d in range(1, groups) for side in range(2)]
 
     def origin(d, side):
@@ -286,7 +289,7 @@
     half = row // 2
     mine = pl.ds(pl.multiple_of(c * half, half), half)
     for g in range(groups):
-        gain[0:2, g * row : (g + 1) * row] = small_v[g, 0:2]
+        gain[0:5, g * row : (g + 1) * row] = small_v[g, 0:5]
         for r in range(3):
             bias[3 * g + r : 3 * g + r + 1] = small_v[g, 6 + r : 7 + r, mine]
     small_o[...] = small_v[...]
@@ -380,19 +383,68 @@
     for n, (a, b) in enumerate(((qs, qs_o), (kr, kr_o), (vb, vb_o), (mix, mix_o))):
         saves.append(pltpu.make_async_copy(a, b, ks.at[3 + n]))
         saves[-1].start()
+    for u in units[2 * (groups - 1) : 4 * (groups - 1)]:
+        complete(u)
+    keep[2].wait()
+    saves.append(pltpu.make_async_copy(wo_v, wo_o, ks.at[7]))
+    saves[-1].start()
+    width = h1.shape[1]
+    left_other, left_self = mix[:, own_count:].T, mix[:, :own_count].T
+
+    def out_other(i, carry):
+        at = tile(i, 256)
+        give[:, at] = dot(left_other, wo_v[..., at].reshape(inner, 256)).astype(BF)
+        return carry
+
+    def out_self(i, carry):
+        at = tile(i, 256)
+        own_f[:, at] = dot(left_self, wo_v[..., at].reshape(inner, 256))
+        return carry
+
+    lax.fori_loop(0, width // 256, out_other, 0)
+    swap = remote(give, take, es.at[2], er.at[2], cn)
+    swap.start()
+    lax.fori_loop(0, width // 256, out_self, 0)
+    step(steps.pop(0))
+    swap.wait()
+
+    def second_norm(i, carry):
+        per = own_count // clips // 128
+        at = tile(i, 128)
+        v = x_v[lax.div(i, per), tile(lax.rem(i, per), 128)].astype(F32)
+        v = v + (own_f[at] + take[at].astype(F32)) + gain[2:3]
+        own_f[at] = v
+        v = v - jnp.mean(v, axis=1, keepdims=True)
+        v = v * lax.rsqrt(jnp.mean(v * v, axis=1, keepdims=True) + EPS)
+        h2[at] = (v * gain[3:4] + gain[4:5]).astype(BF)
+        return carry
+
+    lax.fori_loop(0, own_count // 128, second_norm, 0)
+    swap = remote(h2.at[:own_count], h2.at[own_count:], es.at[0], er.at[0], cn)
+    swap.start()
+    saves.append(pltpu.make_async_copy(own_f, x2_o, ks.at[8]))
+    saves[-1].start()
+    step(steps.pop(0))
+    swap.wait()
+    saves.append(pltpu.make_async_copy(h2, h2_o, ks.at[9]))
+    saves[-1].start()
     while steps:
         step(steps.pop(0))
-    for u in units[2 * (groups - 1) :]:
+    arrive_dy()
+    swap_dy = remote(dy_o.at[:clips], dy_o.at[clips:], es.at[3], er.at[3], cn)
+    swap_dy.start()
+    for u in units[4 * (groups - 1) :]:
         complete(u)
     for u in units:
         settle(u)
     for s in smalls:
         s.wait_send()
-    for k in keep[2:] + saves:
+    for k in keep[3:] + saves:
         k.wait()
+    swap_dy.wait()
+    sent_dy()
     sent_tab()
     sent_x()
-    finish_dy()
 
 
 def half_shape(raw, blocks):
@@ -409,25 +461,27 @@
     feature = (inner, 2 * own)
     shapes = [of((groups,) + h, BF) for h in halves]
     shapes += [of((groups,) + small.shape, F32), of(x.shape, BF), of((HEAD, 2 * own), F32)]
-    shapes += [of(x.shape, BF), of((2 * own, width), BF)] + [of(feature, BF)] * 4
-    shapes += [of((inner // HEAD, 1, 2 * own), F32)]
+    shapes += [of((2 * clips,) + x.shape[1:], BF), of((2 * own, width), BF)] + [of(feature, BF)] * 4
+    shapes += [of((inner // HEAD, 1, 2 * own), F32), of((own, width), F32), of((2 * own, width), BF)]
     vm = pltpu.VMEM
     scratch = [vm(h, BF) for h in halves]
     scratch += [vm((groups,) + halves[0], BF), vm((groups,) + small.shape, F32), vm(x.shape, BF)]
     scratch += [vm(tab.shape, F32)] * 2 + [vm((2 * own, width), BF)] + [vm(feature, BF)] * 4
     scratch += [vm((3, 2 * HEAD, 2 * own), F32), vm((8, width), F32)]
     scratch += [vm((3 * groups + -3 * groups % 8, width // groups // 2), F32)]
+    scratch += [vm((groups,) + halves[1], BF), vm((own, width), F32)]
+    scratch += [vm((own, width), BF)] * 2 + [vm((2 * own, width), BF)]
     return pl.pallas_call(
         functools.partial(forward_body, groups, clips, blocks),
         out_shape=shapes,
         in_specs=[ANY] * count + [VM, ANY, ANY, ANY],
-        out_specs=[ANY] * count + [VM, ANY, VM] + [ANY] * 6 + [VM],
+        out_specs=[ANY] * count + [VM, ANY, VM] + [ANY] * 6 + [VM, ANY, ANY],
         scratch_shapes=scratch
         + [dma((count, 2, groups))] * 6
         + [dma((count, 2, groups, 2))] * 2
         + [dma((count,)), dma((count + 1,)), dma((groups,)), dma((groups,))]
         + [dma((1, clips))] * 6
-        + [dma((2,)), dma((2,)), dma((7,))],
+        + [dma((4,)), dma((4,)), dma((10,))],
         compiler_params=pltpu.CompilerParams(
             collective_id=0, has_side_effects=True, vmem_limit_bytes=60 * 1024 * 1024
         ),
@@ -462,7 +516,7 @@
 
     upper, lower = w1_b.at[:, :width], w1_b.at[:, width:]
     pairs = ((w2.at[:width], upper), (w2.at[width:], lower), (dy_all, low), (h2, h1_b))
-    pairs += ((x2, x2_b), (dy, dy_b), (mix, mix_b), (wo, wo_b))
+    pairs += ((x2, x2_b), (dy.at[:clips], dy_b), (mix, mix_b), (wo, wo_b))
     pairs += ((qs, qs_b), (kr, kr_b), (vb, vb_b), (x, x_b))
     pairs += ((w1, w1_b), (h1, h1_b), (act, gu_b), (w2.at[:width], upper), (w2.at[width:], lower))
     pairs += ((wq, w1_b.at[:, :third_width]),)
@@ -861,7 +915,8 @@
 
 def backward(gw2, arrays, tables, lines, groups, blocks):
     act, slope, w2, w1, wo, wq, mix, qs, kr, vb, h1, h2, x2, x, dy, dy_all = arrays
-    (own, width), clips = x.shape, dy.shape[0]
+    (own, width), clips = x.shape, dy.shape[0] // 2
+    moved = jax.ShapeDtypeStruct((clips,) + dy.shape[1:], BF)
     small = jax.ShapeDtypeStruct((groups, lines + -lines % 8, width // groups), F32)
     count = len(blocks)
     dma = pltpu.SemaphoreType.DMA
@@ -874,17 +929,17 @@
     shapes += [
         jax.ShapeDtypeStruct(split(w1), BF),
         jax.ShapeDtypeStruct(small.shape[1:], F32),
-        jax.ShapeDtypeStruct(dy.shape, BF),
-        jax.ShapeDtypeStruct(dy.shape, BF),
+        moved,
+        moved,
     ]
-    scratch = [pltpu.VMEM(v.shape, v.dtype) for v in (act, w1, wo, mix, qs, kr, vb, h1, x2, x, dy)]
+    scratch = [pltpu.VMEM(v.shape, v.dtype) for v in (act, w1, wo, mix, qs, kr, vb, h1, x2, x, moved)]
     half, low = (own, width), pltpu.VMEM((2 * own, width), BF)
     scratch += [pltpu.VMEM(half, F32)] + [pltpu.VMEM(half, BF)] * 3
     scratch += [pltpu.VMEM(half, F32), low, pltpu.VMEM(mix.shape, BF)]
     scratch += [pltpu.VMEM(split(wo), BF), pltpu.VMEM(split(wq), BF)]
     scratch += [pltpu.VMEM((2 * own, HEAD), F32), pltpu.VMEM((2, 2 * own, HEAD), F32)]
     scratch += [pltpu.VMEM((2 * HEAD, 2 * own), BF)] * 2
-    scratch += [pltpu.VMEM((8, width), F32), pltpu.VMEM(dy.shape, BF)]
+    scratch += [pltpu.VMEM((8, width), F32), pltpu.VMEM(moved.shape, BF)]
     scratch += [pltpu.VMEM((2, 2 * own, 256), BF), pltpu.VMEM((1, act.shape[1]), F32)]
     scratch += [pltpu.VMEM(split(w1)[1:], BF)]
     scratch += [dma((19,)), dma((4,)), dma((4,)), dma((2,))]
@@ -974,13 +1029,14 @@
     ]
     bq, bu = b_qkv.shape[0] // row, b_up.shape[0] // row
     vectors = [ln1_gain, ln1_bias, b_out, ln2_gain, ln2_bias, b_down]
-    vectors += [b_qkv[n * row : (n + 1) * row] for n in range(bq)]
-    vectors += [b_up[n * row : (n + 1) * row] for n in range(bu)]
-    lines = len(vectors)
-    place = lax.broadcasted_iota(jnp.int32, (lines + -lines % 8, row), 0)
-    small = jnp.zeros(place.shape, F32)
-    for n, v in enumerate(vectors):
-        small = jnp.where(place == n, v.astype(F32)[None, :], small)
+    vectors += [b_qkv, b_up]
+    lines = len(vectors) - 2 + bq + bu
+    size, start = (lines + -lines % 8) * row, 0
+    small = jnp.zeros((size,), F32)
+    for v in vectors:
+        small = small + jnp.pad(v.astype(F32), (start, size - start - v.shape[0]))
+        start += v.shape[0]
+    small = small.reshape(-1, row)
     pair = jnp.arange(HEAD // 2)
     band = (pair >= 10).astype(jnp.int32) + (pair >= 21).astype(jnp.int32)
     begin = jnp.where(band == 0, 0, jnp.where(band == 1, 10, 21))
@@ -991,7 +1047,7 @@
     chosen = jnp.where(band == 0, pos[0], jnp.where(band == 1, pos[1], pos[2]))
     angles = chosen * freq[None, :, None]
     tab = jnp.concatenate([jnp.cos(angles), jnp.sin(angles)], axis=1)
-    wq, wo, w1, w2, small, x, tab, dy, h1, qs, kr, vb, mixed, lse = forward(
+    wq, wo, w1, w2, small, x, tab, dy, h1, qs, kr, vb, mixed, lse, x2, h2 = forward(
         raw, blocks, small, tokens, tab, cotangent, groups
     )
     cosine, sine = tab[: HEAD // 2], tab[HEAD // 2 :]
@@ -999,14 +1055,10 @@
     wo = wo.reshape(wide, width)
     w1 = w1.reshape(width, deep)
     w2 = w2.reshape(deep, width)
-    g1, b1, bo, g2, b2, bd = (small[:, n].reshape(1, width) for n in range(6))
+    g1, g2, bd = (small[:, n].reshape(1, width) for n in (0, 3, 5))
     bu_own = pick(small[:, 6 + bq : lines].reshape(groups, 2, deep // groups), 1).reshape(1, deep)
-    grad_out = dy.reshape(own, width)
-    grad_all = both(grad_out)
+    grad_all = dy.reshape(length, width)
     tokens = x.reshape(own, width)
-    x = tokens.astype(F32)
-    x2 = x + own_sum(contract(mixed, wo, 0, 0)) + bo
-    h2 = both((normalize(x2)[0] * g2 + b2).astype(BF))
     u = contract(h2, w1, 1, 0) + bu_own
     cdf = 0.5 * (1.0 + lax.erf(u * F32(0.7071067811865476)))
     act = (u * cdf).astype(BF)

time: 352 us -> 340 us (0.966)
  other arithmetic: 24 us -> 13.3 us
    convert_element_type x8 -> x0, other arithmetic: 5.18 us -> none  [the longest x7 4.78 us: paired(): small = jnp.where(place == n, v.astype(F32)[None, :], small)]
    concatenate x2 -> x0, other arithmetic: 4.69 us -> none  [both(): return jnp.concatenate([value, swap(value)], axis=0)]
    dot_general x3 -> x2, matrix products: 18.5 us -> 17.2 us  [contract(): lax.dot_general(left, right, (((a,), (b,)), ((), ())), preferred_element_...]
  transfers between devices with their start and end apart: 3 -> 0, of which waited for: 1 -> 0; matrix products, arithmetic and copies ran while one was open for 1% -> 0% of each run, Pallas kernels for 0% -> 0%
where the time goes in v8:
time: 340 us; the launch traced here: 339 us
  Pallas kernels  297 us (87%)
  matrix products  17.2 us (5%)
  other arithmetic  13.3 us (4%)
  local copies, waits for them, and re-layouts  10.8 us (3%)
    pallas_call x1, Pallas kernels, backward(): pl.pallas_call(functools.partial(backward_body, groups, clips, blocks), o...  175 us
    pallas_call x1, Pallas kernels, forward(): pl.pallas_call(functools.partial(forward_body, groups, clips, blocks), ou...  122 us
    dot_general x2, matrix products, contract(): lax.dot_general(left, right, (((a,), (b,)), ((), ())), preferred_element_...  17.2 us
    convert_element_type x4, other arithmetic, paired(): g.reshape(shard.shape).astype(F32)  10.8 us

profile of v8, /device:TPU:9, one launch (start us, length us, event | category | flops | bytes accessed | tf_op | source)
XLA Modules:
  0.0 338.8 jit_solution(18404359261439489525)
XLA Ops:
  0.7 0.7 convert_element_type.110
  1.4 0.8 convert_add_fusion
  2.2 0.6 reshape.129.refs_4_
  2.8 0.3 fusion.6
  3.1 0.7 pad_maximum_fusion.refs_6_
  3.8 121.5 %forward.1 = (bf16[4,4,2,32,1536]{4,3,2,1,0:T(8,128)(2,1)}, bf16[4,4,2,16,1024]{4,3,2,1,0:T(8,128)(2,1)}, bf16[4,4,2,32,2048]{4,3,2,1,0:T(8,128)(2,1)}, bf16[4,4...) custom-call(bf16[4,2,32,3072]{3,2,1,0:T(8,128)(2,1)} %bitcast.55, ...), custom_call_target="tpu_custom_call" | custom-call | tf_op jit(solution)/shard_map/forward/pallas_call | solution.py:474
  125.3 1.5 fusion.10
  126.8 0.8 slice.57
  127.6 1.7 fusion.9
  129.3 11.0 %fusion.4 = (bf16[1024,2048]{1,0:T(8,128)(2,1)}, bf16[1024,2048]{1,0:T(8,128)(2,1)S(1)}) fusion(f32[2048]{0:T(1024)S(1)} %bitcast.62, bf16[1024,1024]{1,0:T(8,128)(2,1)} %get-tuple-element.37.refs_12_, bf16[1024,2048]{1,0:T(8,128)(2,1)} %bitcast.48), kind=kOutput, calls=%fused_computation.5 | convolution fusion | flops 4320133120 | bytes 14688256 | tf_op jit(solution)/shard_map/dot_general | solution.py:987
  140.2 0.0 copy-done
  140.2 6.2 %convolution_convert_fusion = bf16[2048,1024]{1,0:T(8,128)(2,1)} fusion(bf16[1024,2048]{1,0:T(8,128)(2,1)S(1)} %get-tuple-element.61.refs_1_, bf16[1024,1024]{1,0:T(8,128)(2,1)S(1)} %bitcast.47), kind=kOutput, calls=%fused_computation.8 | convolution fusion | flops 4297064448 | bytes 10485760 | tf_op jit(solution)/shard_map/dot_general | solution.py:987
  146.5 175.3 %backward.1 = (bf16[4,2,32,3072]{3,2,1,0:T(8,128)(2,1)}, bf16[2,4,2,16,1024]{4,3,2,1,0:T(8,128)(2,1)}, bf16[4,2,32,4096]{3,2,1,0:T(8,128)(2,1)}, bf16[2,4,2,64,1...) custom-call(bf16[4,2,2,2,64,1024]{5,4,3,2,1,0:T(8,128)(2,1)} %bitcas, ...), custom_call_target="tpu_custom_call" | custom-call | tf_op jit(solution)/shard_map/backward/pallas_call | solution.py:965
  321.8 0.9 slice.65
  322.6 0.6 reshape.138
  323.2 0.7 slice_bitcast_fusion
  323.9 1.5 fusion.11
  325.4 0.6 copy.29
  326.0 2.1 bitcast_convert_fusion.3
  328.2 3.4 %bitcast_convert_fusion.2 = f32[256,3072]{1,0:T(8,128)} fusion(bf16[4,2,32,3072]{3,2,1,0:T(8,128)(2,1)} %get-tuple-element.56), kind=kLoop, calls=%fused_computation.11 | loop fusion | flops 786432 | bytes 4718592 | tf_op jit(solution)/shard_map/convert_element_type | solution.py:1073
  331.6 2.6 bitcast_convert_fusion.1
  334.3 2.6 bitcast_convert_fusion
  336.9 1.0 copy.32
  337.8 1.0 copy.33
  (16 shorter events, 0.1 us)
Async XLA Ops:
  129.3 11.0 %copy-start = (bf16[4,256,1024]{2,1,0:T(8,128)(2,1)S(1)}, bf16[4,256,1024]{2,1,0:T(8,128)(2,1)}, u32[]{:S(2)}) copy-start(bf16[4,256,1024]{2,1,0:T(8,128)(2,1)} %get-tuple-element.40.refs_15_) | copy-start | bytes 6291460
  140.2 6.2 %copy-start.1 = (bf16[1024,2048]{1,0:T(8,128)(2,1)}, bf16[1024,2048]{1,0:T(8,128)(2,1)S(1)}, u32[]{:S(2)}) copy-start(bf16[1024,2048]{1,0:T(8,128)(2,1)S(1)} %get-tuple-element.61.refs_1_) | copy-start | bytes 12582916
  321.8 9.8 %copy-start.3 = (bf16[4,2,32,4096]{3,2,1,0:T(8,128)(2,1)S(1)}, bf16[4,2,32,4096]{3,2,1,0:T(8,128)(2,1)}, u32[]{:S(2)}) copy-start(bf16[4,2,32,4096]{3,2,1,0:T(8,128)(2,1)} %get-tuple-element.58) | copy-start | bytes 6291460
  331.6 2.6 copy-start.2
  334.3 2.6 copy-start.5
  334.3 3.6 %copy-start.4 = (bf16[2,256,1024]{2,1,0:T(8,128)(2,1)S(1)}, bf16[2,256,1024]{2,1,0:T(8,128)(2,1)}, u32[]{:S(2)}) copy-start(bf16[2,256,1024]{2,1,0:T(8,128)(2,1)} %get-tuple-element.95) | copy-start | bytes 3145732

commit v9 on v8

--- a/solution.py
+++ b/solution.py
@@ -138,12 +138,12 @@
     count = len(blocks)
     raw, (small, x, tab, dy) = refs[:count], refs[count : count + 4]
     (wq_o, wo_o, *outs) = refs[count + 4 : 2 * count + 4]
-    (small_o, x_o, tab_o, dy_o, h1_o, qs_o, kr_o, vb_o, mix_o, lse_o, x2_o, h2_o) = refs[
-        2 * count + 4 : 2 * count + 16
+    (gain, bu, x_o, tab_o, dy_o, h1_o, qs_o, kr_o, vb_o, mix_o, lse_o, x2_o, h2_o) = refs[
+        2 * count + 4 : 2 * count + 17
     ]
-    halves = refs[2 * count + 16 : 3 * count + 16]
-    (wq_v, small_v, x_v, tab_v, tab_w, h1, qs, kr, vb, mix, qkv, gain, bias) = refs[
-        3 * count + 16 : 3 * count + 29
+    halves = refs[2 * count + 17 : 3 * count + 17]
+    (wq_v, small_v, x_v, tab_v, tab_w, h1, qs, kr, vb, mix, qkv, bias) = refs[
+        3 * count + 17 : 3 * count + 29
     ]
     (wo_v, own_f, give, take, h2) = refs[3 * count + 29 : 3 * count + 34]
     (zs, zr, xs, xr, ys, yr, fs, fr, hs, ls, ss, sr, ts, tr, us, ur, vs, vr, es, er, ks) = refs[
@@ -289,10 +289,13 @@
     half = row // 2
     mine = pl.ds(pl.multiple_of(c * half, half), half)
     for g in range(groups):
-        gain[0:5, g * row : (g + 1) * row] = small_v[g, 0:5]
+        gain[0:6, g * row : (g + 1) * row] = small_v[g, 0:6]
+        share = bu.shape[1] // groups
+        for n in range(share // row):
+            line = small_v[g, pl.ds(9 + c * (share // row) + n, 1)]
+            bu[:, g * share + n * row : g * share + (n + 1) * row] = line
         for r in range(3):
             bias[3 * g + r : 3 * g + r + 1] = small_v[g, 6 + r : 7 + r, mine]
-    small_o[...] = small_v[...]
     own_count = h1.shape[0] // 2
     arrive_x()
     saves = [pltpu.make_async_copy(x_v, x_o, ks.at[0])]
@@ -460,14 +463,15 @@
     of = jax.ShapeDtypeStruct
     feature = (inner, 2 * own)
     shapes = [of((groups,) + h, BF) for h in halves]
-    shapes += [of((groups,) + small.shape, F32), of(x.shape, BF), of((HEAD, 2 * own), F32)]
+    shapes += [of((8, width), F32), of((1, halves[2][-1]), F32)]
+    shapes += [of(x.shape, BF), of((HEAD, 2 * own), F32)]
     shapes += [of((2 * clips,) + x.shape[1:], BF), of((2 * own, width), BF)] + [of(feature, BF)] * 4
     shapes += [of((inner // HEAD, 1, 2 * own), F32), of((own, width), F32), of((2 * own, width), BF)]
     vm = pltpu.VMEM
     scratch = [vm(h, BF) for h in halves]
     scratch += [vm((groups,) + halves[0], BF), vm((groups,) + small.shape, F32), vm(x.shape, BF)]
     scratch += [vm(tab.shape, F32)] * 2 + [vm((2 * own, width), BF)] + [vm(feature, BF)] * 4
-    scratch += [vm((3, 2 * HEAD, 2 * own), F32), vm((8, width), F32)]
+    scratch += [vm((3, 2 * HEAD, 2 * own), F32)]
     scratch += [vm((3 * groups + -3 * groups % 8, width // groups // 2), F32)]
     scratch += [vm((groups,) + halves[1], BF), vm((own, width), F32)]
     scratch += [vm((own, width), BF)] * 2 + [vm((2 * own, width), BF)]
@@ -475,7 +479,7 @@
         functools.partial(forward_body, groups, clips, blocks),
         out_shape=shapes,
         in_specs=[ANY] * count + [VM, ANY, ANY, ANY],
-        out_specs=[ANY] * count + [VM, ANY, VM] + [ANY] * 6 + [VM, ANY, ANY],
+        out_specs=[ANY] * count + [VM, VM, ANY, VM] + [ANY] * 6 + [VM, ANY, ANY],
         scratch_shapes=scratch
         + [dma((count, 2, groups))] * 6
         + [dma((count, 2, groups, 2))] * 2
@@ -492,17 +496,19 @@
 def backward_body(groups, clips, blocks, *refs):
     count = len(blocks)
     (gw2, act, slope, w2, w1, wo, wq, mix, qs, kr, vb, h1, h2, x2, x, dy, dy_all) = refs[:17]
-    (lse, cosine, sine, g1, g2, bd) = refs[17:23]
-    outs = refs[23 : 23 + count]
-    gw1, small_o, gx_o, y_o = refs[23 + count : 27 + count]
-    (gu_b, w1_b, wo_b, mix_b, qs_b, kr_b, vb_b, h1_b, x2_b, x_b, dy_b) = refs[27 + count : 38 + count]
+    lse, tab, gain = refs[17:20]
+    cosine, sine = tab.at[: HEAD // 2], tab.at[HEAD // 2 :]
+    g1, g2, bd = (gain.at[n : n + 1] for n in (0, 3, 5))
+    outs = refs[20 : 20 + count]
+    gw1, small_o, gx_o, y_o = refs[20 + count : 24 + count]
+    (gu_b, w1_b, wo_b, mix_b, qs_b, kr_b, vb_b, h1_b, x2_b, x_b, dy_b) = refs[24 + count : 35 + count]
     (own_f, give, take, y_take, dx2, low, da, gwo, gwq, ak, av, dq2, dk2, acc, gx) = refs[
-        38 + count : 53 + count
+        35 + count : 50 + count
     ]
-    (sl, gbu, stage_b) = refs[53 + count : 56 + count]
-    ld, es, er, sls = refs[56 + count : 60 + count]
+    (sl, gbu, stage_b) = refs[50 + count : 53 + count]
+    ld, es, er, sls = refs[53 + count : 57 + count]
     grads = (gwq, gwo, gw1, gw2)
-    scratch = refs[60 + count :]
+    scratch = refs[57 + count :]
     own_a, own_b, one_a, one_b, two_a, two_b, three, full = (
         scratch[i * count : (i + 1) * count] for i in range(8)
     )
@@ -625,8 +631,9 @@
         for stage, what in todo[step]:
             stage(what)
 
-    def tick():
-        run(steps.pop(0))
+    def tick(times=1):
+        for _ in range(times):
+            run(steps.pop(0))
 
     def half_sum(n, left, right, depth):
         def other(i, carry):
@@ -846,10 +853,10 @@
             return carry
 
         lax.fori_loop(0, third_width // 512, in_grad, 0)
-    tick()
+    tick(3)
     loads[17].wait()
     swap = half_sum(2, dqkv, w1_b, third_width)
-    tick()
+    tick(2)
     swap.wait()
     y_finish()
 
@@ -880,8 +887,7 @@
         copy = remote(small_s, small_r.at[n], ss.at[n], sr.at[n], target)
         copy.start()
         start(n + 1, 4)
-        for _ in range(1 if n == 0 else 3):
-            tick()
+        tick()
         copy.wait()
         small_s[...] += small_r[n]
     tails = [
@@ -975,21 +981,8 @@
     )(gw2, *arrays, *tables)
 
 
-def swap(value):
-    return lax.ppermute(value, "core", [(0, 1), (1, 0)])
-
-
-def both(value):
-    return jnp.concatenate([value, swap(value)], axis=0)
-
-
 def contract(left, right, a, b):
     return lax.dot_general(left, right, (((a,), (b,)), ((), ())), preferred_element_type=F32)
-
-
-def own_sum(partial):
-    half = partial.shape[0] // 2
-    return partial[:half] + swap(partial[half:].astype(BF)).astype(F32)
 
 
 def paired(
@@ -1047,16 +1040,13 @@
     chosen = jnp.where(band == 0, pos[0], jnp.where(band == 1, pos[1], pos[2]))
     angles = chosen * freq[None, :, None]
     tab = jnp.concatenate([jnp.cos(angles), jnp.sin(angles)], axis=1)
-    wq, wo, w1, w2, small, x, tab, dy, h1, qs, kr, vb, mixed, lse, x2, h2 = forward(
+    wq, wo, w1, w2, gain, bu_own, x, tab, dy, h1, qs, kr, vb, mixed, lse, x2, h2 = forward(
         raw, blocks, small, tokens, tab, cotangent, groups
     )
-    cosine, sine = tab[: HEAD // 2], tab[HEAD // 2 :]
     wq = wq.reshape(width, 3 * wide)
     wo = wo.reshape(wide, width)
     w1 = w1.reshape(width, deep)
     w2 = w2.reshape(deep, width)
-    g1, g2, bd = (small[:, n].reshape(1, width) for n in (0, 3, 5))
-    bu_own = pick(small[:, 6 + bq : lines].reshape(groups, 2, deep // groups), 1).reshape(1, deep)
     grad_all = dy.reshape(length, width)
     tokens = x.reshape(own, width)
     u = contract(h2, w1, 1, 0) + bu_own
@@ -1067,7 +1057,7 @@
     gw2 = contract(act, grad_all, 0, 0).astype(BF)
     gw2 = gw2.reshape(groups, 2, 2, 2, gw2.shape[0] // (8 * groups), width)
     arrays = (act, slope, w2, w1, wo, wq, mixed, qs, kr, vb, h1, h2, x2, tokens, dy, grad_all)
-    tables = (lse, cosine, sine, g1, g2, bd)
+    tables = (lse, tab, gain)
     gwq, gwo, gw1, gw2, _, sums, gx, output = backward(gw2, arrays, tables, lines, groups, blocks)
     gwq, gwo, gw1, gw2 = (
         g.reshape(shard.shape).astype(F32)

time: 340 us -> 345 us (1.015)
  Pallas kernels: 297 us -> 306 us
  local copies, waits for them, and re-layouts: 10.8 us -> 6.85 us
    pallas_call x1, Pallas kernels: 175 us -> 184 us  [backward(): pl.pallas_call(functools.partial(backward_body, groups, clips, blocks), o...]
    slice x3 -> x0, local copies, waits for them, and re-layouts: 3.93 us -> none  [the longest x1 1.69 us: paired(): cosine, sine = (tab[:HEAD // 2], tab[HEAD // 2:])]
where the time goes in v9:
time: 345 us; the launch traced here: 344 us
  Pallas kernels  306 us (89%)
  matrix products  17.2 us (5%)
  other arithmetic  13.3 us (4%)
  local copies, waits for them, and re-layouts  6.85 us (2%)
    pallas_call x1, Pallas kernels, backward(): pl.pallas_call(functools.partial(backward_body, groups, clips, blocks), o...  184 us
    pallas_call x1, Pallas kernels, forward(): pl.pallas_call(functools.partial(forward_body, groups, clips, blocks), ou...  122 us
    dot_general x2, matrix products, contract(): lax.dot_general(left, right, (((a,), (b,)), ((), ())), preferred_element_...  17.2 us
    convert_element_type x4, other arithmetic, paired(): g.reshape(shard.shape).astype(F32)  10.8 us

profile of v9, /device:TPU:9, one launch (start us, length us, event | category | flops | bytes accessed | tf_op | source)
XLA Modules:
  0.0 343.9 jit_solution(582777043971119982)
XLA Ops:
  0.7 0.7 convert_element_type.110
  1.4 0.8 convert_add_fusion
  2.2 0.6 reshape.123.refs_4_
  2.8 0.3 fusion.6
  3.1 0.7 pad_maximum_fusion.refs_6_
  3.8 121.5 %forward.1 = (bf16[4,4,2,32,1536]{4,3,2,1,0:T(8,128)(2,1)}, bf16[4,4,2,16,1024]{4,3,2,1,0:T(8,128)(2,1)}, bf16[4,4,2,32,2048]{4,3,2,1,0:T(8,128)(2,1)}, bf16[4,4...) custom-call(bf16[4,2,32,3072]{3,2,1,0:T(8,128)(2,1)} %bitcast.52, ...), custom_call_target="tpu_custom_call" | custom-call | tf_op jit(solution)/shard_map/forward/pallas_call | solution.py:478
  125.3 0.0 copy-start
  125.3 11.0 %fusion.4 = (bf16[1024,2048]{1,0:T(8,128)(2,1)}, bf16[1024,2048]{1,0:T(8,128)(2,1)S(1)}) fusion(f32[2048]{0:T(1024)} %bitcast.63, bf16[1024,1024]{1,0:T(8,128)(2,1)} %get-tuple-element.38.refs_12_, bf16[1024,2048]{1,0:T(8,128)(2,1)} %bitcast.45), kind=kOutput, calls=%fused_computation.5 | convolution fusion | flops 4320133120 | bytes 14688256 | tf_op jit(solution)/shard_map/dot_general | solution.py:985
  136.3 6.2 %convolution_convert_fusion = bf16[2048,1024]{1,0:T(8,128)(2,1)} fusion(bf16[1024,2048]{1,0:T(8,128)(2,1)S(1)} %get-tuple-element.63.refs_1_, bf16[1024,1024]{1,0:T(8,128)(2,1)S(1)} %bitcast.44), kind=kOutput, calls=%fused_computation.8 | convolution fusion | flops 4297064448 | bytes 10485760 | tf_op jit(solution)/shard_map/dot_general | solution.py:985
  142.5 184.3 %backward.1 = (bf16[4,2,32,3072]{3,2,1,0:T(8,128)(2,1)}, bf16[2,4,2,16,1024]{4,3,2,1,0:T(8,128)(2,1)}, bf16[4,2,32,4096]{3,2,1,0:T(8,128)(2,1)}, bf16[2,4,2,64,1...) custom-call(bf16[4,2,2,2,64,1024]{5,4,3,2,1,0:T(8,128)(2,1)} %bitcas, ...), custom_call_target="tpu_custom_call" | custom-call | tf_op jit(solution)/shard_map/backward/pallas_call | solution.py:971
  326.8 0.0 copy-start.3
  326.8 0.9 slice.41
  327.7 0.6 reshape.131
  328.3 0.7 slice_bitcast_fusion
  329.0 1.5 fusion.9
  330.5 0.6 copy.29
  331.1 2.1 bitcast_convert_fusion.3
  333.2 3.4 bitcast_convert_fusion.2
  336.7 2.6 bitcast_convert_fusion.1
  339.3 2.6 bitcast_convert_fusion
  341.9 0.0 copy-done.5
  341.9 1.0 copy.32
  342.9 0.0 copy-done.4
  342.9 1.0 copy.33
  (11 shorter events, 0.0 us)
Async XLA Ops:
  125.3 11.0 %copy-start = (bf16[4,256,1024]{2,1,0:T(8,128)(2,1)S(1)}, bf16[4,256,1024]{2,1,0:T(8,128)(2,1)}, u32[]{:S(2)}) copy-start(bf16[4,256,1024]{2,1,0:T(8,128)(2,1)} %get-tuple-element.41.refs_15_) | copy-start | bytes 6291460
  136.3 6.2 %copy-start.1 = (bf16[1024,2048]{1,0:T(8,128)(2,1)}, bf16[1024,2048]{1,0:T(8,128)(2,1)S(1)}, u32[]{:S(2)}) copy-start(bf16[1024,2048]{1,0:T(8,128)(2,1)S(1)} %get-tuple-element.63.refs_1_) | copy-start | bytes 12582916
  326.8 9.8 %copy-start.3 = (bf16[4,2,32,4096]{3,2,1,0:T(8,128)(2,1)S(1)}, bf16[4,2,32,4096]{3,2,1,0:T(8,128)(2,1)}, u32[]{:S(2)}) copy-start(bf16[4,2,32,4096]{3,2,1,0:T(8,128)(2,1)} %get-tuple-element.60) | copy-start | bytes 6291460
  336.7 2.6 copy-start.2
  339.3 2.6 copy-start.5
  339.3 3.6 %copy-start.4 = (bf16[2,256,1024]{2,1,0:T(8,128)(2,1)S(1)}, bf16[2,256,1024]{2,1,0:T(8,128)(2,1)}, u32[]{:S(2)}) copy-start(bf16[2,256,1024]{2,1,0:T(8,128)(2,1)} %get-tuple-element.92) | copy-start | bytes 3145732

commit v10 on v9

--- a/solution.py
+++ b/solution.py
@@ -615,7 +615,7 @@
             pltpu.make_async_copy(src, dst, ls.at[w]).start()
             remote(src, dst, cs.at[w], cr.at[w], cn).start()
 
-    ahead, lag = 3, 2
+    ahead, lag = 3, 3
     todo = {}
     for n, u in enumerate(units):
         todo.setdefault(max(n - ahead, -1), []).append((stage_zero, u))
@@ -853,10 +853,10 @@
             return carry
 
         lax.fori_loop(0, third_width // 512, in_grad, 0)
-    tick(3)
+    tick()
     loads[17].wait()
     swap = half_sum(2, dqkv, w1_b, third_width)
-    tick(2)
+    tick()
     swap.wait()
     y_finish()
 
@@ -887,7 +887,7 @@
         copy = remote(small_s, small_r.at[n], ss.at[n], sr.at[n], target)
         copy.start()
         start(n + 1, 4)
-        tick()
+        tick(1 if n == 0 else 3)
         copy.wait()
         small_s[...] += small_r[n]
     tails = [

time: 345 us -> 332 us (0.962)
  Pallas kernels: 306 us -> 293 us
    pallas_call x1, Pallas kernels: 184 us -> 171 us  [backward(): pl.pallas_call(functools.partial(backward_body, groups, clips, blocks), o...]
where the time goes in v10:
time: 332 us; the launch traced here: 331 us
  Pallas kernels  293 us (88%)
  matrix products  17.2 us (5%)
  other arithmetic  13.3 us (4%)
  local copies, waits for them, and re-layouts  6.85 us (2%)
    pallas_call x1, Pallas kernels, backward(): pl.pallas_call(functools.partial(backward_body, groups, clips, blocks), o...  171 us
    pallas_call x1, Pallas kernels, forward(): pl.pallas_call(functools.partial(forward_body, groups, clips, blocks), ou...  122 us
    dot_general x2, matrix products, contract(): lax.dot_general(left, right, (((a,), (b,)), ((), ())), preferred_element_...  17.2 us
    convert_element_type x4, other arithmetic, paired(): g.reshape(shard.shape).astype(F32)  10.8 us

profile of v10, /device:TPU:9, one launch (start us, length us, event | category | flops | bytes accessed | tf_op | source)
XLA Modules:
  0.0 331.0 jit_solution(13435017429983085195)
XLA Ops:
  0.7 0.7 convert_element_type.110
  1.4 0.8 convert_add_fusion
  2.2 0.6 reshape.123.refs_4_
  2.8 0.3 fusion.6
  3.1 0.7 pad_maximum_fusion.refs_6_
  3.8 121.5 %forward.1 = (bf16[4,4,2,32,1536]{4,3,2,1,0:T(8,128)(2,1)}, bf16[4,4,2,16,1024]{4,3,2,1,0:T(8,128)(2,1)}, bf16[4,4,2,32,2048]{4,3,2,1,0:T(8,128)(2,1)}, bf16[4,4...) custom-call(bf16[4,2,32,3072]{3,2,1,0:T(8,128)(2,1)} %bitcast.52, ...), custom_call_target="tpu_custom_call" | custom-call | tf_op jit(solution)/shard_map/forward/pallas_call | solution.py:478
  125.3 0.0 copy-start
  125.3 11.0 %fusion.4 = (bf16[1024,2048]{1,0:T(8,128)(2,1)}, bf16[1024,2048]{1,0:T(8,128)(2,1)S(1)}) fusion(f32[2048]{0:T(1024)} %bitcast.63, bf16[1024,1024]{1,0:T(8,128)(2,1)} %get-tuple-element.38.refs_12_, bf16[1024,2048]{1,0:T(8,128)(2,1)} %bitcast.45), kind=kOutput, calls=%fused_computation.5 | convolution fusion | flops 4320133120 | bytes 14688256 | tf_op jit(solution)/shard_map/dot_general | solution.py:985
  136.3 0.0 copy-done
  136.3 6.2 %convolution_convert_fusion = bf16[2048,1024]{1,0:T(8,128)(2,1)} fusion(bf16[1024,2048]{1,0:T(8,128)(2,1)S(1)} %get-tuple-element.63.refs_1_, bf16[1024,1024]{1,0:T(8,128)(2,1)S(1)} %bitcast.44), kind=kOutput, calls=%fused_computation.8 | convolution fusion | flops 4297064448 | bytes 10485760 | tf_op jit(solution)/shard_map/dot_general | solution.py:985
  142.5 0.0 copy-done.1
  142.5 171.4 %backward.1 = (bf16[4,2,32,3072]{3,2,1,0:T(8,128)(2,1)}, bf16[2,4,2,16,1024]{4,3,2,1,0:T(8,128)(2,1)}, bf16[4,2,32,4096]{3,2,1,0:T(8,128)(2,1)}, bf16[2,4,2,64,1...) custom-call(bf16[4,2,2,2,64,1024]{5,4,3,2,1,0:T(8,128)(2,1)} %bitcas, ...), custom_call_target="tpu_custom_call" | custom-call | tf_op jit(solution)/shard_map/backward/pallas_call | solution.py:971
  314.0 0.9 slice.41
  314.8 0.6 reshape.131
  315.4 0.7 slice_bitcast_fusion
  316.1 1.5 fusion.9
  317.6 0.6 copy.29
  318.2 2.1 bitcast_convert_fusion.3
  320.3 3.4 %bitcast_convert_fusion.2 = f32[256,3072]{1,0:T(8,128)} fusion(bf16[4,2,32,3072]{3,2,1,0:T(8,128)(2,1)} %get-tuple-element.58), kind=kLoop, calls=%fused_computation.11 | loop fusion | flops 786432 | bytes 4718592 | tf_op jit(solution)/shard_map/convert_element_type | solution.py:1063
  323.8 0.0 copy-done.3
  323.8 2.6 bitcast_convert_fusion.1
  326.4 2.6 bitcast_convert_fusion
  329.1 1.0 copy.32
  330.0 1.0 copy.33
  (11 shorter events, 0.0 us)
Async XLA Ops:
  125.3 11.0 %copy-start = (bf16[4,256,1024]{2,1,0:T(8,128)(2,1)S(1)}, bf16[4,256,1024]{2,1,0:T(8,128)(2,1)}, u32[]{:S(2)}) copy-start(bf16[4,256,1024]{2,1,0:T(8,128)(2,1)} %get-tuple-element.41.refs_15_) | copy-start | bytes 6291460
  136.3 6.2 %copy-start.1 = (bf16[1024,2048]{1,0:T(8,128)(2,1)}, bf16[1024,2048]{1,0:T(8,128)(2,1)S(1)}, u32[]{:S(2)}) copy-start(bf16[1024,2048]{1,0:T(8,128)(2,1)S(1)} %get-tuple-element.63.refs_1_) | copy-start | bytes 12582916
  313.9 9.8 %copy-start.3 = (bf16[4,2,32,4096]{3,2,1,0:T(8,128)(2,1)S(1)}, bf16[4,2,32,4096]{3,2,1,0:T(8,128)(2,1)}, u32[]{:S(2)}) copy-start(bf16[4,2,32,4096]{3,2,1,0:T(8,128)(2,1)} %get-tuple-element.60) | copy-start | bytes 6291460
  323.8 2.6 copy-start.2
  326.4 2.6 copy-start.5
  326.4 3.6 %copy-start.4 = (bf16[2,256,1024]{2,1,0:T(8,128)(2,1)S(1)}, bf16[2,256,1024]{2,1,0:T(8,128)(2,1)}, u32[]{:S(2)}) copy-start(bf16[2,256,1024]{2,1,0:T(8,128)(2,1)} %get-tuple-element.92) | copy-start | bytes 3145732

commit v11 on v10

--- a/solution.py
+++ b/solution.py
@@ -887,7 +887,7 @@
         copy = remote(small_s, small_r.at[n], ss.at[n], sr.at[n], target)
         copy.start()
         start(n + 1, 4)
-        tick(1 if n == 0 else 3)
+        tick(1 if n == 0 else 2)
         copy.wait()
         small_s[...] += small_r[n]
     tails = [

time: 332 us -> 332 us (level)
  no operation moved by 1% of the time
where the time goes in v11:
time: 332 us; the launch traced here: 331 us
  Pallas kernels  293 us (88%)
  matrix products  17.2 us (5%)
  other arithmetic  13.3 us (4%)
  local copies, waits for them, and re-layouts  6.85 us (2%)
    pallas_call x1, Pallas kernels, backward(): pl.pallas_call(functools.partial(backward_body, groups, clips, blocks), o...  172 us
    pallas_call x1, Pallas kernels, forward(): pl.pallas_call(functools.partial(forward_body, groups, clips, blocks), ou...  122 us
    dot_general x2, matrix products, contract(): lax.dot_general(left, right, (((a,), (b,)), ((), ())), preferred_element_...  17.2 us
    convert_element_type x4, other arithmetic, paired(): g.reshape(shard.shape).astype(F32)  10.8 us

profile of v11, /device:TPU:9, one launch (start us, length us, event | category | flops | bytes accessed | tf_op | source)
XLA Modules:
  0.0 331.4 jit_solution(15608239931438492925)
XLA Ops:
  0.7 0.7 convert_element_type.110
  1.4 0.8 convert_add_fusion
  2.2 0.6 reshape.123.refs_4_
  2.8 0.3 fusion.6
  3.1 0.7 pad_maximum_fusion.refs_6_
  3.8 121.5 %forward.1 = (bf16[4,4,2,32,1536]{4,3,2,1,0:T(8,128)(2,1)}, bf16[4,4,2,16,1024]{4,3,2,1,0:T(8,128)(2,1)}, bf16[4,4,2,32,2048]{4,3,2,1,0:T(8,128)(2,1)}, bf16[4,4...) custom-call(bf16[4,2,32,3072]{3,2,1,0:T(8,128)(2,1)} %bitcast.52, ...), custom_call_target="tpu_custom_call" | custom-call | tf_op jit(solution)/shard_map/forward/pallas_call | solution.py:478
  125.3 0.0 copy-start
  125.3 11.0 %fusion.4 = (bf16[1024,2048]{1,0:T(8,128)(2,1)}, bf16[1024,2048]{1,0:T(8,128)(2,1)S(1)}) fusion(f32[2048]{0:T(1024)} %bitcast.63, bf16[1024,1024]{1,0:T(8,128)(2,1)} %get-tuple-element.38.refs_12_, bf16[1024,2048]{1,0:T(8,128)(2,1)} %bitcast.45), kind=kOutput, calls=%fused_computation.5 | convolution fusion | flops 4320133120 | bytes 14688256 | tf_op jit(solution)/shard_map/dot_general | solution.py:985
  136.3 0.0 copy-done
  136.3 6.2 %convolution_convert_fusion = bf16[2048,1024]{1,0:T(8,128)(2,1)} fusion(bf16[1024,2048]{1,0:T(8,128)(2,1)S(1)} %get-tuple-element.63.refs_1_, bf16[1024,1024]{1,0:T(8,128)(2,1)S(1)} %bitcast.44), kind=kOutput, calls=%fused_computation.8 | convolution fusion | flops 4297064448 | bytes 10485760 | tf_op jit(solution)/shard_map/dot_general | solution.py:985
  142.5 0.0 copy-done.1
  142.5 171.8 %backward.1 = (bf16[4,2,32,3072]{3,2,1,0:T(8,128)(2,1)}, bf16[2,4,2,16,1024]{4,3,2,1,0:T(8,128)(2,1)}, bf16[4,2,32,4096]{3,2,1,0:T(8,128)(2,1)}, bf16[2,4,2,64,1...) custom-call(bf16[4,2,2,2,64,1024]{5,4,3,2,1,0:T(8,128)(2,1)} %bitcas, ...), custom_call_target="tpu_custom_call" | custom-call | tf_op jit(solution)/shard_map/backward/pallas_call | solution.py:971
  314.3 0.9 slice.41
  315.2 0.6 reshape.131
  315.8 0.7 slice_bitcast_fusion
  316.5 1.5 fusion.9
  318.0 0.6 copy.29
  318.6 2.1 bitcast_convert_fusion.3
  320.7 3.4 %bitcast_convert_fusion.2 = f32[256,3072]{1,0:T(8,128)} fusion(bf16[4,2,32,3072]{3,2,1,0:T(8,128)(2,1)} %get-tuple-element.58), kind=kLoop, calls=%fused_computation.11 | loop fusion | flops 786432 | bytes 4718592 | tf_op jit(solution)/shard_map/convert_element_type | solution.py:1063
  324.2 2.6 bitcast_convert_fusion.1
  326.8 0.0 copy-done.2
  326.8 2.6 bitcast_convert_fusion
  329.4 1.0 copy.32
  330.4 1.0 copy.33
  (11 shorter events, 0.0 us)
Async XLA Ops:
  125.3 11.0 %copy-start = (bf16[4,256,1024]{2,1,0:T(8,128)(2,1)S(1)}, bf16[4,256,1024]{2,1,0:T(8,128)(2,1)}, u32[]{:S(2)}) copy-start(bf16[4,256,1024]{2,1,0:T(8,128)(2,1)} %get-tuple-element.41.refs_15_) | copy-start | bytes 6291460
  136.3 6.2 %copy-start.1 = (bf16[1024,2048]{1,0:T(8,128)(2,1)}, bf16[1024,2048]{1,0:T(8,128)(2,1)S(1)}, u32[]{:S(2)}) copy-start(bf16[1024,2048]{1,0:T(8,128)(2,1)S(1)} %get-tuple-element.63.refs_1_) | copy-start | bytes 12582916
  314.3 9.8 %copy-start.3 = (bf16[4,2,32,4096]{3,2,1,0:T(8,128)(2,1)S(1)}, bf16[4,2,32,4096]{3,2,1,0:T(8,128)(2,1)}, u32[]{:S(2)}) copy-start(bf16[4,2,32,4096]{3,2,1,0:T(8,128)(2,1)} %get-tuple-element.60) | copy-start | bytes 6291460
  324.2 2.6 copy-start.2
  326.8 2.6 copy-start.5
  326.8 3.6 %copy-start.4 = (bf16[2,256,1024]{2,1,0:T(8,128)(2,1)S(1)}, bf16[2,256,1024]{2,1,0:T(8,128)(2,1)}, u32[]{:S(2)}) copy-start(bf16[2,256,1024]{2,1,0:T(8,128)(2,1)} %get-tuple-element.92) | copy-start | bytes 3145732
